TPU v7x, 512 devices: a whole 4x4x16 slice. The times are simulated.
512 devices in a mesh: magnet: 16 (over y, x), slab: 32 (over z, core).
Axes of the slice: x: 4, y: 4, z: 16, core: 2. Of those that a mesh axis runs over, the one named last changes fastest.
Arguments:
- foil_warmth: float32 [4096, 512], P(('magnet', 'slab')), may hold values from 0.5 to 4
- terminal_voltage_input: float32 [4096, 512], P(('magnet', 'slab')), may hold values from -6 to 6
- foil_segment_pattern: int32 [4096, 512], P(('magnet', 'slab')), may hold values from 0 to 2
- underlying_block_map: int32 [4096, 512], P('magnet'), may hold values from 3840 to 4095
- prior_block_warmth: float32 [32, 4096, 128], P('slab', 'magnet'), may hold values from 0 to 2
- substance_kind: int32 [32, 4096, 128], P('slab', 'magnet'), may hold values from 0 to 3
Outputs:
- sheet_potential: float32 [4096, 512], P(('magnet', 'slab'))
- brick_heated: float32 [32, 4096, 128], P('slab', 'magnet')
Inputs may be any that keep to these rules, and one draw needn't show every extreme that they name: `foil_segment_pattern`: 0 marks plain heater steel, 1 copper-plated stations, 2 current-lead contacts. `underlying_block_map`: the value is radial layer times 128 plus azimuthal cell. `substance_kind`: 0 insulation, 1 Nb3Sn coil, 2 copper wedge, 3 steel collar.
All inputs are finite; a program needn't handle non-finite values.
Results may differ from a plain program's by a relative error of at most 0.0001.
Values sent between devices are 32-bit elements; how exact they have to be, the bound alone decides.
No kernel may reach another device: no remote copies, remote signals or barrier semaphores. Data moves between devices by JAX's collectives and lax.ppermute only.
A program may use at most 64 MiB of HBM per device.

v0:
```python
import jax
import jax.numpy as jnp
from jax import lax
from jax.sharding import PartitionSpec as P

ITERS = 3
SUBSTEPS = 4


leak_diag = 0.25
contact_gain = 4.0
copper_factor = 3.0
sheet_slope = 0.5
heat_factor = 1.5
time_step = 0.03
conduct_table = (0.3, 1.0, 2.0, 0.6)
capacity_table = (1.0, 1.5, 2.0, 1.2)
diffusivity_derivative = 0.4


def padded_2(shard, sides, width):
    for axis, dim in sides:
        size, length = (lax.axis_size(axis), shard.shape[dim])
        up = [(i, (i + 1) % size) for i in range(size - 1)]
        down = [(j, i) for i, j in up]
        last = lax.slice_in_dim(shard, length - width, length, axis=dim)
        initial = lax.slice_in_dim(shard, 0, width, axis=dim)
        before = lax.ppermute(last, axis, up)
        after = lax.ppermute(initial, axis, down)
        shard = jnp.concatenate([before, shard, after], axis=dim)
    return shard


def lookup_table(substance_kind, table):
    running_total = jnp.zeros(substance_kind.shape, jnp.float32)
    for material_index in range(4):
        running_total = running_total + jnp.where(
            substance_kind == material_index, table[material_index], 0.0
        ).astype(jnp.float32)
    return running_total


def sheet_padded(values_grid):
    extended_field = padded_2(values_grid, ((("magnet", "slab"), 0),), 1)
    return jnp.pad(extended_field, ((0, 0), (1, 1)))


def neighbour_values(padded):
    return (padded[:-2, 1:-1], padded[2:, 1:-1], padded[1:-1, :-2], padded[1:-1, 2:])


def apply_sheet(values_grid, coeffs, diagonal):
    neighbours = neighbour_values(sheet_padded(values_grid))
    result = diagonal * values_grid
    for coeff_face, neighbour in zip(coeffs, neighbours):
        result = result - coeff_face * neighbour
    return result


def squares_sum(residual):
    return lax.psum(jnp.sum(residual * residual), ("magnet", "slab"))


def diffusivity_update(temp_pad, cond_pad, resistive_power_density, specific_storage_grid):
    centre_t = temp_pad[1:-1, 1:-1]
    centre_k = cond_pad[1:-1, 1:-1]
    flux_total = jnp.zeros(centre_t.shape, jnp.float32)
    pairs = (
        (temp_pad[:-2, 1:-1], cond_pad[:-2, 1:-1]),
        (temp_pad[2:, 1:-1], cond_pad[2:, 1:-1]),
        (temp_pad[1:-1, :-2], cond_pad[1:-1, :-2]),
        (temp_pad[1:-1, 2:], cond_pad[1:-1, 2:]),
    )
    for other_t, other_k in pairs:
        flux_total = flux_total + 0.5 * (centre_k + other_k) * (other_t - centre_t)
    for offset in (1, -1):
        other_t = jnp.roll(centre_t, offset, axis=2)
        other_k = jnp.roll(centre_k, offset, axis=2)
        flux_total = flux_total + 0.5 * (centre_k + other_k) * (other_t - centre_t)
    return centre_t + time_step * (flux_total + resistive_power_density) / specific_storage_grid


def local(
    foil_warmth,
    terminal_voltage_input,
    foil_segment_pattern,
    underlying_block_map,
    prior_block_warmth,
    substance_kind,
):
    shells_per_device, axial_rows_per_device, angular_position = prior_block_warmth.shape
    copper = jnp.where(foil_segment_pattern == 1, copper_factor, 1.0).astype(jnp.float32)
    sigma_cells = copper / (1.0 + sheet_slope * foil_warmth)
    sigma_pad = sheet_padded(sigma_cells)
    centre = sigma_pad[1:-1, 1:-1]
    coeffs = tuple((0.5 * (centre + other) for other in neighbour_values(sigma_pad)))
    contact = jnp.where(foil_segment_pattern == 2, contact_gain, 0.0).astype(jnp.float32)
    diagonal = leak_diag + contact + coeffs[0] + coeffs[1] + coeffs[2] + coeffs[3]
    rhs_field = contact * terminal_voltage_input
    voltage_solution = jnp.zeros_like(rhs_field)
    residual = rhs_field
    direction = rhs_field
    norm_now = squares_sum(residual)
    for iteration in range(ITERS):
        image_field = apply_sheet(direction, coeffs, diagonal)
        curvature = lax.psum(jnp.sum(direction * image_field), ("magnet", "slab"))
        step_length = norm_now / curvature
        voltage_solution = voltage_solution + step_length * direction
        residual = residual - step_length * image_field
        if iteration + 1 < ITERS:
            norm_next = squares_sum(residual)
            direction = residual + norm_next / norm_now * direction
            norm_now = norm_next
    neighbours = neighbour_values(sheet_padded(voltage_solution))
    joule = jnp.zeros_like(voltage_solution)
    for coeff_face, neighbour in zip(coeffs, neighbours):
        joule = joule + coeff_face * (voltage_solution - neighbour) ** 2
    joule = heat_factor * joule
    slab_index = lax.axis_index("slab")
    reference_diffusivity = lookup_table(substance_kind, conduct_table)
    specific_storage_grid = lookup_table(substance_kind, capacity_table)
    gathered = lax.all_gather(joule, "slab", axis=0, tiled=True)
    block_cells = shells_per_device * angular_position
    local_cell = underlying_block_map - slab_index * block_cells
    inside = (local_cell >= 0) & (local_cell < block_cells)
    layer_index = jnp.where(inside, local_cell // angular_position, shells_per_device)
    column = local_cell % angular_position
    row_index = jnp.broadcast_to(
        jnp.arange(axial_rows_per_device, dtype=jnp.int32)[:, None], underlying_block_map.shape
    )
    resistive_power_density = (
        jnp.zeros((shells_per_device, axial_rows_per_device, angular_position), jnp.float32)
        .at[layer_index, row_index, column]
        .add(gathered, mode="drop")
    )
    warmth_distribution = prior_block_warmth
    for substep in range(SUBSTEPS):
        diffusivity_coefficient = reference_diffusivity * (
            1.0 + diffusivity_derivative * warmth_distribution
        )
        combined_shell_array = jnp.stack([warmth_distribution, diffusivity_coefficient])
        extended_field = padded_2(combined_shell_array, (("magnet", 2), ("slab", 1)), 1)
        warmth_distribution = diffusivity_update(
            extended_field[0], extended_field[1], resistive_power_density, specific_storage_grid
        )
    return (voltage_solution, warmth_distribution)


def solution(mesh):
    placed = (
        P(("magnet", "slab"), None),
        P(("magnet", "slab"), None),
        P(("magnet", "slab"), None),
        P("magnet", None),
        P("slab", "magnet", None),
        P("slab", "magnet", None),
    )
    return jax.shard_map(
        local,
        mesh=mesh,
        in_specs=placed,
        out_specs=(P(("magnet", "slab"), None), P("slab", "magnet", None)),
        check_vma=False,
    )
```

profile of v0, /device:TPU:1, one launch (start us, length us, event | category | flops | bytes accessed | tf_op | source)
XLA Modules:
  0.0 1351.6 jit_solution(17768950309313427798)
XLA Ops:
  0.6 0.8 select_multiply_fusion
  1.5 8.8 collective-permute-start.3
  10.3 1.9 collective-permute-start.2
  12.2 2.4 collective-permute-start.1
  14.6 3.2 collective-permute-start
  17.8 1.1 multiply_bitcast_fusion.3
  18.9 0.7 pad_maximum_fusion.25
  19.6 1.3 collective-permute-start.9
  20.9 0.6 fusion.1
  21.6 5.5 collective-permute-start.8
  27.3 0.7 multiply_reduce_fusion.4
  28.0 113.5 %all-reduce.5 = (f32[]{:T(128)}, f32[]{:T(128)}) all-reduce(f32[]{:T(128)} %get-tuple-element.3, f32[]{:T(128)} %get-tuple-element.2), channel_id=1, replica_groups=mesh['magnet'=16,'slab'=32] {'magnet','slab'}, use_global_device_ids=true, to_apply=%region_1.2 | all-reduce | flops 2 | bytes 16 | tf_op jit(solution)/shard_map/psum | solution.py:61
  142.9 0.6 multiply_reduce_fusion.3
  143.5 99.3 %psum.44 = f32[]{:T(128)} all-reduce(f32[]{:T(128)} %get-tuple-element.19), channel_id=1, replica_groups=mesh['magnet'=16,'slab'=32] {'magnet','slab'}, use_global_device_ids=true, to_apply=%region_5.6 | all-reduce | flops 1 | bytes 8 | tf_op jit(solution)/shard_map/psum | solution.py:61
  244.1 2.6 collective-permute-start.5
  246.7 3.6 collective-permute-start.4
  250.3 0.3 and_reduce_fusion
  250.7 0.3 collective-permute-done.4
  251.1 0.7 multiply_reduce_fusion.2
  251.8 105.5 %psum.45 = f32[]{:T(128)} all-reduce(f32[]{:T(128)} %get-tuple-element.17), channel_id=1, replica_groups=mesh['magnet'=16,'slab'=32] {'magnet','slab'}, use_global_device_ids=true, to_apply=%region_7.8 | all-reduce | flops 1 | bytes 8 | tf_op jit(solution)/shard_map/psum | solution.py:106
  358.6 0.6 multiply_reduce_fusion.1
  359.2 0.2 multiply_reduce_fusion
  359.5 99.4 %psum.46 = f32[]{:T(128)} all-reduce(f32[]{:T(128)} %multiply_reduce_fusion.1), channel_id=1, replica_groups=mesh['magnet'=16,'slab'=32] {'magnet','slab'}, use_global_device_ids=true, to_apply=%region_9.10 | all-reduce | flops 1 | bytes 8 | tf_op jit(solution)/shard_map/psum | solution.py:61
  460.2 2.6 collective-permute-start.7
  462.8 3.0 collective-permute-start.6
  465.9 0.6 collective-permute-done.6
  466.6 0.7 fusion.114
  467.3 0.1 copy.8
  467.4 105.2 %psum.47 = f32[]{:T(128)} all-reduce(f32[]{:T(128)} %fusion.114), channel_id=1, replica_groups=mesh['magnet'=16,'slab'=32] {'magnet','slab'}, use_global_device_ids=true, to_apply=%region_11.12 | all-reduce | flops 1 | bytes 8 | tf_op jit(solution)/shard_map/psum | solution.py:106
  574.0 3.1 collective-permute-start.13
  577.1 3.6 collective-permute-start.12
  580.8 1.9 collective-permute-start.11
  582.7 3.6 collective-permute-start.10
  586.5 29.2 %all_gather.3 = f32[256,512]{1,0:T(8,128)S(1)} all-gather(f32[8,512]{1,0:T(8,128)S(1)} %fusion.101), channel_id=1, replica_groups=mesh['magnet'=16,'slab'=32] {'slab'}, dimensions={0}, use_global_device_ids=true | all-gather | bytes 540672 | tf_op jit(solution)/shard_map/all_gather | solution.py:122
  615.7 0.1 copy.9
  615.9 682.4 %scatter_custom_fusion = f32[32768]{0:T(1024)S(1)} fusion(s32[131072]{0:T(1024)S(1)} %bitcast.58, f32[131072]{0:T(1024)S(1)} %bitcast.59, f32[]{:T(128)} %constant.24.clone.1), kind=kCustom, calls=%fused_computation.175 | custom fusion | flops 131072 | bytes 131076
  1298.4 0.1 fusion.157
  1298.6 0.1 fusion.158
  1298.7 0.4 multiply_bitcast_fusion.2
  1299.1 1.3 collective-permute-start.15
  1300.4 4.0 collective-permute-start.14
  1304.4 0.7 collective-permute-done.14
  1305.2 3.2 collective-permute-start.17
  1308.4 2.4 collective-permute-start.16
  1310.7 2.2 collective-permute-done.17
  1312.9 1.2 collective-permute-done.16
  1314.3 0.1 fusion.155
  1314.7 0.4 multiply_bitcast_fusion.1
  1315.1 1.3 collective-permute-start.19
  1316.4 4.2 collective-permute-start.18
  1320.6 0.7 collective-permute-done.18
  1321.4 1.9 collective-permute-start.21
  1323.3 5.3 collective-permute-start.20
  1328.6 2.2 collective-permute-done.21
  1330.8 1.2 collective-permute-done.20
  1332.5 0.4 multiply_bitcast_fusion
  1332.9 1.3 collective-permute-start.23
  1334.2 4.5 collective-permute-start.22
  1338.8 0.7 collective-permute-done.22
  1339.5 1.9 collective-permute-start.25
  1341.4 5.2 collective-permute-start.24
  1346.7 2.2 collective-permute-done.25
  1348.9 1.2 collective-permute-done.24
  1350.6 1.0 fusion.14
  (67 shorter events, 2.4 us)
Async XLA Ops:
  0.6 20.3 %copy-start.1 = (s32[256,512]{1,0:T(8,128)S(1)}, s32[256,512]{1,0:T(8,128)}, u32[]{:S(2)}) copy-start(s32[256,512]{1,0:T(8,128)} %param.9) | copy-start | bytes 1572868
  1.5 20.1 %collective-permute-start.3 = (f32[1,512]{1,0:T(1,128)S(1)}, f32[1,512]{1,0:T(1,128)S(1)}, u32[]{:S(2)}, u32[]{:S(2)}) collective-permute-start(f32[1,512]{1,0:T(1,128)S(1)} %get-tuple-element.86), channel_id=1, source_target_pairs={{1,0},{2,1},{3,2},{4,3},{5,4},{6,5},{7,6},{8,7},{9,8},{10,9},{11,1... | collective-permute-start | bytes 6152 | tf_op jit(solution)/shard_map/ppermute | solution.py:29
  10.3 16.8 %collective-permute-start.2 = (f32[1,512]{1,0:T(1,128)S(1)}, f32[1,512]{1,0:T(1,128)S(1)}, u32[]{:S(2)}, u32[]{:S(2)}) collective-permute-start(f32[1,512]{1,0:T(1,128)S(1)} %get-tuple-element.85), channel_id=1, source_target_pairs={{0,1},{1,2},{2,3},{3,4},{4,5},{5,6},{6,7},{7,8},{8,9},{9,10},{10,1... | collective-permute-start | bytes 6152 | tf_op jit(solution)/shard_map/ppermute | solution.py:28
  12.2 15.0 %collective-permute-start.1 = (f32[1,512]{1,0:T(1,128)S(1)}, f32[1,512]{1,0:T(1,128)S(1)}, u32[]{:S(2)}, u32[]{:S(2)}) collective-permute-start(f32[1,512]{1,0:T(1,128)S(1)} %get-tuple-element.83), channel_id=1, source_target_pairs={{1,0},{2,1},{3,2},{4,3},{5,4},{6,5},{7,6},{8,7},{9,8},{10,9},{11,1... | collective-permute-start | bytes 6152 | tf_op jit(solution)/shard_map/ppermute | solution.py:29
  14.6 12.6 collective-permute-start
  19.6 561.1 %collective-permute-start.9 = (f32[2,1,1,128]{3,2,1,0:T(1,128)S(1)}, f32[2,1,1,128]{3,2,1,0:T(1,128)S(1)}, u32[]{:S(2)}, u32[]{:S(2)}) collective-permute-start(f32[2,1,1,128]{3,2,1,0:T(1,128)S(1)} %get-tuple-element.75), channel_id=1, source_target_pairs={{32,0},{64,32},{96,64},{128,96},{160,128},{192,160},{224,192},{256... | collective-permute-start | bytes 3080 | tf_op jit(solution)/shard_map/ppermute | solution.py:29
  21.5 228.8 %copy-start.3 = (s32[3]{0:T(128)S(1)}, s32[3]{0:T(128)}, u32[]{:S(2)}) copy-start(s32[3]{0:T(128)} %constant.97) | copy-start | bytes 40
  21.6 559.2 %collective-permute-start.8 = (f32[2,1,1,128]{3,2,1,0:T(1,128)S(1)}, f32[2,1,1,128]{3,2,1,0:T(1,128)S(1)}, u32[]{:S(2)}, u32[]{:S(2)}) collective-permute-start(f32[2,1,1,128]{3,2,1,0:T(1,128)S(1)} %get-tuple-element.74), channel_id=1, source_target_pairs={{0,32},{32,64},{64,96},{96,128},{128,160},{160,192},{192,224},{224... | collective-permute-start | bytes 3080 | tf_op jit(solution)/shard_map/ppermute | solution.py:28
  244.1 6.6 collective-permute-start.5
  246.7 4.3 collective-permute-start.4
  250.3 108.9 %copy-start.4 = (s32[3]{0:T(128)S(1)}, s32[3]{0:T(128)}, u32[]{:S(2)}) copy-start(s32[3]{0:T(128)} %constant.94) | copy-start | bytes 40
  460.2 5.7 collective-permute-start.7
  462.8 3.7 collective-permute-start.6
  465.9 114.9 %copy-start = (f32[1,256,128]{2,1,0:T(8,128)S(1)}, f32[1,256,128]{2,1,0:T(8,128)}, u32[]{:S(2)}) copy-start(f32[1,256,128]{2,1,0:T(8,128)} %param.10) | copy-start | bytes 393220
  574.0 41.9 %copy-start.2 = (f32[8,512]{1,0:T(8,128)}, f32[8,512]{1,0:T(8,128)S(1)}, u32[]{:S(2)}) copy-start(f32[8,512]{1,0:T(8,128)S(1)} %multiply_add_fusion) | copy-start | bytes 49156
  574.0 12.4 collective-permute-start.13
  577.1 9.2 collective-permute-start.12
  580.8 717.5 %collective-permute-start.11 = (f32[2,1,258,128]{3,2,1,0:T(8,128)S(1)}, f32[2,1,258,128]{3,2,1,0:T(8,128)S(1)}, u32[]{:S(2)}, u32[]{:S(2)}) collective-permute-start(f32[2,1,258,128]{3,2,1,0:T(8,128)S(1)} %pad_maximum_fusion.4), channel_id=1, source_target_pairs={{1,0},{2,1},{3,2},{4,3},{5,4},{6,5},{7,6},{8,7},{9,8},{10,9},{11,1... | collective-permute-start | bytes 792584 | tf_op jit(solution)/shard_map/ppermute | solution.py:29
  582.7 715.6 %collective-permute-start.10 = (f32[2,1,258,128]{3,2,1,0:T(8,128)S(1)}, f32[2,1,258,128]{3,2,1,0:T(8,128)S(1)}, u32[]{:S(2)}, u32[]{:S(2)}) collective-permute-start(f32[2,1,258,128]{3,2,1,0:T(8,128)S(1)} %pad_maximum_fusion.4), channel_id=1, source_target_pairs={{0,1},{1,2},{2,3},{3,4},{4,5},{5,6},{6,7},{7,8},{8,9},{9,10},{10,1... | collective-permute-start | bytes 792584 | tf_op jit(solution)/shard_map/ppermute | solution.py:28
  1299.1 5.3 collective-permute-start.15
  1300.4 4.7 collective-permute-start.14
  1305.2 7.8 collective-permute-start.17
  1308.4 5.7 collective-permute-start.16
  1315.1 5.5 collective-permute-start.19
  1316.4 4.9 collective-permute-start.18
  1321.4 9.4 collective-permute-start.21
  1323.3 8.7 collective-permute-start.20
  1332.9 5.8 collective-permute-start.23
  1334.2 5.2 collective-permute-start.22
  1339.5 9.4 collective-permute-start.25
  1341.4 8.6 collective-permute-start.24
where the time goes:
time: 1360 us; the launch traced here: 1350 us
  other arithmetic  693 us (51%)
  blocking collectives  552 us (41%)
  starting transfers between devices  83.6 us (6%)
    unnamed x4, other arithmetic  683 us
    psum x3, blocking collectives, squares_sum(): return lax.psum(jnp.sum(residual * residual), ('magnet', 'slab'))  312 us
    psum x2, blocking collectives, local(): curvature = lax.psum(jnp.sum(direction * image_field), ('magnet', 'slab'))  211 us
    ppermute x13, starting transfers between devices, padded_2(): before = lax.ppermute(last, axis, up)  50 us
    ppermute x13, starting transfers between devices, padded_2(): after = lax.ppermute(initial, axis, down)  33.6 us
    all_gather x1, blocking collectives, local(): gathered = lax.all_gather(joule, 'slab', axis=0, tiled=True)  29.2 us
  transfers between devices with their start and end apart: 26, of which 11 were waited for; matrix products, arithmetic and copies ran while one was open for 51% of the time, Pallas kernels for 0%

commit v1 on v0

v1 whole, which is shorter than its diff:
```python
import functools

import jax
import jax.numpy as jnp
from jax import lax
from jax.experimental import pallas as pl
from jax.experimental.pallas import tpu as pltpu
from jax.sharding import PartitionSpec as P

SUBSTEPS = 4
HALO = SUBSTEPS
ROWS = 8

leak_diag = 0.25
contact_gain = 4.0
copper_factor = 3.0
sheet_slope = 0.5
heat_factor = 1.5
time_step = 0.03
conduct_table = (0.3, 1.0, 2.0, 0.6)
capacity_table = (1.0, 1.5, 2.0, 1.2)
diffusivity_derivative = 0.4

SHIFT = 9.85
SCALE = 9.6
BOTH = ("magnet", "slab")


def place():
    size = lax.axis_size("slab")
    return lax.axis_index("magnet") * size + lax.axis_index("slab"), lax.axis_size("magnet") * size


def above(v):
    return pltpu.roll(v, 1, 0)


def below(v):
    return pltpu.roll(v, v.shape[0] - 1, 0)


def left(v):
    return pltpu.roll(v, 1, 1)


def right(v):
    return pltpu.roll(v, v.shape[1] - 1, 1)


def rows_inside(shape, margin):
    index, count = place()
    row = lax.broadcasted_iota(jnp.int32, shape, 0)
    low = jnp.where(index > 0, 0, margin)
    high = jnp.where(index < count - 1, shape[0], shape[0] - margin)
    return jnp.where((row >= low) & (row < high), 1.0, 0.0).astype(jnp.float32)


def basis_kernel(own, before, after, moments, w0_out, w1_out, w2_out, down_out, right_out, left_out, cells_out):
    def window(i):
        part = slice(ROWS * i, ROWS * (i + 1))
        return jnp.concatenate([before[part, :], own[part, :], after[part, :]], axis=0)

    warmth, voltage, pattern = window(0), window(1), window(2)
    cells_out[...] = window(3)
    shape = warmth.shape
    inside = rows_inside(shape, ROWS)
    col = lax.broadcasted_iota(jnp.int32, shape, 1)
    last = col == shape[1] - 1
    sigma = inside * jnp.where(pattern == 1.0, copper_factor, 1.0) / (1.0 + sheet_slope * warmth)
    contact = jnp.where(pattern == 2.0, contact_gain, 0.0)
    c_down = 0.5 * (sigma + below(sigma))
    c_right = 0.5 * (sigma + jnp.where(last, 0.0, right(sigma)))
    c_left = jnp.where(col == 0, 0.5 * sigma, left(c_right))
    diagonal = leak_diag + contact + above(c_down) + c_down + c_left + c_right
    diagonal = (diagonal - SHIFT) * (1.0 / SCALE)
    o_down = c_down * inside * below(inside) * (1.0 / SCALE)
    o_up = above(o_down)
    o_right = jnp.where(last, 0.0, c_right) * (1.0 / SCALE)
    o_left = left(o_right)

    def apply(v):
        return diagonal * v - (o_up * above(v) + o_down * below(v)) - (o_left * left(v) + o_right * right(v))

    w0 = contact * voltage
    w1 = apply(w0)
    w2 = 2.0 * apply(w1) - w0
    w3 = apply(w2)
    w0_out[...] = w0
    w1_out[...] = w1
    w2_out[...] = w2
    down_out[...] = c_down
    right_out[...] = c_right
    left_out[...] = c_left
    a, b, c, d = (v[ROWS : 2 * ROWS] for v in (w0, w1, w2, w3))
    lane = lax.broadcasted_iota(jnp.int32, (1, 128), 1)
    line = jnp.zeros((1, 128), jnp.float32)
    for i, (u, v) in enumerate(((a, a), (a, b), (a, c), (b, b), (b, c), (c, c), (c, d))):
        line = jnp.where(lane == i, jnp.sum(u * v, keepdims=True), line)
    moments[...] = jnp.broadcast_to(line, moments.shape)


def sum_kernel(lines, out):
    out[...] = jnp.broadcast_to(jnp.sum(lines[...], axis=0, keepdims=True), out.shape)


def solve_small(lines):
    total = jnp.sum(lines, axis=0, keepdims=True)
    g00, g01, g02, g11, g12, g22, k22 = (total[:, i : i + 1] for i in range(7))
    gram = ((g00, g01, g02), (g01, g11, g12), (g02, g12, g22))
    k11, k12 = 0.5 * (g12 + g01), 0.5 * (g22 + g02)
    shifted = ((g01, g11, g12), (g11, k11, k12), (g12, k12, k22))
    energy = [[SCALE * shifted[i][j] + SHIFT * gram[i][j] for j in range(3)] for i in range(3)]

    def form(m, v):
        return sum(v[i] * (v[i] * m[i][i] + 2.0 * sum((v[j] * m[i][j] for j in range(i + 1, len(v))), 0.0)) for i in range(len(v)))

    def ratio(num, den, low, high):
        return jnp.clip(num / jnp.maximum(den, 1e-37), low, high)

    alpha0 = g00 / energy[0][0]
    r = [1.0 - alpha0 * SHIFT, -alpha0 * SCALE]
    rr1 = jnp.maximum(form(gram, r), 0.0)
    beta = ratio(rr1, g00, 0.0, 1e4)
    p = [r[0] + beta, r[1]]
    alpha1 = ratio(rr1, form(energy, p), 0.05, 4.1)
    half = 0.5 * SCALE * p[1]
    image = [half + SHIFT * p[0], SCALE * p[0] + SHIFT * p[1], half]
    x = [alpha0 + alpha1 * p[0], alpha1 * p[1]]
    r = [r[0] - alpha1 * image[0], r[1] - alpha1 * image[1], -alpha1 * image[2]]
    rr2 = jnp.maximum(form(gram, r), 0.0)
    beta = ratio(rr2, rr1, 0.0, 1e4)
    p = [r[0] + beta * p[0], r[1] + beta * p[1], r[2]]
    alpha2 = ratio(rr2, form(energy, p), 0.05, 4.1)
    return x[0] + alpha2 * p[0], x[1] + alpha2 * p[1], alpha2 * p[2]


def heat_kernel(
    layers, lines, w0, w1, w2, c_down, c_right, c_left, cells, own, before, after, potential, heated, warm, base, store, heat
):
    span = ROWS + 2 * HALO
    f0, f1, f2 = solve_small(lines[...])
    shape = w0.shape
    inside = rows_inside(shape, ROWS)
    x = (f0 * w0[...] + f1 * w1[...] + f2 * w2[...]) * inside
    potential[...] = x[ROWS : 2 * ROWS]
    col = lax.broadcasted_iota(jnp.int32, shape, 1)
    step = x - below(x)
    q_down = c_down[...] * (step * step)
    step = x - jnp.where(col == shape[1] - 1, 0.0, right(x))
    q_right = c_right[...] * (step * step)
    q_left = jnp.where(col == 0, c_left[...] * (x * x), left(q_right))
    joule = heat_factor * ((q_down + above(q_down)) + (q_right + q_left))
    joule = joule[ROWS - HALO : ROWS - HALO + span]
    cell = cells[ROWS - HALO : ROWS - HALO + span, :].astype(jnp.int32)
    spokes = heated.shape[-1]
    azimuth = cell & (spokes - 1)
    outer = cell >= (layers - 1) * spokes
    pieces = []
    for part in (jnp.where(outer, 0.0, joule), jnp.where(outer, joule, 0.0)):
        for _ in range(3):
            piece = part.astype(jnp.bfloat16)
            pieces.append(piece.astype(jnp.float32))
            part = part - piece.astype(jnp.float32)
    stacked = jnp.concatenate(pieces, axis=0)
    row_of = lax.rem(lax.broadcasted_iota(jnp.int32, stacked.shape, 0), span)
    spoke = lax.broadcasted_iota(jnp.int32, (spokes, shape[1]), 0)
    total = jnp.zeros((stacked.shape[0], spokes), jnp.float32)
    for row in range(1, span - 1):
        pick = jnp.where(azimuth[row : row + 1, :] == spoke, 1.0, 0.0).astype(jnp.bfloat16)
        some = jnp.where(row_of == row, stacked, 0.0).astype(jnp.bfloat16)
        total = total + lax.dot_general(some, pick, (((1,), (1,)), ((), ())), preferred_element_type=jnp.float32)
    heat[0] = total[0:span] + (total[span : 2 * span] + total[2 * span : 3 * span])
    heat[1] = total[3 * span : 4 * span] + (total[4 * span : 5 * span] + total[5 * span : 6 * span])

    cut = (span, spokes)
    there = rows_inside(cut, HALO)
    for layer in range(layers):

        def assemble(i):
            part = slice(ROWS * i, ROWS * (i + 1))
            return jnp.concatenate(
                [before[layer, part][ROWS - HALO :], own[layer, part], after[layer, part][:HALO]], axis=0
            )

        kind = assemble(1)
        conduct = jnp.where(kind == 0.0, conduct_table[0], jnp.where(kind == 1.0, conduct_table[1], jnp.where(kind == 2.0, conduct_table[2], conduct_table[3])))
        gain = [0.5 * time_step / c for c in capacity_table]
        gains = jnp.where(kind == 0.0, gain[0], jnp.where(kind == 1.0, gain[1], jnp.where(kind == 2.0, gain[2], gain[3])))
        warm[0, layer] = assemble(0) * there
        base[layer] = conduct * there
        store[layer] = gains * there

    for substep in range(SUBSTEPS):
        now, then = substep % 2, 1 - substep % 2

        def conductivity(layer):
            t = warm[now, layer]
            return t, base[layer] * (1.0 + diffusivity_derivative * t)

        t, k = conductivity(0)
        inner = k * t
        for layer in range(layers):
            if layer + 1 < layers:
                t_next, k_next = conductivity(layer + 1)
                outer_face = (k + k_next) * (t_next - t)
            else:
                t_next, k_next = None, None
                outer_face = -(k * t)
            flux = outer_face - inner
            face = (k + below(k)) * (below(t) - t)
            flux = flux + (face - above(face))
            face = (k + right(k)) * (right(t) - t)
            flux = flux + (face - left(face))
            if layer >= layers - 2:
                flux = flux + 2.0 * heat[layer - (layers - 2)]
            fresh = t + store[layer] * flux
            if substep + 1 < SUBSTEPS:
                warm[then, layer] = fresh
            else:
                heated[layer] = fresh[HALO : HALO + ROWS]
            t, k, inner = t_next, k_next, outer_face


def vmem(count):
    return [pl.BlockSpec(memory_space=pltpu.VMEM)] * count


def local(foil_warmth, terminal_voltage_input, foil_segment_pattern, underlying_block_map, prior_block_warmth, substance_kind):
    f32 = jnp.float32
    magnets, layers = lax.axis_size("magnet"), lax.axis_size("slab")
    count = magnets * layers
    width, spokes = foil_warmth.shape[1], prior_block_warmth.shape[2]
    onward = [(i, i + 1) for i in range(count - 1)]
    backward = [(i + 1, i) for i in range(count - 1)]

    def around(block):
        return lax.ppermute(block, BOTH, onward), lax.ppermute(block, BOTH, backward)

    bricks = jnp.concatenate(
        [
            prior_block_warmth.reshape(layers, ROWS, spokes),
            substance_kind.astype(f32).reshape(layers, ROWS, spokes),
        ],
        axis=1,
    )
    bricks = lax.all_to_all(bricks, "slab", 0, 0)

    cells = lax.dynamic_slice_in_dim(underlying_block_map, lax.axis_index("slab") * ROWS, ROWS, axis=0)
    sheet = jnp.concatenate(
        [foil_warmth, terminal_voltage_input, foil_segment_pattern.astype(f32), cells.astype(f32)], axis=0
    )
    field = jax.ShapeDtypeStruct((3 * ROWS, width), f32)
    moments, *fields = pl.pallas_call(
        basis_kernel,
        out_shape=(jax.ShapeDtypeStruct((layers, 128), f32),) + (field,) * 7,
        in_specs=vmem(3),
        out_specs=vmem(8),
        name="basis",
    )(sheet, *around(sheet))

    lines = lax.all_to_all(moments.reshape(layers, 1, 128), "slab", 0, 0).reshape(layers, 128)
    lines = pl.pallas_call(
        sum_kernel,
        out_shape=jax.ShapeDtypeStruct((magnets, 128), f32),
        in_specs=vmem(1),
        out_specs=vmem(1)[0],
        name="total",
    )(lines)
    lines = lax.all_to_all(lines.reshape(magnets, 1, 128), "magnet", 0, 0).reshape(magnets, 128)

    span = ROWS + 2 * HALO
    potential, heated = pl.pallas_call(
        functools.partial(heat_kernel, layers),
        out_shape=(jax.ShapeDtypeStruct((ROWS, width), f32), jax.ShapeDtypeStruct((layers, ROWS, spokes), f32)),
        in_specs=vmem(11),
        out_specs=vmem(2),
        scratch_shapes=[
            pltpu.VMEM((2, layers, span, spokes), f32),
            pltpu.VMEM((layers, span, spokes), f32),
            pltpu.VMEM((layers, span, spokes), f32),
            pltpu.VMEM((2, span, spokes), f32),
        ],
        name="heat",
    )(lines, *fields, bricks, *around(bricks))
    heated = lax.all_to_all(heated, "slab", 0, 0)
    return potential, heated.reshape(prior_block_warmth.shape)


def solution(mesh):
    placed = (
        P(("magnet", "slab"), None),
        P(("magnet", "slab"), None),
        P(("magnet", "slab"), None),
        P("magnet", None),
        P("slab", "magnet", None),
        P("slab", "magnet", None),
    )
    return jax.shard_map(
        local,
        mesh=mesh,
        in_specs=placed,
        out_specs=(P(("magnet", "slab"), None), P("slab", "magnet", None)),
        check_vma=False,
    )
```

time: 1360 us -> 130 us (0.10)
  other arithmetic: 693 us -> 2.39 us
  blocking collectives: 552 us -> 58.4 us
  starting transfers between devices: 83.6 us -> 27.9 us
  Pallas kernels: 0 us -> 14.1 us
    unnamed x4 -> x0, other arithmetic: 683 us -> none
    psum x5 -> x0, blocking collectives: 523 us -> none  [the longest x3 312 us: squares_sum(): return lax.psum(jnp.sum(residual * residual), ('magnet', 'slab'))]
    ppermute x26 -> x4, starting transfers between devices: 83.6 us -> 11.1 us  [the longest x2 6.3 us: around(): lax.ppermute(block, BOTH, onward)]
    all_to_all x0 -> x3, blocking collectives: none -> 58.4 us  [the longest x1 21.7 us: local(): heated = lax.all_to_all(heated, 'slab', 0, 0)]
    all_gather x1 -> x0, blocking collectives: 29.2 us -> none  [local(): gathered = lax.all_gather(joule, 'slab', axis=0, tiled=True)]
    all_to_all x0 -> x1, waiting for transfers between devices: none -> 22 us  [local(): bricks = lax.all_to_all(bricks, 'slab', 0, 0)]
    all_to_all x0 -> x1, starting transfers between devices: none -> 16.7 us  [local(): bricks = lax.all_to_all(bricks, 'slab', 0, 0)]
    pallas_call x0 -> x3, Pallas kernels: none -> 14.1 us  [the longest x1 10.8 us: local(): pl.pallas_call(functools.partial(heat_kernel, layers), out_shape=(jax.Sha...]
  transfers between devices with their start and end apart: 26 -> 5, of which waited for: 11 -> 2; matrix products, arithmetic and copies ran while one was open for 51% -> 1% of each run, Pallas kernels for 0% -> 3%
where the time goes in v1:
time: 130 us
  blocking collectives  58.4 us (45%)
  starting transfers between devices  27.9 us (21%)
  waiting for transfers between devices  23.3 us (18%)
  Pallas kernels  14.1 us (11%)
  local copies, waits for them, and re-layouts  2.79 us (2%)
  other arithmetic  2.39 us (2%)
    all_to_all x1, waiting for transfers between devices, local(): bricks = lax.all_to_all(bricks, 'slab', 0, 0)  22 us
    all_to_all x1, blocking collectives, local(): heated = lax.all_to_all(heated, 'slab', 0, 0)  21.7 us
    all_to_all x1, blocking collectives, local(): lax.all_to_all(moments.reshape(layers, 1, 128), 'slab', 0, 0)  19.8 us
    all_to_all x1, blocking collectives, local(): lax.all_to_all(lines.reshape(magnets, 1, 128), 'magnet', 0, 0)  16.9 us
    all_to_all x1, starting transfers between devices, local(): bricks = lax.all_to_all(bricks, 'slab', 0, 0)  16.7 us
    pallas_call x1, Pallas kernels, local(): pl.pallas_call(functools.partial(heat_kernel, layers), out_shape=(jax.Sha...  10.8 us
    ppermute x2, starting transfers between devices, around(): lax.ppermute(block, BOTH, onward)  6.3 us
    ppermute x2, starting transfers between devices, around(): lax.ppermute(block, BOTH, backward)  4.81 us
  transfers between devices with their start and end apart: 5, of which 2 were waited for; matrix products, arithmetic and copies ran while one was open for 1% of the time, Pallas kernels for 3%

profile of v1, /device:TPU:1, one launch (start us, length us, event | category | flops | bytes accessed | tf_op | source)
XLA Modules:
  0.0 129.6 jit_solution(582248716732609681)
XLA Ops:
  0.6 0.0 copy-start.4
  0.6 0.9 convert_bitcast_fusion
  1.6 0.0 copy-done.4
  1.6 0.7 pad_maximum_fusion
  2.3 16.7 %all-to-all-start.2 = ((f32[32,16,128]{2,1,0:T(8,128)}), f32[32,16,128]{2,1,0:T(8,128)S(1)}, u32[]{:S(2)}, u32[]{:S(2)}) async-start(f32[32,16,128]{2,1,0:T(8,128)} %pad_maximum_fusion), calls=%async_computation.2 | async-start | bytes 524288 | tf_op jit(solution)/shard_map/all_to_all | solution.py:246
  19.1 0.0 copy-start.7
  19.1 22.0 %all-to-all-done.2.own = f32[32,16,128]{2,1,0:T(8,128)S(1)} async-done(((f32[32,16,128]{2,1,0:T(8,128)}), f32[32,16,128]{2,1,0:T(8,128)S(1)}, u32[]{:S(2)}, u32[]{:S(2)}) %all-to-all-start.2) | async-done | bytes 262176 | tf_op jit(solution)/shard_map/all_to_all | solution.py:246
  41.1 0.0 copy-start
  41.1 2.9 %collective-permute-start.3 = (f32[32,16,128]{2,1,0:T(8,128)S(1)}, f32[32,16,128]{2,1,0:T(8,128)S(1)}, u32[]{:S(2)}, u32[]{:S(2)}) collective-permute-start(f32[32,16,128]{2,1,0:T(8,128)S(1)} %all-to-all-done.2.own), channel_id=1, source_target_pairs={{1,0},{2,1},{3,2},{4,3},{5,4},{6,5},{7,6},{8,7},{9,8},{10,9},{11,1... | collective-permute-start | bytes 786440 | tf_op jit(solution)/shard_map/ppermute | solution.py:237
  44.0 2.7 %collective-permute-start.2 = (f32[32,16,128]{2,1,0:T(8,128)S(1)}, f32[32,16,128]{2,1,0:T(8,128)S(1)}, u32[]{:S(2)}, u32[]{:S(2)}) collective-permute-start(f32[32,16,128]{2,1,0:T(8,128)S(1)} %all-to-all-done.2.own), channel_id=1, source_target_pairs={{0,1},{1,2},{2,3},{3,4},{4,5},{5,6},{6,7},{7,8},{8,9},{9,10},{10,1... | collective-permute-start | bytes 786440 | tf_op jit(solution)/shard_map/ppermute | solution.py:237
  46.6 0.7 dynamic-slice_convert_fusion
  47.4 0.0 copy-done.7
  47.4 0.0 copy-start.8
  47.4 0.0 copy-start.9
  47.4 0.7 copy-done.8
  48.1 0.0 copy-done.9
  48.1 0.0 copy-start.3
  48.1 1.9 %collective-permute-start.1 = (f32[32,512]{1,0:T(8,128)S(1)}, f32[32,512]{1,0:T(8,128)S(1)}, u32[]{:S(2)}, u32[]{:S(2)}) collective-permute-start(f32[32,512]{1,0:T(8,128)S(1)} %pad_maximum_fusion.1.own), channel_id=1, source_target_pairs={{1,0},{2,1},{3,2},{4,3},{5,4},{6,5},{7,6},{8,7},{9,8},{10,9},{11,1... | collective-permute-start | bytes 196616 | tf_op jit(solution)/shard_map/ppermute | solution.py:237
  50.0 3.6 %collective-permute-start = (f32[32,512]{1,0:T(8,128)S(1)}, f32[32,512]{1,0:T(8,128)S(1)}, u32[]{:S(2)}, u32[]{:S(2)}) collective-permute-start(f32[32,512]{1,0:T(8,128)S(1)} %pad_maximum_fusion.1.own), channel_id=1, source_target_pairs={{0,1},{1,2},{2,3},{3,4},{4,5},{5,6},{6,7},{7,8},{8,9},{9,10},{10,1... | collective-permute-start | bytes 196616 | tf_op jit(solution)/shard_map/ppermute | solution.py:237
  53.7 0.0 collective-permute-done.1.after
  53.7 0.0 copy-start.5
  53.7 1.3 collective-permute-done.before
  55.0 0.0 copy-done.3
  55.0 0.0 copy-done.5
  55.0 0.0 copy-start.6
  55.0 0.6 copy-done.6
  55.6 2.0 %basis.1 = (f32[32,128]{1,0:T(8,128)}, f32[24,512]{1,0:T(8,128)}, f32[24,512]{1,0:T(8,128)}, f32[24,512]{1,0:T(8,128)}, f32[24,512]{1,0:T(8,128)}, /*index=5*/f3...) custom-call(f32[32,512]{1,0:T(8,128)} %copy-done.3, f32[32,512]{1,0:T(8,128)} %copy-done.6, f32[32,512]{1,0:T(8,128)} %copy-done.5), custom_call_target="tpu_custom_call" | custom-call | tf_op jit(solution)/shard_map/basis/pallas_call | solution.py:253
  57.6 19.8 %all_to_all.20 = f32[32,1,128]{2,1,0:T(1,128)} all-to-all(f32[32,1,128]{2,1,0:T(1,128)} %bitcast.17), channel_id=1, replica_groups=mesh['magnet'=16,'slab'=32] {'slab'}, dimensions={0} | all-to-all | bytes 32768 | tf_op jit(solution)/shard_map/all_to_all | solution.py:261
  77.4 1.3 %total.1 = f32[16,128]{1,0:T(8,128)} custom-call(f32[32,128]{1,0:T(8,128)} %bitcast.14), custom_call_target="tpu_custom_call" | custom-call | tf_op jit(solution)/shard_map/total/pallas_call | solution.py:262
  78.7 16.9 %all_to_all.21 = f32[16,1,128]{2,1,0:T(1,128)} all-to-all(f32[16,1,128]{2,1,0:T(1,128)} %bitcast.16), channel_id=1, replica_groups=mesh['magnet'=16,'slab'=32] {'magnet'}, dimensions={0} | all-to-all | bytes 16384 | tf_op jit(solution)/shard_map/all_to_all | solution.py:269
  95.7 0.0 collective-permute-done.3.after
  95.7 0.0 copy-start.1
  95.7 0.0 collective-permute-done.2.before
  95.7 0.0 copy-start.2
  95.7 0.0 copy-done
  95.7 0.7 copy-done.1
  96.4 0.1 copy-done.2
  96.5 10.8 %heat.1 = (f32[8,512]{1,0:T(8,128)}, f32[32,8,128]{2,1,0:T(8,128)}) custom-call(f32[16,128]{1,0:T(8,128)} %bitcast.15, f32[24,512]{1,0:T(8,128)} %get-tuple-element.13.w0, f32[24,512]{1,0:T(8,128)} %get-tuple-element.14.w1, f32[24,512]{1,0:T(8,128)} %get-tuple-element.15.w2, f32[24,512]{1,0:T(8,128)} %get-tuple-element.16.c_down, ...), custom_call_target="tpu_custom_call" | custom-call | tf_op jit(solution)/shard_map/heat/pallas_call | solution.py:272
  107.3 21.7 %all_to_all.22 = f32[32,8,128]{2,1,0:T(8,128)S(1)} all-to-all(f32[32,8,128]{2,1,0:T(8,128)} %get-tuple-element.21), channel_id=1, replica_groups=mesh['magnet'=16,'slab'=32] {'slab'}, dimensions={0} | all-to-all | bytes 262144 | tf_op jit(solution)/shard_map/all_to_all | solution.py:285
  128.9 0.7 copy.11
  (2 shorter events, 0.0 us)
Async XLA Ops:
  0.6 1.0 copy-start.4
  2.3 38.8 %all-to-all-start.2 = ((f32[32,16,128]{2,1,0:T(8,128)}), f32[32,16,128]{2,1,0:T(8,128)S(1)}, u32[]{:S(2)}, u32[]{:S(2)}) async-start(f32[32,16,128]{2,1,0:T(8,128)} %pad_maximum_fusion), calls=%async_computation.2 | async-start | bytes 524288 | tf_op jit(solution)/shard_map/all_to_all | solution.py:246
  19.1 28.3 %copy-start.7 = (s32[8,512]{1,0:T(8,128)S(1)}, s32[8,512]{1,0:T(8,128)}, u32[]{:S(2)}) copy-start(s32[8,512]{1,0:T(8,128)} %param.8) | copy-start | bytes 49156
  41.1 54.6 %copy-start = (f32[32,16,128]{2,1,0:T(8,128)}, f32[32,16,128]{2,1,0:T(8,128)S(1)}, u32[]{:S(2)}) copy-start(f32[32,16,128]{2,1,0:T(8,128)S(1)} %all-to-all-done.2.own) | copy-start | bytes 786436
  41.1 54.6 %collective-permute-start.3 = (f32[32,16,128]{2,1,0:T(8,128)S(1)}, f32[32,16,128]{2,1,0:T(8,128)S(1)}, u32[]{:S(2)}, u32[]{:S(2)}) collective-permute-start(f32[32,16,128]{2,1,0:T(8,128)S(1)} %all-to-all-done.2.own), channel_id=1, source_target_pairs={{1,0},{2,1},{3,2},{4,3},{5,4},{6,5},{7,6},{8,7},{9,8},{10,9},{11,1... | collective-permute-start | bytes 786440 | tf_op jit(solution)/shard_map/ppermute | solution.py:237
  44.0 51.7 %collective-permute-start.2 = (f32[32,16,128]{2,1,0:T(8,128)S(1)}, f32[32,16,128]{2,1,0:T(8,128)S(1)}, u32[]{:S(2)}, u32[]{:S(2)}) collective-permute-start(f32[32,16,128]{2,1,0:T(8,128)S(1)} %all-to-all-done.2.own), channel_id=1, source_target_pairs={{0,1},{1,2},{2,3},{3,4},{4,5},{5,6},{6,7},{7,8},{8,9},{9,10},{10,1... | collective-permute-start | bytes 786440 | tf_op jit(solution)/shard_map/ppermute | solution.py:237
  47.4 0.7 copy-start.8
  47.4 0.7 copy-start.9
  48.1 6.9 %copy-start.3 = (f32[32,512]{1,0:T(8,128)}, f32[32,512]{1,0:T(8,128)S(1)}, u32[]{:S(2)}) copy-start(f32[32,512]{1,0:T(8,128)S(1)} %pad_maximum_fusion.1.own) | copy-start | bytes 196612
  48.1 5.6 %collective-permute-start.1 = (f32[32,512]{1,0:T(8,128)S(1)}, f32[32,512]{1,0:T(8,128)S(1)}, u32[]{:S(2)}, u32[]{:S(2)}) collective-permute-start(f32[32,512]{1,0:T(8,128)S(1)} %pad_maximum_fusion.1.own), channel_id=1, source_target_pairs={{1,0},{2,1},{3,2},{4,3},{5,4},{6,5},{7,6},{8,7},{9,8},{10,9},{11,1... | collective-permute-start | bytes 196616 | tf_op jit(solution)/shard_map/ppermute | solution.py:237
  50.0 5.0 %collective-permute-start = (f32[32,512]{1,0:T(8,128)S(1)}, f32[32,512]{1,0:T(8,128)S(1)}, u32[]{:S(2)}, u32[]{:S(2)}) collective-permute-start(f32[32,512]{1,0:T(8,128)S(1)} %pad_maximum_fusion.1.own), channel_id=1, source_target_pairs={{0,1},{1,2},{2,3},{3,4},{4,5},{5,6},{6,7},{7,8},{8,9},{9,10},{10,1... | collective-permute-start | bytes 196616 | tf_op jit(solution)/shard_map/ppermute | solution.py:237
  53.7 1.3 %copy-start.5 = (f32[32,512]{1,0:T(8,128)}, f32[32,512]{1,0:T(8,128)S(1)}, u32[]{:S(2)}) copy-start(f32[32,512]{1,0:T(8,128)S(1)} %collective-permute-done.1.after) | copy-start | bytes 196612
  55.0 0.6 copy-start.6
  95.7 0.7 copy-start.1
  95.7 0.8 copy-start.2

commit v2 on v1

--- a/solution.py
+++ b/solution.py
@@ -55,7 +55,7 @@
     return jnp.where((row >= low) & (row < high), 1.0, 0.0).astype(jnp.float32)
 
 
-def basis_kernel(own, before, after, moments, w0_out, w1_out, w2_out, down_out, right_out, left_out, cells_out):
+def basis_kernel(own, before, after, warmth_in, kind_in, packed, w0_out, w1_out, w2_out, down_out, right_out, left_out, cells_out):
     def window(i):
         part = slice(ROWS * i, ROWS * (i + 1))
         return jnp.concatenate([before[part, :], own[part, :], after[part, :]], axis=0)
@@ -96,11 +96,13 @@
     line = jnp.zeros((1, 128), jnp.float32)
     for i, (u, v) in enumerate(((a, a), (a, b), (a, c), (b, b), (b, c), (c, c), (c, d))):
         line = jnp.where(lane == i, jnp.sum(u * v, keepdims=True), line)
-    moments[...] = jnp.broadcast_to(line, moments.shape)
-
-
-def sum_kernel(lines, out):
-    out[...] = jnp.broadcast_to(jnp.sum(lines[...], axis=0, keepdims=True), out.shape)
+    block = 2 * ROWS + 1
+    for slab in range(packed.shape[0] // block):
+        part = slice(ROWS * slab, ROWS * (slab + 1))
+        at = block * slab
+        packed[at : at + ROWS] = warmth_in[part]
+        packed[at + ROWS : at + 2 * ROWS] = kind_in[part].astype(jnp.float32)
+        packed[at + 2 * ROWS : at + block] = line
 
 
 def solve_small(lines):
@@ -135,9 +137,31 @@
 
 
 def heat_kernel(
-    layers, lines, w0, w1, w2, c_down, c_right, c_left, cells, own, before, after, potential, heated, warm, base, store, heat
+    layers, lines, w0, w1, w2, c_down, c_right, c_left, cells, own, before, after, potential, heated, warm, cond, base, store
 ):
     span = ROWS + 2 * HALO
+    spokes = heated.shape[-1]
+    block = own.shape[0] // layers
+    index, count = place()
+    edge = 8
+    body = slice(edge, edge + layers)
+    inward, outward = slice(edge - 1, edge - 1 + layers), slice(edge + 1, edge + 1 + layers)
+    blank = jnp.zeros((edge, spokes), jnp.float32)
+    for row in range(span):
+        source, at = (before, row + ROWS - HALO) if row < HALO else (own, row - HALO) if row < HALO + ROWS else (after, row - HALO - ROWS)
+        there = jnp.where(index > 0, 1.0, 0.0) if row < HALO else jnp.where(index < count - 1, 1.0, 0.0) if row >= HALO + ROWS else 1.0
+        kind = source[pl.ds(ROWS + at, layers, stride=block), :]
+
+        def table(values):
+            return jnp.where(kind == 0.0, values[0], jnp.where(kind == 1.0, values[1], jnp.where(kind == 2.0, values[2], values[3])))
+
+        base[row] = table(conduct_table) * there
+        store[row] = table([0.5 * time_step / c for c in capacity_table]) * there
+        warm[0, row, body] = source[pl.ds(at, layers, stride=block), :]
+        for field in (warm.at[0, row], warm.at[1, row], cond.at[row]):
+            field[0:edge] = blank
+            field[edge + layers : 2 * edge + layers] = blank
+
     f0, f1, f2 = solve_small(lines[...])
     shape = w0.shape
     inside = rows_inside(shape, ROWS)
@@ -150,75 +174,58 @@
     q_right = c_right[...] * (step * step)
     q_left = jnp.where(col == 0, c_left[...] * (x * x), left(q_right))
     joule = heat_factor * ((q_down + above(q_down)) + (q_right + q_left))
-    joule = joule[ROWS - HALO : ROWS - HALO + span]
-    cell = cells[ROWS - HALO : ROWS - HALO + span, :].astype(jnp.int32)
-    spokes = heated.shape[-1]
+
+    cell = cells[...].astype(jnp.int32)
     azimuth = cell & (spokes - 1)
-    outer = cell >= (layers - 1) * spokes
-    pieces = []
-    for part in (jnp.where(outer, 0.0, joule), jnp.where(outer, joule, 0.0)):
+    target = jnp.where(cell >= (layers - 1) * spokes, 7, 6)
+    spoke = lax.broadcasted_iota(jnp.int32, (spokes, shape[1]), 0)
+    sublane = lax.broadcasted_iota(jnp.int32, (8, shape[1]), 0)
+    heat = {}
+    for row in range(1, span - 1):
+        at = slice(row + ROWS - HALO, row + ROWS - HALO + 1)
+        pick = jnp.where(azimuth[at] == spoke, 1.0, 0.0).astype(jnp.bfloat16)
+        part = jnp.where(target[at] == sublane, joule[at], 0.0)
+        pieces = []
         for _ in range(3):
             piece = part.astype(jnp.bfloat16)
-            pieces.append(piece.astype(jnp.float32))
             part = part - piece.astype(jnp.float32)
-    stacked = jnp.concatenate(pieces, axis=0)
-    row_of = lax.rem(lax.broadcasted_iota(jnp.int32, stacked.shape, 0), span)
-    spoke = lax.broadcasted_iota(jnp.int32, (spokes, shape[1]), 0)
-    total = jnp.zeros((stacked.shape[0], spokes), jnp.float32)
-    for row in range(1, span - 1):
-        pick = jnp.where(azimuth[row : row + 1, :] == spoke, 1.0, 0.0).astype(jnp.bfloat16)
-        some = jnp.where(row_of == row, stacked, 0.0).astype(jnp.bfloat16)
-        total = total + lax.dot_general(some, pick, (((1,), (1,)), ((), ())), preferred_element_type=jnp.float32)
-    heat[0] = total[0:span] + (total[span : 2 * span] + total[2 * span : 3 * span])
-    heat[1] = total[3 * span : 4 * span] + (total[4 * span : 5 * span] + total[5 * span : 6 * span])
-
-    cut = (span, spokes)
-    there = rows_inside(cut, HALO)
-    for layer in range(layers):
-
-        def assemble(i):
-            part = slice(ROWS * i, ROWS * (i + 1))
-            return jnp.concatenate(
-                [before[layer, part][ROWS - HALO :], own[layer, part], after[layer, part][:HALO]], axis=0
-            )
-
-        kind = assemble(1)
-        conduct = jnp.where(kind == 0.0, conduct_table[0], jnp.where(kind == 1.0, conduct_table[1], jnp.where(kind == 2.0, conduct_table[2], conduct_table[3])))
-        gain = [0.5 * time_step / c for c in capacity_table]
-        gains = jnp.where(kind == 0.0, gain[0], jnp.where(kind == 1.0, gain[1], jnp.where(kind == 2.0, gain[2], gain[3])))
-        warm[0, layer] = assemble(0) * there
-        base[layer] = conduct * there
-        store[layer] = gains * there
+            pieces.append(piece)
+        total = lax.dot_general(
+            jnp.concatenate(pieces, axis=0), pick, (((1,), (1,)), ((), ())), preferred_element_type=jnp.float32
+        )
+        heat[row] = 2.0 * (total[0:8] + (total[8:16] + total[16:24]))
 
     for substep in range(SUBSTEPS):
         now, then = substep % 2, 1 - substep % 2
 
-        def conductivity(layer):
-            t = warm[now, layer]
-            return t, base[layer] * (1.0 + diffusivity_derivative * t)
-
-        t, k = conductivity(0)
-        inner = k * t
-        for layer in range(layers):
-            if layer + 1 < layers:
-                t_next, k_next = conductivity(layer + 1)
-                outer_face = (k + k_next) * (t_next - t)
+        def conductivity(row):
+            t = warm[now, row, body]
+            k = base[row] * (1.0 + diffusivity_derivative * t)
+            cond[row, body] = k
+            return t, k
+
+        def between(t, k, t_other, k_other):
+            return (k + k_other) * (t_other - t)
+
+        last = conductivity(substep)
+        here = conductivity(substep + 1)
+        inner = between(*last, *here)
+        for row in range(substep + 1, span - 1 - substep):
+            t, k = here
+            here = conductivity(row + 1)
+            outer = between(t, k, *here)
+            flux = outer - inner
+            inner = outer
+            flux = flux + between(t, k, warm[now, row, inward], cond[row, inward])
+            flux = flux + between(t, k, warm[now, row, outward], cond[row, outward])
+            face = between(t, k, right(t), right(k))
+            flux = flux + (face - left(face))
+            flux = jnp.concatenate([flux[: layers - 8], flux[layers - 8 :] + heat[row]], axis=0)
+            fresh = t + store[row] * flux
+            if substep + 1 < SUBSTEPS:
+                warm[then, row, body] = fresh
             else:
-                t_next, k_next = None, None
-                outer_face = -(k * t)
-            flux = outer_face - inner
-            face = (k + below(k)) * (below(t) - t)
-            flux = flux + (face - above(face))
-            face = (k + right(k)) * (right(t) - t)
-            flux = flux + (face - left(face))
-            if layer >= layers - 2:
-                flux = flux + 2.0 * heat[layer - (layers - 2)]
-            fresh = t + store[layer] * flux
-            if substep + 1 < SUBSTEPS:
-                warm[then, layer] = fresh
-            else:
-                heated[layer] = fresh[HALO : HALO + ROWS]
-            t, k, inner = t_next, k_next, outer_face
+                heated[pl.ds(row - HALO, layers, stride=ROWS), :] = fresh
 
 
 def vmem(count):
@@ -236,53 +243,40 @@
     def around(block):
         return lax.ppermute(block, BOTH, onward), lax.ppermute(block, BOTH, backward)
 
-    bricks = jnp.concatenate(
-        [
-            prior_block_warmth.reshape(layers, ROWS, spokes),
-            substance_kind.astype(f32).reshape(layers, ROWS, spokes),
-        ],
-        axis=1,
-    )
-    bricks = lax.all_to_all(bricks, "slab", 0, 0)
-
     cells = lax.dynamic_slice_in_dim(underlying_block_map, lax.axis_index("slab") * ROWS, ROWS, axis=0)
     sheet = jnp.concatenate(
         [foil_warmth, terminal_voltage_input, foil_segment_pattern.astype(f32), cells.astype(f32)], axis=0
     )
     field = jax.ShapeDtypeStruct((3 * ROWS, width), f32)
-    moments, *fields = pl.pallas_call(
+    block = 2 * ROWS + 1
+    packed, *fields = pl.pallas_call(
         basis_kernel,
-        out_shape=(jax.ShapeDtypeStruct((layers, 128), f32),) + (field,) * 7,
-        in_specs=vmem(3),
+        out_shape=(jax.ShapeDtypeStruct((layers * block, spokes), f32),) + (field,) * 7,
+        in_specs=vmem(5),
         out_specs=vmem(8),
         name="basis",
-    )(sheet, *around(sheet))
-
-    lines = lax.all_to_all(moments.reshape(layers, 1, 128), "slab", 0, 0).reshape(layers, 128)
-    lines = pl.pallas_call(
-        sum_kernel,
-        out_shape=jax.ShapeDtypeStruct((magnets, 128), f32),
-        in_specs=vmem(1),
-        out_specs=vmem(1)[0],
-        name="total",
-    )(lines)
-    lines = lax.all_to_all(lines.reshape(magnets, 1, 128), "magnet", 0, 0).reshape(magnets, 128)
+    )(sheet, *around(sheet), prior_block_warmth.reshape(layers * ROWS, spokes), substance_kind.reshape(layers * ROWS, spokes))
+
+    bricks = lax.all_to_all(packed.reshape(layers, block, 1, spokes), "slab", 0, 0)
+    lines = jnp.sum(bricks[:, 2 * ROWS], axis=0, keepdims=True)
+    lines = lax.all_to_all(jnp.broadcast_to(lines, (magnets, 1, spokes)), "magnet", 0, 0).reshape(magnets, spokes)
+    bricks = bricks.reshape(layers * block, spokes)
 
     span = ROWS + 2 * HALO
     potential, heated = pl.pallas_call(
         functools.partial(heat_kernel, layers),
-        out_shape=(jax.ShapeDtypeStruct((ROWS, width), f32), jax.ShapeDtypeStruct((layers, ROWS, spokes), f32)),
+        out_shape=(jax.ShapeDtypeStruct((ROWS, width), f32), jax.ShapeDtypeStruct((layers * ROWS, spokes), f32)),
         in_specs=vmem(11),
         out_specs=vmem(2),
         scratch_shapes=[
-            pltpu.VMEM((2, layers, span, spokes), f32),
-            pltpu.VMEM((layers, span, spokes), f32),
-            pltpu.VMEM((layers, span, spokes), f32),
-            pltpu.VMEM((2, span, spokes), f32),
+            pltpu.VMEM((2, span, layers + 16, spokes), f32),
+            pltpu.VMEM((span, layers + 16, spokes), f32),
+            pltpu.VMEM((span, layers, spokes), f32),
+            pltpu.VMEM((span, layers, spokes), f32),
         ],
         name="heat",
     )(lines, *fields, bricks, *around(bricks))
-    heated = lax.all_to_all(heated, "slab", 0, 0)
+    heated = lax.all_to_all(heated.reshape(layers, ROWS, spokes), "slab", 0, 0)
     return potential, heated.reshape(prior_block_warmth.shape)
 
 

time: 130 us -> 102 us (0.78)
  waiting for transfers between devices: 23.3 us -> 1.3 us
  blocking collectives: 58.4 us -> 71.7 us
  starting transfers between devices: 27.9 us -> 16.3 us
  Pallas kernels: 14.1 us -> 7.89 us
    all_to_all x1 -> x0, waiting for transfers between devices: 22 us -> none  [local(): bricks = lax.all_to_all(bricks, 'slab', 0, 0)]
    all_to_all x1 -> x0, starting transfers between devices: 16.7 us -> none  [local(): bricks = lax.all_to_all(bricks, 'slab', 0, 0)]
    all_to_all x3, blocking collectives: 58.4 us -> 71.7 us  [the longest x1 36.4 us: local(): lax.all_to_all(packed.reshape(layers, block, 1, spokes), 'slab', 0, 0)]
    ppermute x2, starting transfers between devices: 4.81 us -> 11.4 us  [around(): lax.ppermute(block, BOTH, backward)]
    pallas_call x1, Pallas kernels: 10.8 us -> 5.64 us  [local(): pl.pallas_call(functools.partial(heat_kernel, layers), out_shape=(jax.Sha...]
    ppermute x2, starting transfers between devices: 6.3 us -> 4.86 us  [around(): lax.ppermute(block, BOTH, onward)]
    pallas_call x2 -> x1, Pallas kernels: 3.3 us -> 2.25 us  [local(): pl.pallas_call(basis_kernel, out_shape=(jax.ShapeDtypeStruct((layers * bl...]
    unnamed x21 -> x17, local copies, waits for them, and re-layouts: 2.79 us -> 2.12 us
  transfers between devices with their start and end apart: 5 -> 4, of which waited for: 2 -> 1; matrix products, arithmetic and copies ran while one was open for 1% -> 0% of each run, Pallas kernels for 3% -> 0%
where the time goes in v2:
time: 102 us; the launch traced here: 101 us
  blocking collectives  71.7 us (70%)
  starting transfers between devices  16.3 us (16%)
  Pallas kernels  7.89 us (8%)
  local copies, waits for them, and re-layouts  2.13 us (2%)
  other arithmetic  1.51 us (1%)
  waiting for transfers between devices  1.3 us (1%)
    all_to_all x1, blocking collectives, local(): lax.all_to_all(packed.reshape(layers, block, 1, spokes), 'slab', 0, 0)  36.4 us
    all_to_all x1, blocking collectives, local(): heated = lax.all_to_all(heated.reshape(layers, ROWS, spokes), 'slab', 0, 0)  22.3 us
    all_to_all x1, blocking collectives, local(): lax.all_to_all(jnp.broadcast_to(lines, (magnets, 1, spokes)), 'magnet', 0...  13 us
    ppermute x2, starting transfers between devices, around(): lax.ppermute(block, BOTH, backward)  11.4 us
    pallas_call x1, Pallas kernels, local(): pl.pallas_call(functools.partial(heat_kernel, layers), out_shape=(jax.Sha...  5.64 us
    ppermute x2, starting transfers between devices, around(): lax.ppermute(block, BOTH, onward)  4.86 us
    pallas_call x1, Pallas kernels, local(): pl.pallas_call(basis_kernel, out_shape=(jax.ShapeDtypeStruct((layers * bl...  2.25 us
    unnamed x17, local copies, waits for them, and re-layouts  2.12 us
  transfers between devices with their start and end apart: 4, of which 1 were waited for; matrix products, arithmetic and copies ran while one was open for 0% of the time, Pallas kernels for 0%

profile of v2, /device:TPU:1, one launch (start us, length us, event | category | flops | bytes accessed | tf_op | source)
XLA Modules:
  0.0 101.5 jit_solution(5959881460673359523)
XLA Ops:
  0.6 0.7 convert_element_type.6
  1.4 0.0 copy-start.6
  1.4 0.0 copy-start.7
  1.4 0.7 dynamic-slice_convert_fusion
  2.1 0.0 copy-done.6
  2.1 0.0 copy-done.7
  2.1 0.0 copy-start.3
  2.1 8.8 %collective-permute-start.1 = (f32[32,512]{1,0:T(8,128)S(1)}, f32[32,512]{1,0:T(8,128)S(1)}, u32[]{:S(2)}, u32[]{:S(2)}) collective-permute-start(f32[32,512]{1,0:T(8,128)S(1)} %pad_maximum_fusion.own), channel_id=1, source_target_pairs={{1,0},{2,1},{3,2},{4,3},{5,4},{6,5},{7,6},{8,7},{9,8},{10,9},{11,1... | collective-permute-start | bytes 196616 | tf_op jit(solution)/shard_map/ppermute | solution.py:244
  10.9 1.9 %collective-permute-start = (f32[32,512]{1,0:T(8,128)S(1)}, f32[32,512]{1,0:T(8,128)S(1)}, u32[]{:S(2)}, u32[]{:S(2)}) collective-permute-start(f32[32,512]{1,0:T(8,128)S(1)} %pad_maximum_fusion.own), channel_id=1, source_target_pairs={{0,1},{1,2},{2,3},{3,4},{4,5},{5,6},{6,7},{7,8},{8,9},{9,10},{10,1... | collective-permute-start | bytes 196616 | tf_op jit(solution)/shard_map/ppermute | solution.py:244
  12.8 0.0 collective-permute-done.1.after
  12.9 0.0 copy-start.4
  12.9 1.3 %collective-permute-done.before = f32[32,512]{1,0:T(8,128)S(1)} collective-permute-done((f32[32,512]{1,0:T(8,128)S(1)}, f32[32,512]{1,0:T(8,128)S(1)}, u32[]{:S(2)}, u32[]{:S(2)}) %collective-permute-start) | collective-permute-done | bytes 65568 | tf_op jit(solution)/shard_map/ppermute | solution.py:244
  14.2 0.0 copy-start.5
  14.2 0.0 copy-done.3
  14.2 0.0 copy-done.4
  14.2 0.6 copy-done.5
  14.8 2.2 %basis.1 = (f32[544,128]{1,0:T(8,128)}, f32[24,512]{1,0:T(8,128)}, f32[24,512]{1,0:T(8,128)}, f32[24,512]{1,0:T(8,128)}, f32[24,512]{1,0:T(8,128)}, /*index=5*/f...) custom-call(f32[32,512]{1,0:T(8,128)} %copy-done.3, f32[32,512]{1,0:T(8,128)} %copy-done.5, f32[32,512]{1,0:T(8,128)} %copy-done.4, ...), custom_call_target="tpu_custom_call" | custom-call | tf_op jit(solution)/shard_map/basis/pallas_call | solution.py:252
  17.0 36.4 %all_to_all.15 = f32[32,17,1,128]{3,2,1,0:T(1,128)S(1)} all-to-all(f32[32,17,1,128]{3,2,1,0:T(1,128)} %bitcast.11), channel_id=1, replica_groups=mesh['magnet'=16,'slab'=32] {'slab'}, dimensions={0} | all-to-all | bytes 557056 | tf_op jit(solution)/shard_map/all_to_all | solution.py:260
  53.4 0.0 copy-start
  53.4 2.6 %collective-permute-start.3 = (f32[544,128]{1,0:T(8,128)S(1)}, f32[544,128]{1,0:T(8,128)S(1)}, u32[]{:S(2)}, u32[]{:S(2)}) collective-permute-start(f32[544,128]{1,0:T(8,128)S(1)} %bitcast.7), channel_id=1, source_target_pairs={{1,0},{2,1},{3,2},{4,3},{5,4},{6,5},{7,6},{8,7},{9,8},{10,9},{11,1... | collective-permute-start | bytes 835592 | tf_op jit(solution)/shard_map/ppermute | solution.py:244
  56.1 2.9 %collective-permute-start.2 = (f32[544,128]{1,0:T(8,128)S(1)}, f32[544,128]{1,0:T(8,128)S(1)}, u32[]{:S(2)}, u32[]{:S(2)}) collective-permute-start(f32[544,128]{1,0:T(8,128)S(1)} %bitcast.8), channel_id=1, source_target_pairs={{0,1},{1,2},{2,3},{3,4},{4,5},{5,6},{6,7},{7,8},{8,9},{9,10},{10,1... | collective-permute-start | bytes 835592 | tf_op jit(solution)/shard_map/ppermute | solution.py:244
  59.1 13.0 %all_to_all.16 = f32[16,1,128]{2,1,0:T(1,128)} all-to-all(f32[16,1,128]{2,1,0:T(1,128)S(1)} %broadcast_in_dim.2), channel_id=1, replica_groups=mesh['magnet'=16,'slab'=32] {'magnet'}, dimensions={0} | all-to-all | bytes 16384 | tf_op jit(solution)/shard_map/all_to_all | solution.py:262
  72.0 0.0 collective-permute-done.3.after
  72.0 0.0 copy-start.1
  72.0 0.0 collective-permute-done.2.before
  72.0 0.0 copy-start.2
  72.0 0.0 copy-done
  72.1 0.7 copy-done.1
  72.8 0.1 copy-done.2
  72.9 5.6 %heat.1 = (f32[8,512]{1,0:T(8,128)}, f32[256,128]{1,0:T(8,128)}) custom-call(f32[16,128]{1,0:T(8,128)} %bitcast.15, f32[24,512]{1,0:T(8,128)} %get-tuple-element.13.w0, f32[24,512]{1,0:T(8,128)} %get-tuple-element.14.w1, f32[24,512]{1,0:T(8,128)} %get-tuple-element.15.w2, f32[24,512]{1,0:T(8,128)} %get-tuple-element.16.c_down, ...), custom_call_target="tpu_custom_call" | custom-call | tf_op jit(solution)/shard_map/heat/pallas_call | solution.py:266
  78.5 22.3 %all_to_all.17 = f32[32,8,128]{2,1,0:T(8,128)S(1)} all-to-all(f32[32,8,128]{2,1,0:T(8,128)} %bitcast.14), channel_id=1, replica_groups=mesh['magnet'=16,'slab'=32] {'slab'}, dimensions={0} | all-to-all | bytes 262144 | tf_op jit(solution)/shard_map/all_to_all | solution.py:279
  100.8 0.7 copy.10
  (3 shorter events, 0.1 us)
Async XLA Ops:
  1.4 0.7 copy-start.6
  1.4 0.7 copy-start.7
  2.1 12.0 %copy-start.3 = (f32[32,512]{1,0:T(8,128)}, f32[32,512]{1,0:T(8,128)S(1)}, u32[]{:S(2)}) copy-start(f32[32,512]{1,0:T(8,128)S(1)} %pad_maximum_fusion.own) | copy-start | bytes 196612
  2.1 10.7 %collective-permute-start.1 = (f32[32,512]{1,0:T(8,128)S(1)}, f32[32,512]{1,0:T(8,128)S(1)}, u32[]{:S(2)}, u32[]{:S(2)}) collective-permute-start(f32[32,512]{1,0:T(8,128)S(1)} %pad_maximum_fusion.own), channel_id=1, source_target_pairs={{1,0},{2,1},{3,2},{4,3},{5,4},{6,5},{7,6},{8,7},{9,8},{10,9},{11,1... | collective-permute-start | bytes 196616 | tf_op jit(solution)/shard_map/ppermute | solution.py:244
  10.9 3.2 %collective-permute-start = (f32[32,512]{1,0:T(8,128)S(1)}, f32[32,512]{1,0:T(8,128)S(1)}, u32[]{:S(2)}, u32[]{:S(2)}) collective-permute-start(f32[32,512]{1,0:T(8,128)S(1)} %pad_maximum_fusion.own), channel_id=1, source_target_pairs={{0,1},{1,2},{2,3},{3,4},{4,5},{5,6},{6,7},{7,8},{8,9},{9,10},{10,1... | collective-permute-start | bytes 196616 | tf_op jit(solution)/shard_map/ppermute | solution.py:244
  12.9 1.3 %copy-start.4 = (f32[32,512]{1,0:T(8,128)}, f32[32,512]{1,0:T(8,128)S(1)}, u32[]{:S(2)}) copy-start(f32[32,512]{1,0:T(8,128)S(1)} %collective-permute-done.1.after) | copy-start | bytes 196612
  14.2 0.6 copy-start.5
  53.4 18.6 %copy-start = (f32[32,17,1,128]{3,2,1,0:T(1,128)}, f32[32,17,1,128]{3,2,1,0:T(1,128)S(1)}, u32[]{:S(2)}) copy-start(f32[32,17,1,128]{3,2,1,0:T(1,128)S(1)} %all_to_all.15) | copy-start | bytes 835588
  53.4 18.6 %collective-permute-start.3 = (f32[544,128]{1,0:T(8,128)S(1)}, f32[544,128]{1,0:T(8,128)S(1)}, u32[]{:S(2)}, u32[]{:S(2)}) collective-permute-start(f32[544,128]{1,0:T(8,128)S(1)} %bitcast.7), channel_id=1, source_target_pairs={{1,0},{2,1},{3,2},{4,3},{5,4},{6,5},{7,6},{8,7},{9,8},{10,9},{11,1... | collective-permute-start | bytes 835592 | tf_op jit(solution)/shard_map/ppermute | solution.py:244
  56.1 16.0 %collective-permute-start.2 = (f32[544,128]{1,0:T(8,128)S(1)}, f32[544,128]{1,0:T(8,128)S(1)}, u32[]{:S(2)}, u32[]{:S(2)}) collective-permute-start(f32[544,128]{1,0:T(8,128)S(1)} %bitcast.8), channel_id=1, source_target_pairs={{0,1},{1,2},{2,3},{3,4},{4,5},{5,6},{6,7},{7,8},{8,9},{9,10},{10,1... | collective-permute-start | bytes 835592 | tf_op jit(solution)/shard_map/ppermute | solution.py:244
  72.0 0.7 copy-start.1
  72.0 0.8 copy-start.2

commit v3 on v2

--- a/solution.py
+++ b/solution.py
@@ -136,96 +136,146 @@
     return x[0] + alpha2 * p[0], x[1] + alpha2 * p[1], alpha2 * p[2]
 
 
-def heat_kernel(
-    layers, lines, w0, w1, w2, c_down, c_right, c_left, cells, own, before, after, potential, heated, warm, cond, base, store
-):
-    span = ROWS + 2 * HALO
-    spokes = heated.shape[-1]
-    block = own.shape[0] // layers
-    index, count = place()
-    edge = 8
-    body = slice(edge, edge + layers)
-    inward, outward = slice(edge - 1, edge - 1 + layers), slice(edge + 1, edge + 1 + layers)
-    blank = jnp.zeros((edge, spokes), jnp.float32)
-    for row in range(span):
-        source, at = (before, row + ROWS - HALO) if row < HALO else (own, row - HALO) if row < HALO + ROWS else (after, row - HALO - ROWS)
-        there = jnp.where(index > 0, 1.0, 0.0) if row < HALO else jnp.where(index < count - 1, 1.0, 0.0) if row >= HALO + ROWS else 1.0
-        kind = source[pl.ds(ROWS + at, layers, stride=block), :]
-
-        def table(values):
-            return jnp.where(kind == 0.0, values[0], jnp.where(kind == 1.0, values[1], jnp.where(kind == 2.0, values[2], values[3])))
-
-        base[row] = table(conduct_table) * there
-        store[row] = table([0.5 * time_step / c for c in capacity_table]) * there
-        warm[0, row, body] = source[pl.ds(at, layers, stride=block), :]
-        for field in (warm.at[0, row], warm.at[1, row], cond.at[row]):
-            field[0:edge] = blank
-            field[edge + layers : 2 * edge + layers] = blank
-
-    f0, f1, f2 = solve_small(lines[...])
+PAIRS = ((0, 0), (0, 1), (0, 2), (1, 1), (1, 2), (2, 2))
+SPAN = ROWS + 2 * HALO
+EDGE = 8
+
+
+def deposit_kernel(layers, w0, w1, w2, c_down, c_right, c_left, cells, bins, heats):
+    spokes = bins.shape[-1]
     shape = w0.shape
     inside = rows_inside(shape, ROWS)
-    x = (f0 * w0[...] + f1 * w1[...] + f2 * w2[...]) * inside
-    potential[...] = x[ROWS : 2 * ROWS]
     col = lax.broadcasted_iota(jnp.int32, shape, 1)
-    step = x - below(x)
-    q_down = c_down[...] * (step * step)
-    step = x - jnp.where(col == shape[1] - 1, 0.0, right(x))
-    q_right = c_right[...] * (step * step)
-    q_left = jnp.where(col == 0, c_left[...] * (x * x), left(q_right))
-    joule = heat_factor * ((q_down + above(q_down)) + (q_right + q_left))
-
-    cell = cells[...].astype(jnp.int32)
+    last, first = col == shape[1] - 1, col == 0
+    fields = [w[...] * inside for w in (w0, w1, w2)]
+    falls = [w - below(w) for w in fields]
+    steps = [w - jnp.where(last, 0.0, right(w)) for w in fields]
+    wanted = slice(ROWS - HALO, ROWS - HALO + SPAN)
+    for pair, (i, j) in enumerate(PAIRS):
+        q_down = c_down[...] * (falls[i] * falls[j])
+        q_right = c_right[...] * (steps[i] * steps[j])
+        q_left = jnp.where(first, c_left[...] * (fields[i] * fields[j]), left(q_right))
+        joule = (q_down + above(q_down)) + (q_right + q_left)
+        factor = heat_factor if i == j else 2.0 * heat_factor
+        joule = factor * joule[wanted]
+        for part in range(heats.shape[0]):
+            heats[part, SPAN * pair : SPAN * (pair + 1)] = joule[:, 128 * part : 128 * (part + 1)]
+    for part in range(heats.shape[0]):
+        heats[part, SPAN * len(PAIRS) :] = jnp.zeros((SPAN * (8 - len(PAIRS)), 128), jnp.float32)
+    cell = cells[wanted].astype(jnp.int32)
     azimuth = cell & (spokes - 1)
-    target = jnp.where(cell >= (layers - 1) * spokes, 7, 6)
+    outermost = jnp.where(cell >= (layers - 1) * spokes, 1.0, 0.0)
     spoke = lax.broadcasted_iota(jnp.int32, (spokes, shape[1]), 0)
-    sublane = lax.broadcasted_iota(jnp.int32, (8, shape[1]), 0)
-    heat = {}
-    for row in range(1, span - 1):
-        at = slice(row + ROWS - HALO, row + ROWS - HALO + 1)
-        pick = jnp.where(azimuth[at] == spoke, 1.0, 0.0).astype(jnp.bfloat16)
-        part = jnp.where(target[at] == sublane, joule[at], 0.0)
+    for row in range(1, SPAN - 1):
+        pick = jnp.where(azimuth[row : row + 1] == spoke, 1.0, 0.0).astype(jnp.bfloat16)
+        joule = jnp.concatenate([heats[part, pl.ds(row, 8, stride=SPAN), :] for part in range(heats.shape[0])], axis=1)
+        upper = joule * outermost[row : row + 1]
         pieces = []
-        for _ in range(3):
-            piece = part.astype(jnp.bfloat16)
-            part = part - piece.astype(jnp.float32)
-            pieces.append(piece)
+        for part in (joule - upper, upper):
+            for _ in range(3):
+                piece = part.astype(jnp.bfloat16)
+                part = part - piece.astype(jnp.float32)
+                pieces.append(piece)
         total = lax.dot_general(
             jnp.concatenate(pieces, axis=0), pick, (((1,), (1,)), ((), ())), preferred_element_type=jnp.float32
         )
-        heat[row] = 2.0 * (total[0:8] + (total[8:16] + total[16:24]))
-
-    for substep in range(SUBSTEPS):
-        now, then = substep % 2, 1 - substep % 2
-
-        def conductivity(row):
-            t = warm[now, row, body]
-            k = base[row] * (1.0 + diffusivity_derivative * t)
-            cond[row, body] = k
-            return t, k
-
-        def between(t, k, t_other, k_other):
-            return (k + k_other) * (t_other - t)
-
-        last = conductivity(substep)
-        here = conductivity(substep + 1)
-        inner = between(*last, *here)
-        for row in range(substep + 1, span - 1 - substep):
-            t, k = here
-            here = conductivity(row + 1)
-            outer = between(t, k, *here)
-            flux = outer - inner
-            inner = outer
-            flux = flux + between(t, k, warm[now, row, inward], cond[row, inward])
-            flux = flux + between(t, k, warm[now, row, outward], cond[row, outward])
-            face = between(t, k, right(t), right(k))
-            flux = flux + (face - left(face))
-            flux = jnp.concatenate([flux[: layers - 8], flux[layers - 8 :] + heat[row]], axis=0)
-            fresh = t + store[row] * flux
+        bins[row, 0:8] = total[0:8] + (total[8:16] + total[16:24])
+        bins[row, 8:16] = total[24:32] + (total[32:40] + total[40:48])
+
+
+def substep_rows(rows, layers, warm, cond, base, done):
+    body = slice(EDGE, EDGE + layers)
+    inward, outward = slice(EDGE - 1, EDGE - 1 + layers), slice(EDGE + 1, EDGE + 1 + layers)
+
+    def conductivity(row):
+        t = warm[row, body]
+        k = base[row] * (1.0 + diffusivity_derivative * t)
+        cond[row, body] = k
+        return t, k
+
+    def between(t, k, t_other, k_other):
+        return (k + k_other) * (t_other - t)
+
+    below_row = conductivity(rows[0] - 1)
+    here = conductivity(rows[0])
+    inner = between(*below_row, *here)
+    for row in rows:
+        t, k = here
+        here = conductivity(row + 1)
+        outer = between(t, k, *here)
+        flux = outer - inner
+        inner = outer
+        flux = flux + between(t, k, warm[row, inward], cond[row, inward])
+        flux = flux + between(t, k, warm[row, outward], cond[row, outward])
+        face = between(t, k, right(t), right(k))
+        done(row, t, flux + (face - left(face)))
+
+
+def clear_edges(layers, *fields):
+    for field in fields:
+        blank = jnp.zeros((EDGE, field.shape[-1]), jnp.float32)
+        field[0:EDGE] = blank
+        field[EDGE + layers : 2 * EDGE + layers] = blank
+
+
+def first_kernel(layers, own, before, after, fresh, base, store, warm, cond):
+    block = own.shape[0] // layers
+    index, count = place()
+    body = slice(EDGE, EDGE + layers)
+    for row in range(SPAN):
+        source, at, there = own, row - HALO, 1.0
+        if row < HALO:
+            source, at, there = before, row + ROWS - HALO, jnp.where(index > 0, 1.0, 0.0)
+        elif row >= HALO + ROWS:
+            source, at, there = after, row - HALO - ROWS, jnp.where(index < count - 1, 1.0, 0.0)
+        kind = source[pl.ds(ROWS + at, layers, stride=block), :]
+
+        def table(values):
+            return jnp.where(kind == 0.0, values[0], jnp.where(kind == 1.0, values[1], jnp.where(kind == 2.0, values[2], values[3])))
+
+        base[row] = table(conduct_table) * there
+        store[row] = table([0.5 * time_step / c for c in capacity_table]) * there
+        warm[row, body] = source[pl.ds(at, layers, stride=block), :]
+        clear_edges(layers, warm.at[row], cond.at[row], fresh.at[row])
+
+    def done(row, t, flux):
+        fresh[row, body] = t + store[row] * flux
+
+    substep_rows(range(1, SPAN - 1), layers, warm, cond, base, done)
+
+
+def heat_kernel(layers, lines, w0, w1, w2, bins, fresh, base, store, potential, heated, warm, cond):
+    spokes = heated.shape[-1]
+    body = slice(EDGE, EDGE + layers)
+    f = solve_small(lines[...])
+    own = slice(ROWS, 2 * ROWS)
+    potential[...] = f[0] * w0[own] + f[1] * w1[own] + f[2] * w2[own]
+    sublane = lax.broadcasted_iota(jnp.int32, (8, spokes), 0)
+    weight = jnp.zeros((8, spokes), jnp.float32)
+    for pair, (i, j) in enumerate(PAIRS):
+        weight = jnp.where(sublane == pair, f[i] * f[j], weight)
+    weight = 2.0 * weight
+    heat = {}
+    top = slice(layers - 8, layers)
+    for row in range(1, SPAN - 1):
+        inner = jnp.sum(weight * bins[row, 0:8], axis=0, keepdims=True)
+        outer = jnp.sum(weight * bins[row, 8:16], axis=0, keepdims=True)
+        heat[row] = jnp.where(sublane == 6, inner, jnp.where(sublane == 7, outer, 0.0))
+        warm[1, row] = fresh[row]
+        warm[1, row, EDGE + layers - 8 : EDGE + layers] = fresh[row, EDGE + layers - 8 : EDGE + layers] + store[row, top] * heat[row]
+        clear_edges(layers, warm.at[0, row], cond.at[row])
+
+    for substep in range(1, SUBSTEPS):
+
+        def done(row, t, flux):
+            flux = jnp.concatenate([flux[: layers - 8], flux[top] + heat[row]], axis=0)
+            t = t + store[row] * flux
             if substep + 1 < SUBSTEPS:
-                warm[then, row, body] = fresh
+                warm[1 - substep % 2, row, body] = t
             else:
-                heated[pl.ds(row - HALO, layers, stride=ROWS), :] = fresh
+                heated[pl.ds(row - HALO, layers, stride=ROWS), :] = t
+
+        substep_rows(range(substep + 1, SPAN - 1 - substep), layers, warm.at[substep % 2], cond, base, done)
 
 
 def vmem(count):
@@ -258,24 +308,39 @@
     )(sheet, *around(sheet), prior_block_warmth.reshape(layers * ROWS, spokes), substance_kind.reshape(layers * ROWS, spokes))
 
     bricks = lax.all_to_all(packed.reshape(layers, block, 1, spokes), "slab", 0, 0)
+    bins = pl.pallas_call(
+        functools.partial(deposit_kernel, layers),
+        out_shape=jax.ShapeDtypeStruct((SPAN, 16, spokes), f32),
+        in_specs=vmem(7),
+        out_specs=vmem(1)[0],
+        scratch_shapes=[pltpu.VMEM((width // 128, 8 * SPAN, 128), f32)],
+        cost_estimate=pl.CostEstimate(flops=10**8, bytes_accessed=2 * 10**6, transcendentals=0),
+        name="deposit",
+    )(*fields)
     lines = jnp.sum(bricks[:, 2 * ROWS], axis=0, keepdims=True)
-    lines = lax.all_to_all(jnp.broadcast_to(lines, (magnets, 1, spokes)), "magnet", 0, 0).reshape(magnets, spokes)
-    bricks = bricks.reshape(layers * block, spokes)
-
-    span = ROWS + 2 * HALO
+    lines = jnp.broadcast_to(lines, (magnets, 1, spokes))
+    lines, bricks, bins = lax.optimization_barrier((lines, bricks.reshape(layers * block, spokes), bins))
+    lines = lax.all_to_all(lines, "magnet", 0, 0).reshape(magnets, spokes)
+
+    padded = (SPAN, layers + 2 * EDGE, spokes)
+    plain = (SPAN, layers, spokes)
+    stage = pl.pallas_call(
+        functools.partial(first_kernel, layers),
+        out_shape=tuple(jax.ShapeDtypeStruct(dims, f32) for dims in (padded, plain, plain)),
+        in_specs=vmem(3),
+        out_specs=vmem(3),
+        scratch_shapes=[pltpu.VMEM(padded, f32), pltpu.VMEM(padded, f32)],
+        cost_estimate=pl.CostEstimate(flops=10**7, bytes_accessed=2 * 10**6, transcendentals=0),
+        name="first",
+    )(bricks, *around(bricks))
     potential, heated = pl.pallas_call(
         functools.partial(heat_kernel, layers),
         out_shape=(jax.ShapeDtypeStruct((ROWS, width), f32), jax.ShapeDtypeStruct((layers * ROWS, spokes), f32)),
-        in_specs=vmem(11),
+        in_specs=vmem(8),
         out_specs=vmem(2),
-        scratch_shapes=[
-            pltpu.VMEM((2, span, layers + 16, spokes), f32),
-            pltpu.VMEM((span, layers + 16, spokes), f32),
-            pltpu.VMEM((span, layers, spokes), f32),
-            pltpu.VMEM((span, layers, spokes), f32),
-        ],
+        scratch_shapes=[pltpu.VMEM((2,) + padded, f32), pltpu.VMEM(padded, f32)],
         name="heat",
-    )(lines, *fields, bricks, *around(bricks))
+    )(lines, *fields[:3], bins, *stage)
     heated = lax.all_to_all(heated.reshape(layers, ROWS, spokes), "slab", 0, 0)
     return potential, heated.reshape(prior_block_warmth.shape)
 

time: 102 us -> 100 us (0.980)
  blocking collectives: 71.7 us -> 22.3 us
  waiting for transfers between devices: 1.3 us -> 24.2 us
  starting transfers between devices: 16.3 us -> 36.5 us
  Pallas kernels: 7.89 us -> 10.7 us
  local copies, waits for them, and re-layouts: 2.13 us -> 3.93 us
    all_to_all x2 -> x0, blocking collectives: 49.4 us -> none  [the longest x1 36.4 us: local(): lax.all_to_all(packed.reshape(layers, block, 1, spokes), 'slab', 0, 0)]
    all_to_all x0 -> x2, waiting for transfers between devices: none -> 22.9 us  [the longest x1 20.4 us: local(): lax.all_to_all(packed.reshape(layers, block, 1, spokes), 'slab', 0, 0)]
    all_to_all x0 -> x2, starting transfers between devices: none -> 20.2 us  [the longest x1 13.4 us: local(): lax.all_to_all(packed.reshape(layers, block, 1, spokes), 'slab', 0, 0)]
    pallas_call x0 -> x2, Pallas kernels: none -> 5.01 us  [the longest x1 2.6 us: local(): pl.pallas_call(functools.partial(deposit_kernel, layers), out_shape=jax.S...]
    pallas_call x1, Pallas kernels: 5.64 us -> 3.4 us  [local(): pl.pallas_call(functools.partial(heat_kernel, layers), out_shape=(jax.Sha...]
    unnamed x17 -> x19, local copies, waits for them, and re-layouts: 2.12 us -> 3.29 us
  transfers between devices with their start and end apart: 4 -> 6, of which waited for: 1 -> 3; matrix products, arithmetic and copies ran while one was open for 0% -> 0% of each run, Pallas kernels for 0% -> 5%
where the time goes in v3:
time: 100 us; the launch traced here: 99.8 us
  starting transfers between devices  36.5 us (36%)
  waiting for transfers between devices  24.2 us (24%)
  blocking collectives  22.3 us (22%)
  Pallas kernels  10.7 us (11%)
  local copies, waits for them, and re-layouts  3.93 us (4%)
  other arithmetic  1.51 us (2%)
    all_to_all x1, blocking collectives, local(): heated = lax.all_to_all(heated.reshape(layers, ROWS, spokes), 'slab', 0, 0)  22.3 us
    all_to_all x1, waiting for transfers between devices, local(): lax.all_to_all(packed.reshape(layers, block, 1, spokes), 'slab', 0, 0)  20.4 us
    all_to_all x1, starting transfers between devices, local(): lax.all_to_all(packed.reshape(layers, block, 1, spokes), 'slab', 0, 0)  13.4 us
    ppermute x2, starting transfers between devices, around(): lax.ppermute(block, BOTH, backward)  11.4 us
    all_to_all x1, starting transfers between devices, local(): lines = lax.all_to_all(lines, 'magnet', 0, 0).reshape(magnets, spokes)  6.77 us
    ppermute x2, starting transfers between devices, around(): lax.ppermute(block, BOTH, onward)  4.86 us
    pallas_call x1, Pallas kernels, local(): pl.pallas_call(functools.partial(heat_kernel, layers), out_shape=(jax.Sha...  3.4 us
    unnamed x19, local copies, waits for them, and re-layouts  3.29 us
  transfers between devices with their start and end apart: 6, of which 3 were waited for; matrix products, arithmetic and copies ran while one was open for 0% of the time, Pallas kernels for 5%

profile of v3, /device:TPU:1, one launch (start us, length us, event | category | flops | bytes accessed | tf_op | source)
XLA Modules:
  0.0 99.8 jit_solution(17736038374372854687)
XLA Ops:
  0.6 0.7 convert_element_type.6
  1.4 0.0 copy-start.7
  1.4 0.0 copy-start.8
  1.4 0.7 dynamic-slice_convert_fusion
  2.1 0.0 copy-done.7
  2.1 0.0 copy-done.8
  2.1 0.0 copy-start.3
  2.1 8.8 %collective-permute-start.1 = (f32[32,512]{1,0:T(8,128)S(1)}, f32[32,512]{1,0:T(8,128)S(1)}, u32[]{:S(2)}, u32[]{:S(2)}) collective-permute-start(f32[32,512]{1,0:T(8,128)S(1)} %pad_maximum_fusion.own), channel_id=1, source_target_pairs={{1,0},{2,1},{3,2},{4,3},{5,4},{6,5},{7,6},{8,7},{9,8},{10,9},{11,1... | collective-permute-start | bytes 196616 | tf_op jit(solution)/shard_map/ppermute | solution.py:294
  10.9 1.9 %collective-permute-start = (f32[32,512]{1,0:T(8,128)S(1)}, f32[32,512]{1,0:T(8,128)S(1)}, u32[]{:S(2)}, u32[]{:S(2)}) collective-permute-start(f32[32,512]{1,0:T(8,128)S(1)} %pad_maximum_fusion.own), channel_id=1, source_target_pairs={{0,1},{1,2},{2,3},{3,4},{4,5},{5,6},{6,7},{7,8},{8,9},{9,10},{10,1... | collective-permute-start | bytes 196616 | tf_op jit(solution)/shard_map/ppermute | solution.py:294
  12.8 0.0 collective-permute-done.1.after
  12.9 0.0 copy-start.4
  12.9 1.3 %collective-permute-done.before = f32[32,512]{1,0:T(8,128)S(1)} collective-permute-done((f32[32,512]{1,0:T(8,128)S(1)}, f32[32,512]{1,0:T(8,128)S(1)}, u32[]{:S(2)}, u32[]{:S(2)}) %collective-permute-start) | collective-permute-done | bytes 65568 | tf_op jit(solution)/shard_map/ppermute | solution.py:294
  14.2 0.0 copy-start.5
  14.2 0.0 copy-done.3
  14.2 0.0 copy-done.4
  14.2 0.6 copy-done.5
  14.8 2.2 %basis.1 = (f32[544,128]{1,0:T(8,128)}, f32[24,512]{1,0:T(8,128)}, f32[24,512]{1,0:T(8,128)}, f32[24,512]{1,0:T(8,128)}, f32[24,512]{1,0:T(8,128)}, /*index=5*/f...) custom-call(f32[32,512]{1,0:T(8,128)} %copy-done.3, f32[32,512]{1,0:T(8,128)} %copy-done.5, f32[32,512]{1,0:T(8,128)} %copy-done.4, ...), custom_call_target="tpu_custom_call" | custom-call | tf_op jit(solution)/shard_map/basis/pallas_call | solution.py:302
  17.0 13.4 %all-to-all-start = ((f32[32,17,1,128]{3,2,1,0:T(1,128)}), f32[32,17,1,128]{3,2,1,0:T(1,128)S(1)}, u32[]{:S(2)}, u32[]{:S(2)}) async-start(f32[32,17,1,128]{3,2,1,0:T(1,128)} %bitcast.11), calls=%async_computation | async-start | bytes 557056 | tf_op jit(solution)/shard_map/all_to_all | solution.py:310
  30.5 2.6 %deposit.1.bins = f32[16,16,128]{2,1,0:T(8,128)} custom-call(f32[24,512]{1,0:T(8,128)} %get-tuple-element.19.w0, f32[24,512]{1,0:T(8,128)} %get-tuple-element.20.w1, f32[24,512]{1,0:T(8,128)} %get-tuple-element.21.w2, f32[24,512]{1,0:T(8,128)} %get-tuple-element.22.c_down, f32[24,512]{1,0:T(8,128)} %get-tuple-element.23.c_right, ...), custom_call_target="tpu_custom_call" | custom-call | flops 100000000 | bytes 2000000 | tf_op jit(solution)/shard_map/deposit/pallas_call | solution.py:311
  33.1 20.4 %all-to-all-done = f32[32,17,1,128]{3,2,1,0:T(1,128)S(1)} async-done(((f32[32,17,1,128]{3,2,1,0:T(1,128)}), f32[32,17,1,128]{3,2,1,0:T(1,128)S(1)}, u32[]{:S(2)}, u32[]{:S(2)}) %all-to-all-start) | async-done | bytes 278560 | tf_op jit(solution)/shard_map/all_to_all | solution.py:310
  53.5 0.0 copy-start
  53.5 0.6 broadcast_in_dim.2
  54.1 2.6 %collective-permute-start.3 = (f32[544,128]{1,0:T(8,128)S(1)}, f32[544,128]{1,0:T(8,128)S(1)}, u32[]{:S(2)}, u32[]{:S(2)}) collective-permute-start(f32[544,128]{1,0:T(8,128)S(1)} %bitcast.7), channel_id=1, source_target_pairs={{1,0},{2,1},{3,2},{4,3},{5,4},{6,5},{7,6},{8,7},{9,8},{10,9},{11,1... | collective-permute-start | bytes 835592 | tf_op jit(solution)/shard_map/ppermute | solution.py:294
  56.8 2.9 %collective-permute-start.2 = (f32[544,128]{1,0:T(8,128)S(1)}, f32[544,128]{1,0:T(8,128)S(1)}, u32[]{:S(2)}, u32[]{:S(2)}) collective-permute-start(f32[544,128]{1,0:T(8,128)S(1)} %bitcast.8), channel_id=1, source_target_pairs={{0,1},{1,2},{2,3},{3,4},{4,5},{5,6},{6,7},{7,8},{8,9},{9,10},{10,1... | collective-permute-start | bytes 835592 | tf_op jit(solution)/shard_map/ppermute | solution.py:294
  59.7 6.8 %all-to-all-start.1 = ((f32[16,1,128]{2,1,0:T(1,128)}), f32[16,1,128]{2,1,0:T(1,128)S(1)}, u32[]{:S(2)}, u32[]{:S(2)}) async-start(f32[16,1,128]{2,1,0:T(1,128)} %broadcast_in_dim.2), calls=%async_computation.1 | async-start | bytes 16384 | tf_op jit(solution)/shard_map/all_to_all | solution.py:323
  66.5 0.0 collective-permute-done.3.after
  66.5 0.0 copy-start.1
  66.5 0.0 collective-permute-done.2.before
  66.5 0.0 copy-done
  66.5 0.7 copy-done.1
  67.2 0.0 copy-start.2
  67.2 0.7 copy-done.2
  67.9 2.4 %first.1 = (f32[16,48,128]{2,1,0:T(8,128)}, f32[16,32,128]{2,1,0:T(8,128)}, f32[16,32,128]{2,1,0:T(8,128)}) custom-call(f32[544,128]{1,0:T(8,128)} %bitcast.9, f32[544,128]{1,0:T(8,128)} %copy-done.2, f32[544,128]{1,0:T(8,128)} %copy-done.1), custom_call_target="tpu_custom_call" | custom-call | flops 10000000 | bytes 2000000 | tf_op jit(solution)/shard_map/first/pallas_call | solution.py:327
  70.3 2.5 %all-to-all-done.1 = f32[16,1,128]{2,1,0:T(1,128)S(1)} async-done(((f32[16,1,128]{2,1,0:T(1,128)}), f32[16,1,128]{2,1,0:T(1,128)S(1)}, u32[]{:S(2)}, u32[]{:S(2)}) %all-to-all-start.1) | async-done | bytes 8224 | tf_op jit(solution)/shard_map/all_to_all | solution.py:323
  72.9 0.0 copy-start.6
  72.9 0.6 copy-done.6
  73.5 3.4 %heat.1 = (f32[8,512]{1,0:T(8,128)}, f32[256,128]{1,0:T(8,128)}) custom-call(f32[16,128]{1,0:T(8,128)} %bitcast.15, f32[24,512]{1,0:T(8,128)} %get-tuple-element.19.w0, f32[24,512]{1,0:T(8,128)} %get-tuple-element.20.w1, f32[24,512]{1,0:T(8,128)} %get-tuple-element.21.w2, f32[16,16,128]{2,1,0:T(8,128)} %deposit.1.bins, ...), custom_call_target="tpu_custom_call" | custom-call | tf_op jit(solution)/shard_map/heat/pallas_call | solution.py:336
  76.9 22.3 %all_to_all.15 = f32[32,8,128]{2,1,0:T(8,128)S(1)} all-to-all(f32[32,8,128]{2,1,0:T(8,128)} %bitcast.14), channel_id=1, replica_groups=mesh['magnet'=16,'slab'=32] {'slab'}, dimensions={0} | all-to-all | bytes 262144 | tf_op jit(solution)/shard_map/all_to_all | solution.py:344
  99.2 0.7 copy.10
  (2 shorter events, 0.1 us)
Async XLA Ops:
  1.4 0.7 copy-start.7
  1.4 0.7 copy-start.8
  2.1 12.0 %copy-start.3 = (f32[32,512]{1,0:T(8,128)}, f32[32,512]{1,0:T(8,128)S(1)}, u32[]{:S(2)}) copy-start(f32[32,512]{1,0:T(8,128)S(1)} %pad_maximum_fusion.own) | copy-start | bytes 196612
  2.1 10.7 %collective-permute-start.1 = (f32[32,512]{1,0:T(8,128)S(1)}, f32[32,512]{1,0:T(8,128)S(1)}, u32[]{:S(2)}, u32[]{:S(2)}) collective-permute-start(f32[32,512]{1,0:T(8,128)S(1)} %pad_maximum_fusion.own), channel_id=1, source_target_pairs={{1,0},{2,1},{3,2},{4,3},{5,4},{6,5},{7,6},{8,7},{9,8},{10,9},{11,1... | collective-permute-start | bytes 196616 | tf_op jit(solution)/shard_map/ppermute | solution.py:294
  10.9 3.2 %collective-permute-start = (f32[32,512]{1,0:T(8,128)S(1)}, f32[32,512]{1,0:T(8,128)S(1)}, u32[]{:S(2)}, u32[]{:S(2)}) collective-permute-start(f32[32,512]{1,0:T(8,128)S(1)} %pad_maximum_fusion.own), channel_id=1, source_target_pairs={{0,1},{1,2},{2,3},{3,4},{4,5},{5,6},{6,7},{7,8},{8,9},{9,10},{10,1... | collective-permute-start | bytes 196616 | tf_op jit(solution)/shard_map/ppermute | solution.py:294
  12.9 1.3 %copy-start.4 = (f32[32,512]{1,0:T(8,128)}, f32[32,512]{1,0:T(8,128)S(1)}, u32[]{:S(2)}) copy-start(f32[32,512]{1,0:T(8,128)S(1)} %collective-permute-done.1.after) | copy-start | bytes 196612
  14.2 0.6 copy-start.5
  17.0 36.4 %all-to-all-start = ((f32[32,17,1,128]{3,2,1,0:T(1,128)}), f32[32,17,1,128]{3,2,1,0:T(1,128)S(1)}, u32[]{:S(2)}, u32[]{:S(2)}) async-start(f32[32,17,1,128]{3,2,1,0:T(1,128)} %bitcast.11), calls=%async_computation | async-start | bytes 557056 | tf_op jit(solution)/shard_map/all_to_all | solution.py:310
  53.5 13.1 %copy-start = (f32[32,17,1,128]{3,2,1,0:T(1,128)}, f32[32,17,1,128]{3,2,1,0:T(1,128)S(1)}, u32[]{:S(2)}) copy-start(f32[32,17,1,128]{3,2,1,0:T(1,128)S(1)} %all-to-all-done) | copy-start | bytes 835588
  54.1 12.3 %collective-permute-start.3 = (f32[544,128]{1,0:T(8,128)S(1)}, f32[544,128]{1,0:T(8,128)S(1)}, u32[]{:S(2)}, u32[]{:S(2)}) collective-permute-start(f32[544,128]{1,0:T(8,128)S(1)} %bitcast.7), channel_id=1, source_target_pairs={{1,0},{2,1},{3,2},{4,3},{5,4},{6,5},{7,6},{8,7},{9,8},{10,9},{11,1... | collective-permute-start | bytes 835592 | tf_op jit(solution)/shard_map/ppermute | solution.py:294
  56.8 9.7 %collective-permute-start.2 = (f32[544,128]{1,0:T(8,128)S(1)}, f32[544,128]{1,0:T(8,128)S(1)}, u32[]{:S(2)}, u32[]{:S(2)}) collective-permute-start(f32[544,128]{1,0:T(8,128)S(1)} %bitcast.8), channel_id=1, source_target_pairs={{0,1},{1,2},{2,3},{3,4},{4,5},{5,6},{6,7},{7,8},{8,9},{9,10},{10,1... | collective-permute-start | bytes 835592 | tf_op jit(solution)/shard_map/ppermute | solution.py:294
  59.7 13.2 %all-to-all-start.1 = ((f32[16,1,128]{2,1,0:T(1,128)}), f32[16,1,128]{2,1,0:T(1,128)S(1)}, u32[]{:S(2)}, u32[]{:S(2)}) async-start(f32[16,1,128]{2,1,0:T(1,128)} %broadcast_in_dim.2), calls=%async_computation.1 | async-start | bytes 16384 | tf_op jit(solution)/shard_map/all_to_all | solution.py:323
  66.5 0.7 copy-start.1
  67.2 0.7 copy-start.2
  72.9 0.6 copy-start.6

commit v4 on v3

--- a/solution.py
+++ b/solution.py
@@ -304,6 +304,7 @@
         out_shape=(jax.ShapeDtypeStruct((layers * block, spokes), f32),) + (field,) * 7,
         in_specs=vmem(5),
         out_specs=vmem(8),
+        compiler_params=pltpu.CompilerParams(vmem_limit_bytes=8388608),
         name="basis",
     )(sheet, *around(sheet), prior_block_warmth.reshape(layers * ROWS, spokes), substance_kind.reshape(layers * ROWS, spokes))
 
@@ -315,6 +316,7 @@
         out_specs=vmem(1)[0],
         scratch_shapes=[pltpu.VMEM((width // 128, 8 * SPAN, 128), f32)],
         cost_estimate=pl.CostEstimate(flops=10**8, bytes_accessed=2 * 10**6, transcendentals=0),
+        compiler_params=pltpu.CompilerParams(vmem_limit_bytes=8388608),
         name="deposit",
     )(*fields)
     lines = jnp.sum(bricks[:, 2 * ROWS], axis=0, keepdims=True)
@@ -331,6 +333,7 @@
         out_specs=vmem(3),
         scratch_shapes=[pltpu.VMEM(padded, f32), pltpu.VMEM(padded, f32)],
         cost_estimate=pl.CostEstimate(flops=10**7, bytes_accessed=2 * 10**6, transcendentals=0),
+        compiler_params=pltpu.CompilerParams(vmem_limit_bytes=8388608),
         name="first",
     )(bricks, *around(bricks))
     potential, heated = pl.pallas_call(
@@ -339,6 +342,7 @@
         in_specs=vmem(8),
         out_specs=vmem(2),
         scratch_shapes=[pltpu.VMEM((2,) + padded, f32), pltpu.VMEM(padded, f32)],
+        compiler_params=pltpu.CompilerParams(vmem_limit_bytes=8388608),
         name="heat",
     )(lines, *fields[:3], bins, *stage)
     heated = lax.all_to_all(heated.reshape(layers, ROWS, spokes), "slab", 0, 0)

time: 100 us -> 97.7 us (0.977)
  Pallas kernels: 10.7 us -> 4.1 us
  waiting for transfers between devices: 24.2 us -> 29.2 us
  local copies, waits for them, and re-layouts: 3.93 us -> 2.17 us
    all_to_all x1, waiting for transfers between devices: 2.54 us -> 5.93 us  [local(): lines = lax.all_to_all(lines, 'magnet', 0, 0).reshape(magnets, spokes)]
    pallas_call x1, Pallas kernels: 2.41 us -> 0.43 us  [local(): pl.pallas_call(functools.partial(first_kernel, layers), out_shape=tuple((...]
    pallas_call x1, Pallas kernels: 3.4 us -> 1.48 us  [local(): pl.pallas_call(functools.partial(heat_kernel, layers), out_shape=(jax.Sha...]
    unnamed x19 -> x5, local copies, waits for them, and re-layouts: 3.29 us -> 1.56 us
    pallas_call x1, Pallas kernels: 2.6 us -> 1.01 us  [local(): pl.pallas_call(functools.partial(deposit_kernel, layers), out_shape=jax.S...]
    all_to_all x1, waiting for transfers between devices: 20.4 us -> 22 us  [local(): lax.all_to_all(packed.reshape(layers, block, 1, spokes), 'slab', 0, 0)]
    pallas_call x1, Pallas kernels: 2.25 us -> 1.18 us  [local(): pl.pallas_call(basis_kernel, out_shape=(jax.ShapeDtypeStruct((layers * bl...]
  transfers between devices with their start and end apart: 6 -> 6, of which waited for: 3 -> 3; matrix products, arithmetic and copies ran while one was open for 0% -> 0% of each run, Pallas kernels for 5% -> 1%
where the time goes in v4:
time: 97.7 us; the launch traced here: 97 us
  starting transfers between devices  36.5 us (37%)
  waiting for transfers between devices  29.2 us (30%)
  blocking collectives  22.1 us (23%)
  Pallas kernels  4.1 us (4%)
  other arithmetic  2.26 us (2%)
  local copies, waits for them, and re-layouts  2.17 us (2%)
    all_to_all x1, blocking collectives, local(): heated = lax.all_to_all(heated.reshape(layers, ROWS, spokes), 'slab', 0, 0)  22.1 us
    all_to_all x1, waiting for transfers between devices, local(): lax.all_to_all(packed.reshape(layers, block, 1, spokes), 'slab', 0, 0)  22 us
    all_to_all x1, starting transfers between devices, local(): lax.all_to_all(packed.reshape(layers, block, 1, spokes), 'slab', 0, 0)  13.4 us
    ppermute x2, starting transfers between devices, around(): lax.ppermute(block, BOTH, backward)  11.4 us
    all_to_all x1, starting transfers between devices, local(): lines = lax.all_to_all(lines, 'magnet', 0, 0).reshape(magnets, spokes)  6.77 us
    all_to_all x1, waiting for transfers between devices, local(): lines = lax.all_to_all(lines, 'magnet', 0, 0).reshape(magnets, spokes)  5.93 us
    ppermute x2, starting transfers between devices, around(): lax.ppermute(block, BOTH, onward)  4.86 us
  transfers between devices with their start and end apart: 6, of which 3 were waited for; matrix products, arithmetic and copies ran while one was open for 0% of the time, Pallas kernels for 1%

profile of v4, /device:TPU:1, one launch (start us, length us, event | category | flops | bytes accessed | tf_op | source)
XLA Modules:
  0.0 97.0 jit_solution(9645448481813951155)
XLA Ops:
  0.6 0.0 copy-start
  0.6 0.8 convert_element_type.6
  1.4 0.7 dynamic-slice_convert_fusion
  2.1 0.7 pad_maximum_fusion.own
  2.9 8.8 %collective-permute-start.1 = (f32[32,512]{1,0:T(8,128)S(1)}, f32[32,512]{1,0:T(8,128)S(1)}, u32[]{:S(2)}, u32[]{:S(2)}) collective-permute-start(f32[32,512]{1,0:T(8,128)S(1)} %pad_maximum_fusion.own), channel_id=1, source_target_pairs={{1,0},{2,1},{3,2},{4,3},{5,4},{6,5},{7,6},{8,7},{9,8},{10,9},{11,1... | collective-permute-start | bytes 196616 | tf_op jit(solution)/shard_map/ppermute | solution.py:294
  11.6 1.9 %collective-permute-start = (f32[32,512]{1,0:T(8,128)S(1)}, f32[32,512]{1,0:T(8,128)S(1)}, u32[]{:S(2)}, u32[]{:S(2)}) collective-permute-start(f32[32,512]{1,0:T(8,128)S(1)} %pad_maximum_fusion.own), channel_id=1, source_target_pairs={{0,1},{1,2},{2,3},{3,4},{4,5},{5,6},{6,7},{7,8},{8,9},{9,10},{10,1... | collective-permute-start | bytes 196616 | tf_op jit(solution)/shard_map/ppermute | solution.py:294
  13.6 0.0 collective-permute-done.1.after
  13.6 1.3 %collective-permute-done.before = f32[32,512]{1,0:T(8,128)S(1)} collective-permute-done((f32[32,512]{1,0:T(8,128)S(1)}, f32[32,512]{1,0:T(8,128)S(1)}, u32[]{:S(2)}, u32[]{:S(2)}) %collective-permute-start) | collective-permute-done | bytes 65568 | tf_op jit(solution)/shard_map/ppermute | solution.py:294
  14.9 0.0 copy-done
  14.9 0.0 copy-start.1
  14.9 0.9 copy-done.1
  15.8 1.2 %basis.1 = (f32[544,128]{1,0:T(8,128)}, f32[24,512]{1,0:T(8,128)S(1)}, f32[24,512]{1,0:T(8,128)S(1)}, f32[24,512]{1,0:T(8,128)S(1)}, f32[24,512]{1,0:T(8,128)S(1...) custom-call(f32[32,512]{1,0:T(8,128)S(1)} %pad_maximum_fusion.own, ...), custom_call_target="tpu_custom_call" | custom-call | tf_op jit(solution)/shard_map/basis/pallas_call | solution.py:302
  17.0 13.4 %all-to-all-start = ((f32[32,17,1,128]{3,2,1,0:T(1,128)}), f32[32,17,1,128]{3,2,1,0:T(1,128)S(1)}, u32[]{:S(2)}, u32[]{:S(2)}) async-start(f32[32,17,1,128]{3,2,1,0:T(1,128)} %bitcast.2), calls=%async_computation | async-start | bytes 557056 | tf_op jit(solution)/shard_map/all_to_all | solution.py:311
  30.4 1.0 %deposit.1.bins = f32[16,16,128]{2,1,0:T(8,128)S(1)} custom-call(f32[24,512]{1,0:T(8,128)S(1)} %get-tuple-element.19.w0, f32[24,512]{1,0:T(8,128)S(1)} %get-tuple-element.20.w1, f32[24,512]{1,0:T(8,128)S(1)} %get-tuple-element.21.w2, f32[24,512]{1,0:T(8,128)S(1)} %get-tuple-element.22.c_down, f32[24,512]{1,0:T(8,128)S(1)} %get-tuple-element.23.c_right, ...), custom_call_target="tpu_custom_call" | custom-call | flops 100000000 | bytes 2000000 | tf_op jit(solution)/shard_map/deposit/pallas_call | solution.py:312
  31.4 22.0 %all-to-all-done = f32[32,17,1,128]{3,2,1,0:T(1,128)S(1)} async-done(((f32[32,17,1,128]{3,2,1,0:T(1,128)}), f32[32,17,1,128]{3,2,1,0:T(1,128)S(1)}, u32[]{:S(2)}, u32[]{:S(2)}) %all-to-all-start) | async-done | bytes 278560 | tf_op jit(solution)/shard_map/all_to_all | solution.py:311
  53.4 0.6 broadcast_in_dim.2
  54.0 2.6 %collective-permute-start.3 = (f32[544,128]{1,0:T(8,128)S(1)}, f32[544,128]{1,0:T(8,128)S(1)}, u32[]{:S(2)}, u32[]{:S(2)}) collective-permute-start(f32[544,128]{1,0:T(8,128)S(1)} %bitcast.7), channel_id=1, source_target_pairs={{1,0},{2,1},{3,2},{4,3},{5,4},{6,5},{7,6},{8,7},{9,8},{10,9},{11,1... | collective-permute-start | bytes 835592 | tf_op jit(solution)/shard_map/ppermute | solution.py:294
  56.7 2.9 %collective-permute-start.2 = (f32[544,128]{1,0:T(8,128)S(1)}, f32[544,128]{1,0:T(8,128)S(1)}, u32[]{:S(2)}, u32[]{:S(2)}) collective-permute-start(f32[544,128]{1,0:T(8,128)S(1)} %bitcast.8), channel_id=1, source_target_pairs={{0,1},{1,2},{2,3},{3,4},{4,5},{5,6},{6,7},{7,8},{8,9},{9,10},{10,1... | collective-permute-start | bytes 835592 | tf_op jit(solution)/shard_map/ppermute | solution.py:294
  59.6 6.8 %all-to-all-start.1 = ((f32[16,1,128]{2,1,0:T(1,128)}), f32[16,1,128]{2,1,0:T(1,128)S(1)}, u32[]{:S(2)}, u32[]{:S(2)}) async-start(f32[16,1,128]{2,1,0:T(1,128)} %broadcast_in_dim.2), calls=%async_computation.1 | async-start | bytes 16384 | tf_op jit(solution)/shard_map/all_to_all | solution.py:325
  66.4 0.0 collective-permute-done.3.after
  66.4 0.0 collective-permute-done.2.before
  66.4 0.4 first.1
  66.8 5.9 %all-to-all-done.1 = f32[16,1,128]{2,1,0:T(1,128)S(1)} async-done(((f32[16,1,128]{2,1,0:T(1,128)}), f32[16,1,128]{2,1,0:T(1,128)S(1)}, u32[]{:S(2)}, u32[]{:S(2)}) %all-to-all-start.1) | async-done | bytes 8224 | tf_op jit(solution)/shard_map/all_to_all | solution.py:325
  72.8 1.5 %heat.1 = (f32[8,512]{1,0:T(8,128)}, f32[256,128]{1,0:T(8,128)S(1)}) custom-call(f32[16,128]{1,0:T(8,128)S(1)} %bitcast.13, f32[24,512]{1,0:T(8,128)S(1)} %get-tuple-element.19.w0, f32[24,512]{1,0:T(8,128)S(1)} %get-tuple-element.20.w1, f32[24,512]{1,0:T(8,128)S(1)} %get-tuple-element.21.w2, f32[16,16,128]{2,1,0:T(8,128)S(1)} %deposit.1.bins, ...), custom_call_target="tpu_custom_call" | custom-call | tf_op jit(solution)/shard_map/heat/pallas_call | solution.py:339
  74.3 22.1 %all_to_all.15 = f32[32,8,128]{2,1,0:T(8,128)S(1)} all-to-all(f32[32,8,128]{2,1,0:T(8,128)S(1)} %bitcast.12), channel_id=1, replica_groups=mesh['magnet'=16,'slab'=32] {'slab'}, dimensions={0} | all-to-all | bytes 262144 | tf_op jit(solution)/shard_map/all_to_all | solution.py:348
  96.3 0.7 copy.10
  (1 shorter events, 0.0 us)
Async XLA Ops:
  0.6 14.3 %copy-start = (f32[1,256,128]{2,1,0:T(8,128)S(1)}, f32[1,256,128]{2,1,0:T(8,128)}, u32[]{:S(2)}) copy-start(f32[1,256,128]{2,1,0:T(8,128)} %param.10) | copy-start | bytes 393220
  2.9 10.7 %collective-permute-start.1 = (f32[32,512]{1,0:T(8,128)S(1)}, f32[32,512]{1,0:T(8,128)S(1)}, u32[]{:S(2)}, u32[]{:S(2)}) collective-permute-start(f32[32,512]{1,0:T(8,128)S(1)} %pad_maximum_fusion.own), channel_id=1, source_target_pairs={{1,0},{2,1},{3,2},{4,3},{5,4},{6,5},{7,6},{8,7},{9,8},{10,9},{11,1... | collective-permute-start | bytes 196616 | tf_op jit(solution)/shard_map/ppermute | solution.py:294
  11.6 3.2 %collective-permute-start = (f32[32,512]{1,0:T(8,128)S(1)}, f32[32,512]{1,0:T(8,128)S(1)}, u32[]{:S(2)}, u32[]{:S(2)}) collective-permute-start(f32[32,512]{1,0:T(8,128)S(1)} %pad_maximum_fusion.own), channel_id=1, source_target_pairs={{0,1},{1,2},{2,3},{3,4},{4,5},{5,6},{6,7},{7,8},{8,9},{9,10},{10,1... | collective-permute-start | bytes 196616 | tf_op jit(solution)/shard_map/ppermute | solution.py:294
  14.9 0.9 copy-start.1
  17.0 36.4 %all-to-all-start = ((f32[32,17,1,128]{3,2,1,0:T(1,128)}), f32[32,17,1,128]{3,2,1,0:T(1,128)S(1)}, u32[]{:S(2)}, u32[]{:S(2)}) async-start(f32[32,17,1,128]{3,2,1,0:T(1,128)} %bitcast.2), calls=%async_computation | async-start | bytes 557056 | tf_op jit(solution)/shard_map/all_to_all | solution.py:311
  54.0 12.3 %collective-permute-start.3 = (f32[544,128]{1,0:T(8,128)S(1)}, f32[544,128]{1,0:T(8,128)S(1)}, u32[]{:S(2)}, u32[]{:S(2)}) collective-permute-start(f32[544,128]{1,0:T(8,128)S(1)} %bitcast.7), channel_id=1, source_target_pairs={{1,0},{2,1},{3,2},{4,3},{5,4},{6,5},{7,6},{8,7},{9,8},{10,9},{11,1... | collective-permute-start | bytes 835592 | tf_op jit(solution)/shard_map/ppermute | solution.py:294
  56.7 9.7 %collective-permute-start.2 = (f32[544,128]{1,0:T(8,128)S(1)}, f32[544,128]{1,0:T(8,128)S(1)}, u32[]{:S(2)}, u32[]{:S(2)}) collective-permute-start(f32[544,128]{1,0:T(8,128)S(1)} %bitcast.8), channel_id=1, source_target_pairs={{0,1},{1,2},{2,3},{3,4},{4,5},{5,6},{6,7},{7,8},{8,9},{9,10},{10,1... | collective-permute-start | bytes 835592 | tf_op jit(solution)/shard_map/ppermute | solution.py:294
  59.6 13.2 %all-to-all-start.1 = ((f32[16,1,128]{2,1,0:T(1,128)}), f32[16,1,128]{2,1,0:T(1,128)S(1)}, u32[]{:S(2)}, u32[]{:S(2)}) async-start(f32[16,1,128]{2,1,0:T(1,128)} %broadcast_in_dim.2), calls=%async_computation.1 | async-start | bytes 16384 | tf_op jit(solution)/shard_map/all_to_all | solution.py:325

commit v5 on v3

--- a/solution.py
+++ b/solution.py
@@ -24,6 +24,7 @@
 SHIFT = 9.85
 SCALE = 9.6
 BOTH = ("magnet", "slab")
+BLOCK = 2 * ROWS + 1
 
 
 def place():
@@ -47,23 +48,50 @@
     return pltpu.roll(v, v.shape[1] - 1, 1)
 
 
-def rows_inside(shape, margin):
+def rows_inside(shape, margin, ends_here=False):
     index, count = place()
     row = lax.broadcasted_iota(jnp.int32, shape, 0)
     low = jnp.where(index > 0, 0, margin)
-    high = jnp.where(index < count - 1, shape[0], shape[0] - margin)
+    high = shape[0] - margin if ends_here else jnp.where(index < count - 1, shape[0], shape[0] - margin)
     return jnp.where((row >= low) & (row < high), 1.0, 0.0).astype(jnp.float32)
 
 
-def basis_kernel(own, before, after, warmth_in, kind_in, packed, w0_out, w1_out, w2_out, down_out, right_out, left_out, cells_out):
+def sheet_kernel(warmth, voltage, pattern, cells, sheet, pattern_here, cells_here, sems):
+    at = pl.multiple_of(lax.axis_index("slab") * ROWS, ROWS)
+    copies = [
+        pltpu.make_async_copy(pattern, pattern_here, sems.at[0]),
+        pltpu.make_async_copy(cells.at[pl.ds(at, ROWS)], cells_here, sems.at[1]),
+        pltpu.make_async_copy(warmth, sheet.at[0:ROWS], sems.at[2]),
+        pltpu.make_async_copy(voltage, sheet.at[ROWS : 2 * ROWS], sems.at[3]),
+    ]
+    for copy in copies:
+        copy.start()
+    copies[0].wait()
+    sheet[2 * ROWS : 3 * ROWS] = pattern_here[...].astype(jnp.float32)
+    copies[1].wait()
+    sheet[3 * ROWS : 4 * ROWS] = cells_here[...].astype(jnp.float32)
+    copies[2].wait()
+    copies[3].wait()
+
+
+def pack_kernel(warmth, kind, packed):
+    for slab in range(packed.shape[0] // BLOCK):
+        part = slice(ROWS * slab, ROWS * (slab + 1))
+        at = BLOCK * slab
+        packed[at : at + ROWS] = warmth[part]
+        packed[at + ROWS : at + 2 * ROWS] = kind[part].astype(jnp.float32)
+        packed[at + 2 * ROWS : at + BLOCK] = jnp.zeros((1, packed.shape[1]), jnp.float32)
+
+
+def basis(before, own, after):
     def window(i):
         part = slice(ROWS * i, ROWS * (i + 1))
-        return jnp.concatenate([before[part, :], own[part, :], after[part, :]], axis=0)
+        mine = own[part]
+        return jnp.concatenate([before[part], mine, jnp.zeros_like(mine) if after is None else after[part]], axis=0)
 
     warmth, voltage, pattern = window(0), window(1), window(2)
-    cells_out[...] = window(3)
     shape = warmth.shape
-    inside = rows_inside(shape, ROWS)
+    inside = rows_inside(shape, ROWS, after is None)
     col = lax.broadcasted_iota(jnp.int32, shape, 1)
     last = col == shape[1] - 1
     sigma = inside * jnp.where(pattern == 1.0, copper_factor, 1.0) / (1.0 + sheet_slope * warmth)
@@ -84,25 +112,23 @@
     w0 = contact * voltage
     w1 = apply(w0)
     w2 = 2.0 * apply(w1) - w0
+    return (w0, w1, w2), apply, inside, (c_down, c_right, c_left)
+
+
+def gram_kernel(own, before, packed_in, packed):
+    (w0, w1, w2), apply, _, _ = basis(before, own, None)
     w3 = apply(w2)
-    w0_out[...] = w0
-    w1_out[...] = w1
-    w2_out[...] = w2
-    down_out[...] = c_down
-    right_out[...] = c_right
-    left_out[...] = c_left
-    a, b, c, d = (v[ROWS : 2 * ROWS] for v in (w0, w1, w2, w3))
+    index, count = place()
+    row = lax.broadcasted_iota(jnp.int32, w0.shape, 0)
+    taken = (row >= ROWS - HALO) & (row < jnp.where(index < count - 1, 2 * ROWS - HALO, 2 * ROWS))
     lane = lax.broadcasted_iota(jnp.int32, (1, 128), 1)
     line = jnp.zeros((1, 128), jnp.float32)
-    for i, (u, v) in enumerate(((a, a), (a, b), (a, c), (b, b), (b, c), (c, c), (c, d))):
-        line = jnp.where(lane == i, jnp.sum(u * v, keepdims=True), line)
-    block = 2 * ROWS + 1
-    for slab in range(packed.shape[0] // block):
-        part = slice(ROWS * slab, ROWS * (slab + 1))
-        at = block * slab
-        packed[at : at + ROWS] = warmth_in[part]
-        packed[at + ROWS : at + 2 * ROWS] = kind_in[part].astype(jnp.float32)
-        packed[at + 2 * ROWS : at + block] = line
+    for i, (u, v) in enumerate(((w0, w0), (w0, w1), (w0, w2), (w1, w1), (w1, w2), (w2, w2), (w2, w3))):
+        line = jnp.where(lane == i, jnp.sum(jnp.where(taken, u * v, 0.0), keepdims=True), line)
+    for slab in range(packed.shape[0] // BLOCK):
+        at = BLOCK * slab
+        packed[at : at + 2 * ROWS] = packed_in[at : at + 2 * ROWS]
+        packed[at + 2 * ROWS : at + BLOCK] = line
 
 
 def solve_small(lines):
@@ -141,20 +167,22 @@
 EDGE = 8
 
 
-def deposit_kernel(layers, w0, w1, w2, c_down, c_right, c_left, cells, bins, heats):
+def deposit_kernel(layers, own, before, after, bins, w0_out, w1_out, w2_out, heats):
     spokes = bins.shape[-1]
-    shape = w0.shape
-    inside = rows_inside(shape, ROWS)
+    fields, _, inside, (c_down, c_right, c_left) = basis(before, own, after)
+    for out, w in zip((w0_out, w1_out, w2_out), fields):
+        out[...] = w[ROWS : 2 * ROWS]
+    shape = inside.shape
     col = lax.broadcasted_iota(jnp.int32, shape, 1)
     last, first = col == shape[1] - 1, col == 0
-    fields = [w[...] * inside for w in (w0, w1, w2)]
+    fields = [w * inside for w in fields]
     falls = [w - below(w) for w in fields]
     steps = [w - jnp.where(last, 0.0, right(w)) for w in fields]
     wanted = slice(ROWS - HALO, ROWS - HALO + SPAN)
     for pair, (i, j) in enumerate(PAIRS):
-        q_down = c_down[...] * (falls[i] * falls[j])
-        q_right = c_right[...] * (steps[i] * steps[j])
-        q_left = jnp.where(first, c_left[...] * (fields[i] * fields[j]), left(q_right))
+        q_down = c_down * (falls[i] * falls[j])
+        q_right = c_right * (steps[i] * steps[j])
+        q_left = jnp.where(first, c_left * (fields[i] * fields[j]), left(q_right))
         joule = (q_down + above(q_down)) + (q_right + q_left)
         factor = heat_factor if i == j else 2.0 * heat_factor
         joule = factor * joule[wanted]
@@ -162,7 +190,8 @@
             heats[part, SPAN * pair : SPAN * (pair + 1)] = joule[:, 128 * part : 128 * (part + 1)]
     for part in range(heats.shape[0]):
         heats[part, SPAN * len(PAIRS) :] = jnp.zeros((SPAN * (8 - len(PAIRS)), 128), jnp.float32)
-    cell = cells[wanted].astype(jnp.int32)
+    part = slice(3 * ROWS, 4 * ROWS)
+    cell = jnp.concatenate([before[part], own[part], after[part]], axis=0)[wanted].astype(jnp.int32)
     azimuth = cell & (spokes - 1)
     outermost = jnp.where(cell >= (layers - 1) * spokes, 1.0, 0.0)
     spoke = lax.broadcasted_iota(jnp.int32, (spokes, shape[1]), 0)
@@ -248,8 +277,7 @@
     spokes = heated.shape[-1]
     body = slice(EDGE, EDGE + layers)
     f = solve_small(lines[...])
-    own = slice(ROWS, 2 * ROWS)
-    potential[...] = f[0] * w0[own] + f[1] * w1[own] + f[2] * w2[own]
+    potential[...] = f[0] * w0[...] + f[1] * w1[...] + f[2] * w2[...]
     sublane = lax.broadcasted_iota(jnp.int32, (8, spokes), 0)
     weight = jnp.zeros((8, spokes), jnp.float32)
     for pair, (i, j) in enumerate(PAIRS):
@@ -278,10 +306,6 @@
         substep_rows(range(substep + 1, SPAN - 1 - substep), layers, warm.at[substep % 2], cond, base, done)
 
 
-def vmem(count):
-    return [pl.BlockSpec(memory_space=pltpu.VMEM)] * count
-
-
 def local(foil_warmth, terminal_voltage_input, foil_segment_pattern, underlying_block_map, prior_block_warmth, substance_kind):
     f32 = jnp.float32
     magnets, layers = lax.axis_size("magnet"), lax.axis_size("slab")
@@ -290,57 +314,78 @@
     onward = [(i, i + 1) for i in range(count - 1)]
     backward = [(i + 1, i) for i in range(count - 1)]
 
-    def around(block):
-        return lax.ppermute(block, BOTH, onward), lax.ppermute(block, BOTH, backward)
-
-    cells = lax.dynamic_slice_in_dim(underlying_block_map, lax.axis_index("slab") * ROWS, ROWS, axis=0)
-    sheet = jnp.concatenate(
-        [foil_warmth, terminal_voltage_input, foil_segment_pattern.astype(f32), cells.astype(f32)], axis=0
-    )
-    field = jax.ShapeDtypeStruct((3 * ROWS, width), f32)
-    block = 2 * ROWS + 1
-    packed, *fields = pl.pallas_call(
-        basis_kernel,
-        out_shape=(jax.ShapeDtypeStruct((layers * block, spokes), f32),) + (field,) * 7,
-        in_specs=vmem(5),
-        out_specs=vmem(8),
-        name="basis",
-    )(sheet, *around(sheet), prior_block_warmth.reshape(layers * ROWS, spokes), substance_kind.reshape(layers * ROWS, spokes))
-
-    bricks = lax.all_to_all(packed.reshape(layers, block, 1, spokes), "slab", 0, 0)
-    bins = pl.pallas_call(
+    def call(kernel, name, shapes, *operands, scratch=(), spaces=None, cost=None, room=8 << 20):
+        return pl.pallas_call(
+            kernel,
+            out_shape=tuple(jax.ShapeDtypeStruct(dims, f32) for dims in shapes),
+            in_specs=[pl.BlockSpec(memory_space=spaces or pltpu.VMEM)] * len(operands),
+            out_specs=(pl.BlockSpec(memory_space=pltpu.VMEM),) * len(shapes),
+            scratch_shapes=scratch,
+            cost_estimate=cost,
+            compiler_params=pltpu.CompilerParams(vmem_limit_bytes=room),
+            name=name,
+        )(*operands)
+
+    rows = (ROWS, width)
+    (sheet,) = call(
+        sheet_kernel,
+        "sheet",
+        [(4 * ROWS, width)],
+        foil_warmth,
+        terminal_voltage_input,
+        foil_segment_pattern,
+        underlying_block_map,
+        scratch=[pltpu.VMEM(rows, jnp.int32), pltpu.VMEM(rows, jnp.int32), pltpu.SemaphoreType.DMA((4,))],
+        spaces=pltpu.HBM,
+        room=66846720,
+    )
+    before = lax.ppermute(sheet, BOTH, onward)
+    stack = (layers * BLOCK, spokes)
+    (packed,) = call(
+        pack_kernel, "pack", [stack], prior_block_warmth.reshape(-1, spokes), substance_kind.reshape(-1, spokes)
+    )
+    (packed,) = call(gram_kernel, "gram", [stack], sheet, before, packed)
+
+    packed, later = lax.optimization_barrier((packed, sheet))
+    bricks = lax.all_to_all(packed.reshape(layers, BLOCK, 1, spokes), "slab", 0, 0)
+    after = lax.ppermute(later, BOTH, backward)
+    bins, *fields = call(
         functools.partial(deposit_kernel, layers),
-        out_shape=jax.ShapeDtypeStruct((SPAN, 16, spokes), f32),
-        in_specs=vmem(7),
-        out_specs=vmem(1)[0],
-        scratch_shapes=[pltpu.VMEM((width // 128, 8 * SPAN, 128), f32)],
-        cost_estimate=pl.CostEstimate(flops=10**8, bytes_accessed=2 * 10**6, transcendentals=0),
-        name="deposit",
-    )(*fields)
+        "deposit",
+        [(SPAN, 16, spokes), rows, rows, rows],
+        sheet,
+        before,
+        after,
+        scratch=[pltpu.VMEM((width // 128, 8 * SPAN, 128), f32)],
+        cost=pl.CostEstimate(flops=10**8, bytes_accessed=2 * 10**6, transcendentals=0),
+    )
     lines = jnp.sum(bricks[:, 2 * ROWS], axis=0, keepdims=True)
     lines = jnp.broadcast_to(lines, (magnets, 1, spokes))
-    lines, bricks, bins = lax.optimization_barrier((lines, bricks.reshape(layers * block, spokes), bins))
+    lines, bricks, bins = lax.optimization_barrier((lines, bricks.reshape(stack), bins))
     lines = lax.all_to_all(lines, "magnet", 0, 0).reshape(magnets, spokes)
 
     padded = (SPAN, layers + 2 * EDGE, spokes)
     plain = (SPAN, layers, spokes)
-    stage = pl.pallas_call(
+    stage = call(
         functools.partial(first_kernel, layers),
-        out_shape=tuple(jax.ShapeDtypeStruct(dims, f32) for dims in (padded, plain, plain)),
-        in_specs=vmem(3),
-        out_specs=vmem(3),
-        scratch_shapes=[pltpu.VMEM(padded, f32), pltpu.VMEM(padded, f32)],
-        cost_estimate=pl.CostEstimate(flops=10**7, bytes_accessed=2 * 10**6, transcendentals=0),
-        name="first",
-    )(bricks, *around(bricks))
-    potential, heated = pl.pallas_call(
+        "first",
+        [padded, plain, plain],
+        bricks,
+        lax.ppermute(bricks, BOTH, onward),
+        lax.ppermute(bricks, BOTH, backward),
+        scratch=[pltpu.VMEM(padded, f32), pltpu.VMEM(padded, f32)],
+        cost=pl.CostEstimate(flops=10**7, bytes_accessed=2 * 10**6, transcendentals=0),
+    )
+    potential, heated = call(
         functools.partial(heat_kernel, layers),
-        out_shape=(jax.ShapeDtypeStruct((ROWS, width), f32), jax.ShapeDtypeStruct((layers * ROWS, spokes), f32)),
-        in_specs=vmem(8),
-        out_specs=vmem(2),
-        scratch_shapes=[pltpu.VMEM((2,) + padded, f32), pltpu.VMEM(padded, f32)],
-        name="heat",
-    )(lines, *fields[:3], bins, *stage)
+        "heat",
+        [rows, (layers * ROWS, spokes)],
+        lines,
+        *fields,
+        bins,
+        *stage,
+        scratch=[pltpu.VMEM((2,) + padded, f32), pltpu.VMEM(padded, f32)],
+    )
     heated = lax.all_to_all(heated.reshape(layers, ROWS, spokes), "slab", 0, 0)
     return potential, heated.reshape(prior_block_warmth.shape)
 

time: 100 us -> 94.2 us (0.942)
  Pallas kernels: 10.7 us -> 5.85 us
  waiting for transfers between devices: 24.2 us -> 28.7 us
  starting transfers between devices: 36.5 us -> 34 us
  local copies, waits for them, and re-layouts: 3.93 us -> 2.17 us
  other arithmetic: 1.51 us -> 0.05 us
    ppermute x4, waiting for transfers between devices: 1.3 us -> 15.4 us  [the longest x1 12.2 us: local(): after = lax.ppermute(later, BOTH, backward)]
    all_to_all x1, waiting for transfers between devices: 20.4 us -> 7.42 us  [local(): lax.all_to_all(packed.reshape(layers, BLOCK, 1, spokes), 'slab', 0, 0)]
    pallas_call x4 -> x6, Pallas kernels: 10.7 us -> 5.85 us  [call(): pl.pallas_call(kernel, out_shape=tuple((jax.ShapeDtypeStruct(dims, f32) f...]
    ppermute x4, starting transfers between devices: 16.3 us -> 12.6 us  [the longest x1 4.94 us: local(): before = lax.ppermute(sheet, BOTH, onward)]
    all_to_all x1, waiting for transfers between devices: 2.54 us -> 5.87 us  [local(): lines = lax.all_to_all(lines, 'magnet', 0, 0).reshape(magnets, spokes)]
    unnamed x19 -> x7, local copies, waits for them, and re-layouts: 3.29 us -> 1.56 us
    convert_element_type x2 -> x0, other arithmetic: 1.46 us -> none  [the longest x1 0.74 us: local(): cells.astype(f32)]
    all_to_all x1, starting transfers between devices: 13.4 us -> 14.6 us  [local(): lax.all_to_all(packed.reshape(layers, BLOCK, 1, spokes), 'slab', 0, 0)]
  transfers between devices with their start and end apart: 6 -> 6, of which waited for: 3 -> 4; matrix products, arithmetic and copies ran while one was open for 0% -> 0% of each run, Pallas kernels for 5% -> 2%
where the time goes in v5:
time: 94.2 us; the launch traced here: 93.7 us
  starting transfers between devices  34 us (36%)
  waiting for transfers between devices  28.7 us (30%)
  blocking collectives  22.2 us (24%)
  Pallas kernels  5.85 us (6%)
  local copies, waits for them, and re-layouts  2.17 us (2%)
    all_to_all x1, blocking collectives, local(): heated = lax.all_to_all(heated.reshape(layers, ROWS, spokes), 'slab', 0, 0)  22.2 us
    all_to_all x1, starting transfers between devices, local(): lax.all_to_all(packed.reshape(layers, BLOCK, 1, spokes), 'slab', 0, 0)  14.6 us
    ppermute x1, waiting for transfers between devices, local(): after = lax.ppermute(later, BOTH, backward)  12.2 us
    all_to_all x1, waiting for transfers between devices, local(): lax.all_to_all(packed.reshape(layers, BLOCK, 1, spokes), 'slab', 0, 0)  7.42 us
    all_to_all x1, starting transfers between devices, local(): lines = lax.all_to_all(lines, 'magnet', 0, 0).reshape(magnets, spokes)  6.77 us
    all_to_all x1, waiting for transfers between devices, local(): lines = lax.all_to_all(lines, 'magnet', 0, 0).reshape(magnets, spokes)  5.87 us
    pallas_call x6, Pallas kernels, call(): pl.pallas_call(kernel, out_shape=tuple((jax.ShapeDtypeStruct(dims, f32) f...  5.85 us
    ppermute x1, starting transfers between devices, local(): before = lax.ppermute(sheet, BOTH, onward)  4.94 us
  transfers between devices with their start and end apart: 6, of which 4 were waited for; matrix products, arithmetic and copies ran while one was open for 0% of the time, Pallas kernels for 2%

profile of v5, /device:TPU:1, one launch (start us, length us, event | category | flops | bytes accessed | tf_op | source)
XLA Modules:
  0.0 93.7 jit_solution(9656611542845223047)
XLA Ops:
  0.6 0.0 copy-start.1
  0.6 1.5 %sheet.1.own = f32[32,512]{1,0:T(8,128)} custom-call(f32[8,512]{1,0:T(8,128)} %warmth.1, f32[8,512]{1,0:T(8,128)} %voltage.1, s32[8,512]{1,0:T(8,128)} %pattern.1, s32[256,512]{1,0:T(8,128)} %cells.1), custom_call_target="tpu_custom_call" | custom-call | tf_op jit(solution)/shard_map/sheet/pallas_call | solution.py:318
  2.1 4.9 %collective-permute-start = (f32[32,512]{1,0:T(8,128)}, f32[32,512]{1,0:T(8,128)S(1)}, u32[]{:S(2)}, u32[]{:S(2)}) collective-permute-start(f32[32,512]{1,0:T(8,128)} %sheet.1.own), channel_id=1, source_target_pairs={{0,1},{1,2},{2,3},{3,4},{4,5},{5,6},{6,7},{7,8},{8,9},{9,10},{10,1... | collective-permute-start | bytes 196616 | tf_op jit(solution)/shard_map/ppermute | solution.py:342
  7.1 0.0 copy-done.1
  7.1 0.0 copy-start.2
  7.1 0.9 copy-done.2
  8.0 0.0 copy-start
  8.0 3.2 %collective-permute-done.before = f32[32,512]{1,0:T(8,128)S(1)} collective-permute-done((f32[32,512]{1,0:T(8,128)}, f32[32,512]{1,0:T(8,128)S(1)}, u32[]{:S(2)}, u32[]{:S(2)}) %collective-permute-start) | collective-permute-done | bytes 65568 | tf_op jit(solution)/shard_map/ppermute | solution.py:342
  11.2 0.0 copy-done
  11.2 1.2 %gram.1 = f32[544,128]{1,0:T(8,128)} custom-call(f32[32,512]{1,0:T(8,128)S(1)} %copy-done, f32[32,512]{1,0:T(8,128)S(1)} %collective-permute-done.before, f32[544,128]{1,0:T(8,128)S(1)} %pack.1.packed_in), custom_call_target="tpu_custom_call" | custom-call | tf_op jit(solution)/shard_map/gram/pallas_call | solution.py:318
  12.4 14.6 %all-to-all-start = ((f32[32,17,1,128]{3,2,1,0:T(1,128)}), f32[32,17,1,128]{3,2,1,0:T(1,128)S(1)}, u32[]{:S(2)}, u32[]{:S(2)}) async-start(f32[32,17,1,128]{3,2,1,0:T(1,128)} %bitcast.2), calls=%async_computation | async-start | bytes 557056 | tf_op jit(solution)/shard_map/all_to_all | solution.py:350
  27.1 2.1 %collective-permute-start.1 = (f32[32,512]{1,0:T(8,128)S(1)}, f32[32,512]{1,0:T(8,128)S(1)}, u32[]{:S(2)}, u32[]{:S(2)}) collective-permute-start(f32[32,512]{1,0:T(8,128)S(1)} %copy-done), channel_id=1, source_target_pairs={{1,0},{2,1},{3,2},{4,3},{5,4},{6,5},{7,6},{8,7},{9,8},{10,9},{11,1... | collective-permute-start | bytes 196616 | tf_op jit(solution)/shard_map/ppermute | solution.py:351
  29.2 12.2 %collective-permute-done.1.after = f32[32,512]{1,0:T(8,128)S(1)} collective-permute-done((f32[32,512]{1,0:T(8,128)S(1)}, f32[32,512]{1,0:T(8,128)S(1)}, u32[]{:S(2)}, u32[]{:S(2)}) %collective-permute-start.1) | collective-permute-done | bytes 65568 | tf_op jit(solution)/shard_map/ppermute | solution.py:351
  41.4 1.2 %deposit.1 = (f32[16,16,128]{2,1,0:T(8,128)S(1)}, f32[8,512]{1,0:T(8,128)S(1)}, f32[8,512]{1,0:T(8,128)S(1)}, f32[8,512]{1,0:T(8,128)S(1)}) custom-call(f32[32,512]{1,0:T(8,128)S(1)} %copy-done, f32[32,512]{1,0:T(8,128)S(1)} %collective-permute-done.before, f32[32,512]{1,0:T(8,128)S(1)} %collective-permute-done.1.after), custom_call_target="tpu_custom_call" | custom-call | flops 100000000 | bytes 2000000 | tf_op jit(solution)/shard_map/deposit/pallas_call | solution.py:318
  42.6 7.4 %all-to-all-done = f32[32,17,1,128]{3,2,1,0:T(1,128)S(1)} async-done(((f32[32,17,1,128]{3,2,1,0:T(1,128)}), f32[32,17,1,128]{3,2,1,0:T(1,128)S(1)}, u32[]{:S(2)}, u32[]{:S(2)}) %all-to-all-start) | async-done | bytes 278560 | tf_op jit(solution)/shard_map/all_to_all | solution.py:350
  50.1 0.6 broadcast_in_dim.2
  50.7 2.6 %collective-permute-start.3 = (f32[544,128]{1,0:T(8,128)S(1)}, f32[544,128]{1,0:T(8,128)S(1)}, u32[]{:S(2)}, u32[]{:S(2)}) collective-permute-start(f32[544,128]{1,0:T(8,128)S(1)} %bitcast.7), channel_id=1, source_target_pairs={{1,0},{2,1},{3,2},{4,3},{5,4},{6,5},{7,6},{8,7},{9,8},{10,9},{11,1... | collective-permute-start | bytes 835592 | tf_op jit(solution)/shard_map/ppermute | solution.py:375
  53.3 2.9 %collective-permute-start.2 = (f32[544,128]{1,0:T(8,128)S(1)}, f32[544,128]{1,0:T(8,128)S(1)}, u32[]{:S(2)}, u32[]{:S(2)}) collective-permute-start(f32[544,128]{1,0:T(8,128)S(1)} %bitcast.8), channel_id=1, source_target_pairs={{0,1},{1,2},{2,3},{3,4},{4,5},{5,6},{6,7},{7,8},{8,9},{9,10},{10,1... | collective-permute-start | bytes 835592 | tf_op jit(solution)/shard_map/ppermute | solution.py:374
  56.3 6.8 %all-to-all-start.1 = ((f32[16,1,128]{2,1,0:T(1,128)}), f32[16,1,128]{2,1,0:T(1,128)S(1)}, u32[]{:S(2)}, u32[]{:S(2)}) async-start(f32[16,1,128]{2,1,0:T(1,128)} %broadcast_in_dim.2), calls=%async_computation.1 | async-start | bytes 16384 | tf_op jit(solution)/shard_map/all_to_all | solution.py:365
  63.1 0.0 collective-permute-done.3.after
  63.1 0.0 collective-permute-done.2.before
  63.1 0.4 first.1
  63.5 5.9 %all-to-all-done.1 = f32[16,1,128]{2,1,0:T(1,128)S(1)} async-done(((f32[16,1,128]{2,1,0:T(1,128)}), f32[16,1,128]{2,1,0:T(1,128)S(1)}, u32[]{:S(2)}, u32[]{:S(2)}) %all-to-all-start.1) | async-done | bytes 8224 | tf_op jit(solution)/shard_map/all_to_all | solution.py:365
  69.4 1.5 %heat.1 = (f32[8,512]{1,0:T(8,128)}, f32[256,128]{1,0:T(8,128)S(1)}) custom-call(f32[16,128]{1,0:T(8,128)S(1)} %bitcast.13, f32[8,512]{1,0:T(8,128)S(1)} %get-tuple-element.20.w0, f32[8,512]{1,0:T(8,128)S(1)} %get-tuple-element.21.w1, f32[8,512]{1,0:T(8,128)S(1)} %get-tuple-element.22.w2, f32[16,16,128]{2,1,0:T(8,128)S(1)} %get-tuple-element.23.bins, ...), custom_call_target="tpu_custom_call" | custom-call | tf_op jit(solution)/shard_map/heat/pallas_call | solution.py:318
  70.9 22.2 %all_to_all.15 = f32[32,8,128]{2,1,0:T(8,128)S(1)} all-to-all(f32[32,8,128]{2,1,0:T(8,128)S(1)} %bitcast.10), channel_id=1, replica_groups=mesh['magnet'=16,'slab'=32] {'slab'}, dimensions={0} | all-to-all | bytes 262144 | tf_op jit(solution)/shard_map/all_to_all | solution.py:389
  93.1 0.7 copy.10
  (2 shorter events, 0.1 us)
Async XLA Ops:
  0.6 6.4 %copy-start.1 = (f32[1,256,128]{2,1,0:T(8,128)S(1)}, f32[1,256,128]{2,1,0:T(8,128)}, u32[]{:S(2)}) copy-start(f32[1,256,128]{2,1,0:T(8,128)} %param.10) | copy-start | bytes 393220
  2.1 9.1 %collective-permute-start = (f32[32,512]{1,0:T(8,128)}, f32[32,512]{1,0:T(8,128)S(1)}, u32[]{:S(2)}, u32[]{:S(2)}) collective-permute-start(f32[32,512]{1,0:T(8,128)} %sheet.1.own), channel_id=1, source_target_pairs={{0,1},{1,2},{2,3},{3,4},{4,5},{5,6},{6,7},{7,8},{8,9},{9,10},{10,1... | collective-permute-start | bytes 196616 | tf_op jit(solution)/shard_map/ppermute | solution.py:342
  7.1 0.9 copy-start.2
  8.0 3.3 %copy-start = (f32[32,512]{1,0:T(8,128)S(1)}, f32[32,512]{1,0:T(8,128)}, u32[]{:S(2)}) copy-start(f32[32,512]{1,0:T(8,128)} %sheet.1.own) | copy-start | bytes 196612
  12.4 37.6 %all-to-all-start = ((f32[32,17,1,128]{3,2,1,0:T(1,128)}), f32[32,17,1,128]{3,2,1,0:T(1,128)S(1)}, u32[]{:S(2)}, u32[]{:S(2)}) async-start(f32[32,17,1,128]{3,2,1,0:T(1,128)} %bitcast.2), calls=%async_computation | async-start | bytes 557056 | tf_op jit(solution)/shard_map/all_to_all | solution.py:350
  27.1 14.3 %collective-permute-start.1 = (f32[32,512]{1,0:T(8,128)S(1)}, f32[32,512]{1,0:T(8,128)S(1)}, u32[]{:S(2)}, u32[]{:S(2)}) collective-permute-start(f32[32,512]{1,0:T(8,128)S(1)} %copy-done), channel_id=1, source_target_pairs={{1,0},{2,1},{3,2},{4,3},{5,4},{6,5},{7,6},{8,7},{9,8},{10,9},{11,1... | collective-permute-start | bytes 196616 | tf_op jit(solution)/shard_map/ppermute | solution.py:351
  50.7 12.3 %collective-permute-start.3 = (f32[544,128]{1,0:T(8,128)S(1)}, f32[544,128]{1,0:T(8,128)S(1)}, u32[]{:S(2)}, u32[]{:S(2)}) collective-permute-start(f32[544,128]{1,0:T(8,128)S(1)} %bitcast.7), channel_id=1, source_target_pairs={{1,0},{2,1},{3,2},{4,3},{5,4},{6,5},{7,6},{8,7},{9,8},{10,9},{11,1... | collective-permute-start | bytes 835592 | tf_op jit(solution)/shard_map/ppermute | solution.py:375
  53.3 9.7 %collective-permute-start.2 = (f32[544,128]{1,0:T(8,128)S(1)}, f32[544,128]{1,0:T(8,128)S(1)}, u32[]{:S(2)}, u32[]{:S(2)}) collective-permute-start(f32[544,128]{1,0:T(8,128)S(1)} %bitcast.8), channel_id=1, source_target_pairs={{0,1},{1,2},{2,3},{3,4},{4,5},{5,6},{6,7},{7,8},{8,9},{9,10},{10,1... | collective-permute-start | bytes 835592 | tf_op jit(solution)/shard_map/ppermute | solution.py:374
  56.3 13.1 %all-to-all-start.1 = ((f32[16,1,128]{2,1,0:T(1,128)}), f32[16,1,128]{2,1,0:T(1,128)S(1)}, u32[]{:S(2)}, u32[]{:S(2)}) async-start(f32[16,1,128]{2,1,0:T(1,128)} %broadcast_in_dim.2), calls=%async_computation.1 | async-start | bytes 16384 | tf_op jit(solution)/shard_map/all_to_all | solution.py:365

commit v6 on v5

--- a/solution.py
+++ b/solution.py
@@ -48,11 +48,11 @@
     return pltpu.roll(v, v.shape[1] - 1, 1)
 
 
-def rows_inside(shape, margin, ends_here=False):
+def rows_inside(shape, margin):
     index, count = place()
     row = lax.broadcasted_iota(jnp.int32, shape, 0)
     low = jnp.where(index > 0, 0, margin)
-    high = shape[0] - margin if ends_here else jnp.where(index < count - 1, shape[0], shape[0] - margin)
+    high = jnp.where(index < count - 1, shape[0], shape[0] - margin)
     return jnp.where((row >= low) & (row < high), 1.0, 0.0).astype(jnp.float32)
 
 
@@ -83,15 +83,24 @@
         packed[at + 2 * ROWS : at + BLOCK] = jnp.zeros((1, packed.shape[1]), jnp.float32)
 
 
-def basis(before, own, after):
+def sides(index, mate, cross):
+    even = index % 2 == 0
+    return jnp.where(even, cross, mate), jnp.where(even, mate, cross)
+
+
+def window_of(own, mate, cross, i):
+    part = slice(ROWS * i, ROWS * (i + 1))
+    before, after = sides(place()[0], mate[part], cross[part])
+    return jnp.concatenate([before, own[part], after], axis=0)
+
+
+def basis(own, mate, cross):
     def window(i):
-        part = slice(ROWS * i, ROWS * (i + 1))
-        mine = own[part]
-        return jnp.concatenate([before[part], mine, jnp.zeros_like(mine) if after is None else after[part]], axis=0)
+        return window_of(own, mate, cross, i)
 
     warmth, voltage, pattern = window(0), window(1), window(2)
     shape = warmth.shape
-    inside = rows_inside(shape, ROWS, after is None)
+    inside = rows_inside(shape, ROWS)
     col = lax.broadcasted_iota(jnp.int32, shape, 1)
     last = col == shape[1] - 1
     sigma = inside * jnp.where(pattern == 1.0, copper_factor, 1.0) / (1.0 + sheet_slope * warmth)
@@ -115,16 +124,13 @@
     return (w0, w1, w2), apply, inside, (c_down, c_right, c_left)
 
 
-def gram_kernel(own, before, packed_in, packed):
-    (w0, w1, w2), apply, _, _ = basis(before, own, None)
-    w3 = apply(w2)
-    index, count = place()
-    row = lax.broadcasted_iota(jnp.int32, w0.shape, 0)
-    taken = (row >= ROWS - HALO) & (row < jnp.where(index < count - 1, 2 * ROWS - HALO, 2 * ROWS))
+def gram_kernel(own, mate, cross, packed_in, packed):
+    (w0, w1, w2), apply, _, _ = basis(own, mate, cross)
+    w0, w1, w2, w3 = (w[ROWS : 2 * ROWS] for w in (w0, w1, w2, apply(w2)))
     lane = lax.broadcasted_iota(jnp.int32, (1, 128), 1)
     line = jnp.zeros((1, 128), jnp.float32)
     for i, (u, v) in enumerate(((w0, w0), (w0, w1), (w0, w2), (w1, w1), (w1, w2), (w2, w2), (w2, w3))):
-        line = jnp.where(lane == i, jnp.sum(jnp.where(taken, u * v, 0.0), keepdims=True), line)
+        line = jnp.where(lane == i, jnp.sum(u * v, keepdims=True), line)
     for slab in range(packed.shape[0] // BLOCK):
         at = BLOCK * slab
         packed[at : at + 2 * ROWS] = packed_in[at : at + 2 * ROWS]
@@ -167,9 +173,9 @@
 EDGE = 8
 
 
-def deposit_kernel(layers, own, before, after, bins, w0_out, w1_out, w2_out, heats):
+def deposit_kernel(layers, own, mate, cross, bins, w0_out, w1_out, w2_out, heats):
     spokes = bins.shape[-1]
-    fields, _, inside, (c_down, c_right, c_left) = basis(before, own, after)
+    fields, _, inside, (c_down, c_right, c_left) = basis(own, mate, cross)
     for out, w in zip((w0_out, w1_out, w2_out), fields):
         out[...] = w[ROWS : 2 * ROWS]
     shape = inside.shape
@@ -190,8 +196,7 @@
             heats[part, SPAN * pair : SPAN * (pair + 1)] = joule[:, 128 * part : 128 * (part + 1)]
     for part in range(heats.shape[0]):
         heats[part, SPAN * len(PAIRS) :] = jnp.zeros((SPAN * (8 - len(PAIRS)), 128), jnp.float32)
-    part = slice(3 * ROWS, 4 * ROWS)
-    cell = jnp.concatenate([before[part], own[part], after[part]], axis=0)[wanted].astype(jnp.int32)
+    cell = window_of(own, mate, cross, 3)[wanted].astype(jnp.int32)
     azimuth = cell & (spokes - 1)
     outermost = jnp.where(cell >= (layers - 1) * spokes, 1.0, 0.0)
     spoke = lax.broadcasted_iota(jnp.int32, (spokes, shape[1]), 0)
@@ -247,24 +252,31 @@
         field[EDGE + layers : 2 * EDGE + layers] = blank
 
 
-def first_kernel(layers, own, before, after, fresh, base, store, warm, cond):
+def first_kernel(layers, own, mate, cross, fresh, base, store, warm, cond):
     block = own.shape[0] // layers
     index, count = place()
     body = slice(EDGE, EDGE + layers)
     for row in range(SPAN):
-        source, at, there = own, row - HALO, 1.0
+
+        def rows_of(first):
+            if HALO <= row < HALO + ROWS:
+                return own[pl.ds(first + row - HALO, layers, stride=block), :]
+            at = first + (row + ROWS - HALO) % ROWS
+            return sides(index, *(ref[pl.ds(at, layers, stride=block), :] for ref in (mate, cross)))[int(row >= HALO)]
+
+        there = 1.0
         if row < HALO:
-            source, at, there = before, row + ROWS - HALO, jnp.where(index > 0, 1.0, 0.0)
+            there = jnp.where(index > 0, 1.0, 0.0)
         elif row >= HALO + ROWS:
-            source, at, there = after, row - HALO - ROWS, jnp.where(index < count - 1, 1.0, 0.0)
-        kind = source[pl.ds(ROWS + at, layers, stride=block), :]
+            there = jnp.where(index < count - 1, 1.0, 0.0)
+        kind = rows_of(ROWS)
 
         def table(values):
             return jnp.where(kind == 0.0, values[0], jnp.where(kind == 1.0, values[1], jnp.where(kind == 2.0, values[2], values[3])))
 
         base[row] = table(conduct_table) * there
         store[row] = table([0.5 * time_step / c for c in capacity_table]) * there
-        warm[row, body] = source[pl.ds(at, layers, stride=block), :]
+        warm[row, body] = rows_of(0)
         clear_edges(layers, warm.at[row], cond.at[row], fresh.at[row])
 
     def done(row, t, flux):
@@ -311,8 +323,11 @@
     magnets, layers = lax.axis_size("magnet"), lax.axis_size("slab")
     count = magnets * layers
     width, spokes = foil_warmth.shape[1], prior_block_warmth.shape[2]
-    onward = [(i, i + 1) for i in range(count - 1)]
-    backward = [(i + 1, i) for i in range(count - 1)]
+    mates = [(i, i ^ 1) for i in range(count)]
+    crossing = [(i, i + 1) for i in range(1, count - 1, 2)] + [(i + 1, i) for i in range(1, count - 1, 2)]
+
+    def exchange(array):
+        return lax.ppermute(array, BOTH, mates), lax.ppermute(array, BOTH, crossing)
 
     def call(kernel, name, shapes, *operands, scratch=(), spaces=None, cost=None, room=8 << 20):
         return pl.pallas_call(
@@ -339,23 +354,20 @@
         spaces=pltpu.HBM,
         room=66846720,
     )
-    before = lax.ppermute(sheet, BOTH, onward)
+    around = exchange(sheet)
     stack = (layers * BLOCK, spokes)
     (packed,) = call(
         pack_kernel, "pack", [stack], prior_block_warmth.reshape(-1, spokes), substance_kind.reshape(-1, spokes)
     )
-    (packed,) = call(gram_kernel, "gram", [stack], sheet, before, packed)
-
-    packed, later = lax.optimization_barrier((packed, sheet))
+    (packed,) = call(gram_kernel, "gram", [stack], sheet, *around, packed)
+
     bricks = lax.all_to_all(packed.reshape(layers, BLOCK, 1, spokes), "slab", 0, 0)
-    after = lax.ppermute(later, BOTH, backward)
     bins, *fields = call(
         functools.partial(deposit_kernel, layers),
         "deposit",
         [(SPAN, 16, spokes), rows, rows, rows],
         sheet,
-        before,
-        after,
+        *around,
         scratch=[pltpu.VMEM((width // 128, 8 * SPAN, 128), f32)],
         cost=pl.CostEstimate(flops=10**8, bytes_accessed=2 * 10**6, transcendentals=0),
     )
@@ -371,8 +383,7 @@
         "first",
         [padded, plain, plain],
         bricks,
-        lax.ppermute(bricks, BOTH, onward),
-        lax.ppermute(bricks, BOTH, backward),
+        *exchange(bricks),
         scratch=[pltpu.VMEM(padded, f32), pltpu.VMEM(padded, f32)],
         cost=pl.CostEstimate(flops=10**7, bytes_accessed=2 * 10**6, transcendentals=0),
     )

time: 94.2 us -> 93.4 us (level)
  waiting for transfers between devices: 28.7 us -> 27.7 us
    ppermute x4, waiting for transfers between devices: 15.4 us -> 0.14 us  [the longest x2 0.13 us: exchange(): lax.ppermute(array, BOTH, mates)]
    all_to_all x1, waiting for transfers between devices: 7.42 us -> 21.7 us  [local(): lax.all_to_all(packed.reshape(layers, BLOCK, 1, spokes), 'slab', 0, 0)]
    all_to_all x1, starting transfers between devices: 14.6 us -> 12.5 us  [local(): lax.all_to_all(packed.reshape(layers, BLOCK, 1, spokes), 'slab', 0, 0)]
    ppermute x4, starting transfers between devices: 12.6 us -> 13.6 us  [the longest x2 7.17 us: exchange(): lax.ppermute(array, BOTH, crossing)]
  transfers between devices with their start and end apart: 6 -> 6, of which waited for: 4 -> 3; matrix products, arithmetic and copies ran while one was open for 0% -> 0% of each run, Pallas kernels for 2% -> 2%
where the time goes in v6:
time: 93.4 us; the launch traced here: 92.9 us
  starting transfers between devices  33.3 us (36%)
  waiting for transfers between devices  27.7 us (30%)
  blocking collectives  22.5 us (24%)
  Pallas kernels  5.8 us (6%)
  local copies, waits for them, and re-layouts  2.83 us (3%)
    all_to_all x1, blocking collectives, local(): heated = lax.all_to_all(heated.reshape(layers, ROWS, spokes), 'slab', 0, 0)  22.5 us
    all_to_all x1, waiting for transfers between devices, local(): lax.all_to_all(packed.reshape(layers, BLOCK, 1, spokes), 'slab', 0, 0)  21.7 us
    all_to_all x1, starting transfers between devices, local(): lax.all_to_all(packed.reshape(layers, BLOCK, 1, spokes), 'slab', 0, 0)  12.5 us
    ppermute x2, starting transfers between devices, exchange(): lax.ppermute(array, BOTH, crossing)  7.17 us
    all_to_all x1, starting transfers between devices, local(): lines = lax.all_to_all(lines, 'magnet', 0, 0).reshape(magnets, spokes)  7.14 us
    ppermute x2, starting transfers between devices, exchange(): lax.ppermute(array, BOTH, mates)  6.44 us
    all_to_all x1, waiting for transfers between devices, local(): lines = lax.all_to_all(lines, 'magnet', 0, 0).reshape(magnets, spokes)  5.88 us
    pallas_call x6, Pallas kernels, call(): pl.pallas_call(kernel, out_shape=tuple((jax.ShapeDtypeStruct(dims, f32) f...  5.8 us
  transfers between devices with their start and end apart: 6, of which 3 were waited for; matrix products, arithmetic and copies ran while one was open for 0% of the time, Pallas kernels for 2%

profile of v6, /device:TPU:1, one launch (start us, length us, event | category | flops | bytes accessed | tf_op | source)
XLA Modules:
  0.0 92.9 jit_solution(8628724769287575345)
XLA Ops:
  0.6 0.0 copy-start.1
  0.6 1.5 %sheet.1.own = f32[32,512]{1,0:T(8,128)} custom-call(f32[8,512]{1,0:T(8,128)} %warmth.1, f32[8,512]{1,0:T(8,128)} %voltage.1, s32[8,512]{1,0:T(8,128)} %pattern.1, s32[256,512]{1,0:T(8,128)} %cells.1), custom_call_target="tpu_custom_call" | custom-call | tf_op jit(solution)/shard_map/sheet/pallas_call | solution.py:333
  2.1 4.9 %collective-permute-start.1 = (f32[32,512]{1,0:T(8,128)}, f32[32,512]{1,0:T(8,128)S(1)}, u32[]{:S(2)}, u32[]{:S(2)}) collective-permute-start(f32[32,512]{1,0:T(8,128)} %sheet.1.own), channel_id=1, source_target_pairs={{1,2},{3,4},{5,6},{7,8},{9,10},{11,12},{13,14},{15,16},{17,18},{19... | collective-permute-start | bytes 196616 | tf_op jit(solution)/shard_map/ppermute | solution.py:330
  7.1 4.5 %collective-permute-start = (f32[32,512]{1,0:T(8,128)}, f32[32,512]{1,0:T(8,128)S(1)}, u32[]{:S(2)}, u32[]{:S(2)}) collective-permute-start(f32[32,512]{1,0:T(8,128)} %sheet.1.own), channel_id=1, source_target_pairs={{0,1},{1,0},{2,3},{3,2},{4,5},{5,4},{6,7},{7,6},{8,9},{9,8},{10,11... | collective-permute-start | bytes 196616 | tf_op jit(solution)/shard_map/ppermute | solution.py:330
  11.6 0.0 copy-done.1
  11.6 0.0 copy-start.2
  11.6 0.9 copy-done.2
  12.5 0.0 copy-start
  12.5 0.0 collective-permute-done.1.cross
  12.5 0.1 collective-permute-done.mate
  12.7 0.7 copy-done
  13.3 1.2 %gram.1 = f32[544,128]{1,0:T(8,128)} custom-call(f32[32,512]{1,0:T(8,128)S(1)} %copy-done, f32[32,512]{1,0:T(8,128)S(1)} %collective-permute-done.mate, f32[32,512]{1,0:T(8,128)S(1)} %collective-permute-done.1.cross, f32[544,128]{1,0:T(8,128)S(1)} %pack.1.packed_in), custom_call_target="tpu_custom_call" | custom-call | tf_op jit(solution)/shard_map/gram/pallas_call | solution.py:333
  14.5 12.5 %all-to-all-start = ((f32[32,17,1,128]{3,2,1,0:T(1,128)}), f32[32,17,1,128]{3,2,1,0:T(1,128)S(1)}, u32[]{:S(2)}, u32[]{:S(2)}) async-start(f32[32,17,1,128]{3,2,1,0:T(1,128)} %bitcast.2), calls=%async_computation | async-start | bytes 557056 | tf_op jit(solution)/shard_map/all_to_all | solution.py:364
  27.0 1.2 %deposit.1 = (f32[16,16,128]{2,1,0:T(8,128)S(1)}, f32[8,512]{1,0:T(8,128)S(1)}, f32[8,512]{1,0:T(8,128)S(1)}, f32[8,512]{1,0:T(8,128)S(1)}) custom-call(f32[32,512]{1,0:T(8,128)S(1)} %copy-done, f32[32,512]{1,0:T(8,128)S(1)} %collective-permute-done.mate, f32[32,512]{1,0:T(8,128)S(1)} %collective-permute-done.1.cross), custom_call_target="tpu_custom_call" | custom-call | flops 100000000 | bytes 2000000 | tf_op jit(solution)/shard_map/deposit/pallas_call | solution.py:333
  28.3 21.7 %all-to-all-done = f32[32,17,1,128]{3,2,1,0:T(1,128)S(1)} async-done(((f32[32,17,1,128]{3,2,1,0:T(1,128)}), f32[32,17,1,128]{3,2,1,0:T(1,128)S(1)}, u32[]{:S(2)}, u32[]{:S(2)}) %all-to-all-start) | async-done | bytes 278560 | tf_op jit(solution)/shard_map/all_to_all | solution.py:364
  50.1 0.6 broadcast_in_dim.2
  50.7 2.2 %collective-permute-start.3 = (f32[544,128]{1,0:T(8,128)S(1)}, f32[544,128]{1,0:T(8,128)S(1)}, u32[]{:S(2)}, u32[]{:S(2)}) collective-permute-start(f32[544,128]{1,0:T(8,128)S(1)} %bitcast.7), channel_id=1, source_target_pairs={{1,2},{3,4},{5,6},{7,8},{9,10},{11,12},{13,14},{15,16},{17,18},{19... | collective-permute-start | bytes 835592 | tf_op jit(solution)/shard_map/ppermute | solution.py:330
  52.9 1.9 %collective-permute-start.2 = (f32[544,128]{1,0:T(8,128)S(1)}, f32[544,128]{1,0:T(8,128)S(1)}, u32[]{:S(2)}, u32[]{:S(2)}) collective-permute-start(f32[544,128]{1,0:T(8,128)S(1)} %bitcast.8), channel_id=1, source_target_pairs={{0,1},{1,0},{2,3},{3,2},{4,5},{5,4},{6,7},{7,6},{8,9},{9,8},{10,11... | collective-permute-start | bytes 835592 | tf_op jit(solution)/shard_map/ppermute | solution.py:330
  54.8 7.1 %all-to-all-start.1 = ((f32[16,1,128]{2,1,0:T(1,128)}), f32[16,1,128]{2,1,0:T(1,128)S(1)}, u32[]{:S(2)}, u32[]{:S(2)}) async-start(f32[16,1,128]{2,1,0:T(1,128)} %broadcast_in_dim.2), calls=%async_computation.1 | async-start | bytes 16384 | tf_op jit(solution)/shard_map/all_to_all | solution.py:377
  62.0 0.0 collective-permute-done.3.cross
  62.0 0.0 collective-permute-done.2.mate
  62.0 0.4 first.1
  62.4 5.9 %all-to-all-done.1 = f32[16,1,128]{2,1,0:T(1,128)S(1)} async-done(((f32[16,1,128]{2,1,0:T(1,128)}), f32[16,1,128]{2,1,0:T(1,128)S(1)}, u32[]{:S(2)}, u32[]{:S(2)}) %all-to-all-start.1) | async-done | bytes 8224 | tf_op jit(solution)/shard_map/all_to_all | solution.py:377
  68.3 1.5 %heat.1 = (f32[8,512]{1,0:T(8,128)}, f32[256,128]{1,0:T(8,128)S(1)}) custom-call(f32[16,128]{1,0:T(8,128)S(1)} %bitcast.13, f32[8,512]{1,0:T(8,128)S(1)} %get-tuple-element.16.w0, f32[8,512]{1,0:T(8,128)S(1)} %get-tuple-element.17.w1, f32[8,512]{1,0:T(8,128)S(1)} %get-tuple-element.18.w2, f32[16,16,128]{2,1,0:T(8,128)S(1)} %get-tuple-element.19.bins, ...), custom_call_target="tpu_custom_call" | custom-call | tf_op jit(solution)/shard_map/heat/pallas_call | solution.py:333
  69.8 22.5 %all_to_all.15 = f32[32,8,128]{2,1,0:T(8,128)S(1)} all-to-all(f32[32,8,128]{2,1,0:T(8,128)S(1)} %bitcast.10), channel_id=1, replica_groups=mesh['magnet'=16,'slab'=32] {'slab'}, dimensions={0} | all-to-all | bytes 262144 | tf_op jit(solution)/shard_map/all_to_all | solution.py:400
  92.3 0.7 copy.10
  (2 shorter events, 0.1 us)
Async XLA Ops:
  0.6 11.0 %copy-start.1 = (f32[1,256,128]{2,1,0:T(8,128)S(1)}, f32[1,256,128]{2,1,0:T(8,128)}, u32[]{:S(2)}) copy-start(f32[1,256,128]{2,1,0:T(8,128)} %param.10) | copy-start | bytes 393220
  2.1 10.4 %collective-permute-start.1 = (f32[32,512]{1,0:T(8,128)}, f32[32,512]{1,0:T(8,128)S(1)}, u32[]{:S(2)}, u32[]{:S(2)}) collective-permute-start(f32[32,512]{1,0:T(8,128)} %sheet.1.own), channel_id=1, source_target_pairs={{1,2},{3,4},{5,6},{7,8},{9,10},{11,12},{13,14},{15,16},{17,18},{19... | collective-permute-start | bytes 196616 | tf_op jit(solution)/shard_map/ppermute | solution.py:330
  7.1 5.6 %collective-permute-start = (f32[32,512]{1,0:T(8,128)}, f32[32,512]{1,0:T(8,128)S(1)}, u32[]{:S(2)}, u32[]{:S(2)}) collective-permute-start(f32[32,512]{1,0:T(8,128)} %sheet.1.own), channel_id=1, source_target_pairs={{0,1},{1,0},{2,3},{3,2},{4,5},{5,4},{6,7},{7,6},{8,9},{9,8},{10,11... | collective-permute-start | bytes 196616 | tf_op jit(solution)/shard_map/ppermute | solution.py:330
  11.6 0.9 copy-start.2
  12.5 0.8 copy-start
  14.5 35.5 %all-to-all-start = ((f32[32,17,1,128]{3,2,1,0:T(1,128)}), f32[32,17,1,128]{3,2,1,0:T(1,128)S(1)}, u32[]{:S(2)}, u32[]{:S(2)}) async-start(f32[32,17,1,128]{3,2,1,0:T(1,128)} %bitcast.2), calls=%async_computation | async-start | bytes 557056 | tf_op jit(solution)/shard_map/all_to_all | solution.py:364
  50.7 11.3 %collective-permute-start.3 = (f32[544,128]{1,0:T(8,128)S(1)}, f32[544,128]{1,0:T(8,128)S(1)}, u32[]{:S(2)}, u32[]{:S(2)}) collective-permute-start(f32[544,128]{1,0:T(8,128)S(1)} %bitcast.7), channel_id=1, source_target_pairs={{1,2},{3,4},{5,6},{7,8},{9,10},{11,12},{13,14},{15,16},{17,18},{19... | collective-permute-start | bytes 835592 | tf_op jit(solution)/shard_map/ppermute | solution.py:330
  52.9 9.1 %collective-permute-start.2 = (f32[544,128]{1,0:T(8,128)S(1)}, f32[544,128]{1,0:T(8,128)S(1)}, u32[]{:S(2)}, u32[]{:S(2)}) collective-permute-start(f32[544,128]{1,0:T(8,128)S(1)} %bitcast.8), channel_id=1, source_target_pairs={{0,1},{1,0},{2,3},{3,2},{4,5},{5,4},{6,7},{7,6},{8,9},{9,8},{10,11... | collective-permute-start | bytes 835592 | tf_op jit(solution)/shard_map/ppermute | solution.py:330
  54.8 13.5 %all-to-all-start.1 = ((f32[16,1,128]{2,1,0:T(1,128)}), f32[16,1,128]{2,1,0:T(1,128)S(1)}, u32[]{:S(2)}, u32[]{:S(2)}) async-start(f32[16,1,128]{2,1,0:T(1,128)} %broadcast_in_dim.2), calls=%async_computation.1 | async-start | bytes 16384 | tf_op jit(solution)/shard_map/all_to_all | solution.py:377

commit v7 on v6

--- a/solution.py
+++ b/solution.py
@@ -252,24 +252,41 @@
         field[EDGE + layers : 2 * EDGE + layers] = blank
 
 
+def share_kernel(layers, own, lines, for_mate, for_cross):
+    mine = own[pl.ds(2 * ROWS, layers, stride=BLOCK), :]
+    for magnet in range(lines.shape[0] // layers):
+        lines[layers * magnet : layers * (magnet + 1)] = mine
+    even = place()[0] % 2 == 0
+    for layer in range(layers):
+        at = BLOCK * layer
+
+        def rows_from(first):
+            return jnp.concatenate([own[at + i + first : at + i + first + HALO] for i in (0, ROWS)], axis=0)
+
+        early, late = rows_from(0), rows_from(ROWS - HALO)
+        part = slice(2 * HALO * layer, 2 * HALO * (layer + 1))
+        for_mate[part] = jnp.where(even, late, early)
+        for_cross[part] = jnp.where(even, early, late)
+
+
 def first_kernel(layers, own, mate, cross, fresh, base, store, warm, cond):
     block = own.shape[0] // layers
     index, count = place()
     body = slice(EDGE, EDGE + layers)
     for row in range(SPAN):
 
-        def rows_of(first):
+        def rows_of(array):
             if HALO <= row < HALO + ROWS:
-                return own[pl.ds(first + row - HALO, layers, stride=block), :]
-            at = first + (row + ROWS - HALO) % ROWS
-            return sides(index, *(ref[pl.ds(at, layers, stride=block), :] for ref in (mate, cross)))[int(row >= HALO)]
+                return own[pl.ds(ROWS * array + row - HALO, layers, stride=block), :]
+            at = HALO * array + row % HALO
+            return sides(index, *(ref[pl.ds(at, layers, stride=2 * HALO), :] for ref in (mate, cross)))[int(row >= HALO)]
 
         there = 1.0
         if row < HALO:
             there = jnp.where(index > 0, 1.0, 0.0)
         elif row >= HALO + ROWS:
             there = jnp.where(index < count - 1, 1.0, 0.0)
-        kind = rows_of(ROWS)
+        kind = rows_of(1)
 
         def table(values):
             return jnp.where(kind == 0.0, values[0], jnp.where(kind == 1.0, values[1], jnp.where(kind == 2.0, values[2], values[3])))
@@ -326,8 +343,8 @@
     mates = [(i, i ^ 1) for i in range(count)]
     crossing = [(i, i + 1) for i in range(1, count - 1, 2)] + [(i + 1, i) for i in range(1, count - 1, 2)]
 
-    def exchange(array):
-        return lax.ppermute(array, BOTH, mates), lax.ppermute(array, BOTH, crossing)
+    def exchange(for_mate, for_cross):
+        return lax.ppermute(for_mate, BOTH, mates), lax.ppermute(for_cross, BOTH, crossing)
 
     def call(kernel, name, shapes, *operands, scratch=(), spaces=None, cost=None, room=8 << 20):
         return pl.pallas_call(
@@ -354,7 +371,7 @@
         spaces=pltpu.HBM,
         room=66846720,
     )
-    around = exchange(sheet)
+    around = exchange(sheet, sheet)
     stack = (layers * BLOCK, spokes)
     (packed,) = call(
         pack_kernel, "pack", [stack], prior_block_warmth.reshape(-1, spokes), substance_kind.reshape(-1, spokes)
@@ -371,10 +388,14 @@
         scratch=[pltpu.VMEM((width // 128, 8 * SPAN, 128), f32)],
         cost=pl.CostEstimate(flops=10**8, bytes_accessed=2 * 10**6, transcendentals=0),
     )
-    lines = jnp.sum(bricks[:, 2 * ROWS], axis=0, keepdims=True)
-    lines = jnp.broadcast_to(lines, (magnets, 1, spokes))
-    lines, bricks, bins = lax.optimization_barrier((lines, bricks.reshape(stack), bins))
-    lines = lax.all_to_all(lines, "magnet", 0, 0).reshape(magnets, spokes)
+    bricks, bins = lax.optimization_barrier((bricks.reshape(stack), bins))
+    lines, *edges = call(
+        functools.partial(share_kernel, layers),
+        "share",
+        [(magnets * layers, spokes)] + [(2 * HALO * layers, spokes)] * 2,
+        bricks,
+    )
+    lines = lax.all_to_all(lines.reshape(magnets, layers, spokes), "magnet", 0, 0).reshape(count, spokes)
 
     padded = (SPAN, layers + 2 * EDGE, spokes)
     plain = (SPAN, layers, spokes)
@@ -383,9 +404,9 @@
         "first",
         [padded, plain, plain],
         bricks,
-        *exchange(bricks),
+        *exchange(*edges),
         scratch=[pltpu.VMEM(padded, f32), pltpu.VMEM(padded, f32)],
-        cost=pl.CostEstimate(flops=10**7, bytes_accessed=2 * 10**6, transcendentals=0),
+        cost=pl.CostEstimate(flops=0, bytes_accessed=0, transcendentals=0),
     )
     potential, heated = call(
         functools.partial(heat_kernel, layers),

time: 93.4 us -> 93.3 us (level)
  the two profiles are of different devices: /device:TPU:1 before, /device:TPU:8 now
where the time goes in v7:
time: 93.3 us; the launch traced here: 92.7 us
  starting transfers between devices  31.9 us (34%)
  waiting for transfers between devices  31.2 us (33%)
  blocking collectives  20.2 us (22%)
  Pallas kernels  6.72 us (7%)
  local copies, waits for them, and re-layouts  1.89 us (2%)
    all_to_all x1, waiting for transfers between devices, local(): lax.all_to_all(packed.reshape(layers, BLOCK, 1, spokes), 'slab', 0, 0)  22.2 us
    all_to_all x1, blocking collectives, local(): heated = lax.all_to_all(heated.reshape(layers, ROWS, spokes), 'slab', 0, 0)  20.2 us
    ppermute x2, starting transfers between devices, exchange(): lax.ppermute(for_cross, BOTH, crossing)  14.8 us
    ppermute x2, waiting for transfers between devices, exchange(): lax.ppermute(for_cross, BOTH, crossing)  8.57 us
    all_to_all x1, starting transfers between devices, local(): lax.all_to_all(lines.reshape(magnets, layers, spokes), 'magnet', 0, 0)  7.39 us
    pallas_call x7, Pallas kernels, call(): pl.pallas_call(kernel, out_shape=tuple((jax.ShapeDtypeStruct(dims, f32) f...  6.72 us
    all_to_all x1, starting transfers between devices, local(): lax.all_to_all(packed.reshape(layers, BLOCK, 1, spokes), 'slab', 0, 0)  5.88 us
    ppermute x2, starting transfers between devices, exchange(): lax.ppermute(for_mate, BOTH, mates)  3.83 us
  transfers between devices with their start and end apart: 6, of which 3 were waited for; matrix products, arithmetic and copies ran while one was open for 0% of the time, Pallas kernels for 2%

profile of v7, /device:TPU:8, one launch (start us, length us, event | category | flops | bytes accessed | tf_op | source)
XLA Modules:
  0.0 92.7 jit_solution(17050296431871446097)
XLA Ops:
  0.6 0.0 copy-start.1
  0.6 1.5 %sheet.1.own = f32[32,512]{1,0:T(8,128)} custom-call(f32[8,512]{1,0:T(8,128)} %warmth.1, f32[8,512]{1,0:T(8,128)} %voltage.1, s32[8,512]{1,0:T(8,128)} %pattern.1, s32[256,512]{1,0:T(8,128)} %cells.1), custom_call_target="tpu_custom_call" | custom-call | tf_op jit(solution)/shard_map/sheet/pallas_call | solution.py:350
  2.1 12.9 %collective-permute-start.1 = (f32[32,512]{1,0:T(8,128)}, f32[32,512]{1,0:T(8,128)S(1)}, u32[]{:S(2)}, u32[]{:S(2)}) collective-permute-start(f32[32,512]{1,0:T(8,128)} %sheet.1.own), channel_id=1, source_target_pairs={{1,2},{3,4},{5,6},{7,8},{9,10},{11,12},{13,14},{15,16},{17,18},{19... | collective-permute-start | bytes 196616 | tf_op jit(solution)/shard_map/ppermute | solution.py:347
  15.0 1.9 %collective-permute-start = (f32[32,512]{1,0:T(8,128)}, f32[32,512]{1,0:T(8,128)S(1)}, u32[]{:S(2)}, u32[]{:S(2)}) collective-permute-start(f32[32,512]{1,0:T(8,128)} %sheet.1.own), channel_id=1, source_target_pairs={{0,1},{1,0},{2,3},{3,2},{4,5},{5,4},{6,7},{7,6},{8,9},{9,8},{10,11... | collective-permute-start | bytes 196616 | tf_op jit(solution)/shard_map/ppermute | solution.py:347
  17.0 0.0 copy-done.1
  17.0 0.0 copy-start.2
  17.0 0.9 copy-done.2
  17.9 0.0 copy-start
  17.9 0.0 collective-permute-done.1.cross
  17.9 0.5 collective-permute-done.mate
  18.4 0.3 copy-done
  18.7 1.1 %gram.1 = f32[544,128]{1,0:T(8,128)} custom-call(f32[32,512]{1,0:T(8,128)S(1)} %copy-done, f32[32,512]{1,0:T(8,128)S(1)} %collective-permute-done.mate, f32[32,512]{1,0:T(8,128)S(1)} %collective-permute-done.1.cross, f32[544,128]{1,0:T(8,128)S(1)} %pack.1.packed_in), custom_call_target="tpu_custom_call" | custom-call | tf_op jit(solution)/shard_map/gram/pallas_call | solution.py:350
  19.9 5.9 %all-to-all-start = ((f32[32,17,1,128]{3,2,1,0:T(1,128)}), f32[32,17,1,128]{3,2,1,0:T(1,128)S(1)}, u32[]{:S(2)}, u32[]{:S(2)}) async-start(f32[32,17,1,128]{3,2,1,0:T(1,128)} %bitcast.2), calls=%async_computation | async-start | bytes 557056 | tf_op jit(solution)/shard_map/all_to_all | solution.py:381
  25.8 1.2 %deposit.1 = (f32[16,16,128]{2,1,0:T(8,128)S(1)}, f32[8,512]{1,0:T(8,128)S(1)}, f32[8,512]{1,0:T(8,128)S(1)}, f32[8,512]{1,0:T(8,128)S(1)}) custom-call(f32[32,512]{1,0:T(8,128)S(1)} %copy-done, f32[32,512]{1,0:T(8,128)S(1)} %collective-permute-done.mate, f32[32,512]{1,0:T(8,128)S(1)} %collective-permute-done.1.cross), custom_call_target="tpu_custom_call" | custom-call | flops 100000000 | bytes 2000000 | tf_op jit(solution)/shard_map/deposit/pallas_call | solution.py:350
  27.0 22.2 %all-to-all-done = f32[32,17,1,128]{3,2,1,0:T(1,128)S(1)} async-done(((f32[32,17,1,128]{3,2,1,0:T(1,128)}), f32[32,17,1,128]{3,2,1,0:T(1,128)S(1)}, u32[]{:S(2)}, u32[]{:S(2)}) %all-to-all-start) | async-done | bytes 278560 | tf_op jit(solution)/shard_map/all_to_all | solution.py:381
  49.2 0.8 share.1
  50.0 7.4 %all-to-all-start.1 = ((f32[16,32,128]{2,1,0:T(8,128)}), f32[16,32,128]{2,1,0:T(8,128)S(1)}, u32[]{:S(2)}, u32[]{:S(2)}) async-start(f32[16,32,128]{2,1,0:T(8,128)} %bitcast.4), calls=%async_computation.1 | async-start | bytes 524288 | tf_op jit(solution)/shard_map/all_to_all | solution.py:398
  57.4 1.9 %collective-permute-start.2 = (f32[256,128]{1,0:T(8,128)S(1)}, f32[256,128]{1,0:T(8,128)S(1)}, u32[]{:S(2)}, u32[]{:S(2)}) collective-permute-start(f32[256,128]{1,0:T(8,128)S(1)} %get-tuple-element.23), channel_id=1, source_target_pairs={{0,1},{1,0},{2,3},{3,2},{4,5},{5,4},{6,7},{7,6},{8,9},{9,8},{10,11... | collective-permute-start | bytes 393224 | tf_op jit(solution)/shard_map/ppermute | solution.py:347
  59.3 1.9 %collective-permute-start.3 = (f32[256,128]{1,0:T(8,128)S(1)}, f32[256,128]{1,0:T(8,128)S(1)}, u32[]{:S(2)}, u32[]{:S(2)}) collective-permute-start(f32[256,128]{1,0:T(8,128)S(1)} %get-tuple-element.24), channel_id=1, source_target_pairs={{1,2},{3,4},{5,6},{7,8},{9,10},{11,12},{13,14},{15,16},{17,18},{19... | collective-permute-start | bytes 393224 | tf_op jit(solution)/shard_map/ppermute | solution.py:347
  61.2 0.0 collective-permute-done.2.mate
  61.2 8.6 %collective-permute-done.3.cross = f32[256,128]{1,0:T(8,128)S(1)} collective-permute-done((f32[256,128]{1,0:T(8,128)S(1)}, f32[256,128]{1,0:T(8,128)S(1)}, u32[]{:S(2)}, u32[]{:S(2)}) %collective-permute-start.3) | collective-permute-done | bytes 131104 | tf_op jit(solution)/shard_map/ppermute | solution.py:347
  69.8 0.5 first.1
  70.2 0.0 all-to-all-done.1
  70.3 1.6 %heat.1 = (f32[8,512]{1,0:T(8,128)}, f32[256,128]{1,0:T(8,128)S(1)}) custom-call(f32[512,128]{1,0:T(8,128)S(1)} %bitcast.10, f32[8,512]{1,0:T(8,128)S(1)} %get-tuple-element.19.w0, f32[8,512]{1,0:T(8,128)S(1)} %get-tuple-element.20.w1, f32[8,512]{1,0:T(8,128)S(1)} %get-tuple-element.21.w2, f32[16,16,128]{2,1,0:T(8,128)S(1)} %get-tuple-element.22.bins, ...), custom_call_target="tpu_custom_call" | custom-call | tf_op jit(solution)/shard_map/heat/pallas_call | solution.py:350
  71.9 20.2 %all_to_all.15 = f32[32,8,128]{2,1,0:T(8,128)S(1)} all-to-all(f32[32,8,128]{2,1,0:T(8,128)S(1)} %bitcast.11), channel_id=1, replica_groups=mesh['magnet'=16,'slab'=32] {'slab'}, dimensions={0} | all-to-all | bytes 262144 | tf_op jit(solution)/shard_map/all_to_all | solution.py:421
  92.0 0.7 copy.10
  (1 shorter events, 0.0 us)
Async XLA Ops:
  0.6 16.3 %copy-start.1 = (f32[1,256,128]{2,1,0:T(8,128)S(1)}, f32[1,256,128]{2,1,0:T(8,128)}, u32[]{:S(2)}) copy-start(f32[1,256,128]{2,1,0:T(8,128)} %param.10) | copy-start | bytes 393220
  2.1 15.8 %collective-permute-start.1 = (f32[32,512]{1,0:T(8,128)}, f32[32,512]{1,0:T(8,128)S(1)}, u32[]{:S(2)}, u32[]{:S(2)}) collective-permute-start(f32[32,512]{1,0:T(8,128)} %sheet.1.own), channel_id=1, source_target_pairs={{1,2},{3,4},{5,6},{7,8},{9,10},{11,12},{13,14},{15,16},{17,18},{19... | collective-permute-start | bytes 196616 | tf_op jit(solution)/shard_map/ppermute | solution.py:347
  15.0 3.4 %collective-permute-start = (f32[32,512]{1,0:T(8,128)}, f32[32,512]{1,0:T(8,128)S(1)}, u32[]{:S(2)}, u32[]{:S(2)}) collective-permute-start(f32[32,512]{1,0:T(8,128)} %sheet.1.own), channel_id=1, source_target_pairs={{0,1},{1,0},{2,3},{3,2},{4,5},{5,4},{6,7},{7,6},{8,9},{9,8},{10,11... | collective-permute-start | bytes 196616 | tf_op jit(solution)/shard_map/ppermute | solution.py:347
  17.0 0.9 copy-start.2
  17.9 0.8 copy-start
  19.9 29.3 %all-to-all-start = ((f32[32,17,1,128]{3,2,1,0:T(1,128)}), f32[32,17,1,128]{3,2,1,0:T(1,128)S(1)}, u32[]{:S(2)}, u32[]{:S(2)}) async-start(f32[32,17,1,128]{3,2,1,0:T(1,128)} %bitcast.2), calls=%async_computation | async-start | bytes 557056 | tf_op jit(solution)/shard_map/all_to_all | solution.py:381
  50.0 20.3 %all-to-all-start.1 = ((f32[16,32,128]{2,1,0:T(8,128)}), f32[16,32,128]{2,1,0:T(8,128)S(1)}, u32[]{:S(2)}, u32[]{:S(2)}) async-start(f32[16,32,128]{2,1,0:T(8,128)} %bitcast.4), calls=%async_computation.1 | async-start | bytes 524288 | tf_op jit(solution)/shard_map/all_to_all | solution.py:398
  57.4 3.8 %collective-permute-start.2 = (f32[256,128]{1,0:T(8,128)S(1)}, f32[256,128]{1,0:T(8,128)S(1)}, u32[]{:S(2)}, u32[]{:S(2)}) collective-permute-start(f32[256,128]{1,0:T(8,128)S(1)} %get-tuple-element.23), channel_id=1, source_target_pairs={{0,1},{1,0},{2,3},{3,2},{4,5},{5,4},{6,7},{7,6},{8,9},{9,8},{10,11... | collective-permute-start | bytes 393224 | tf_op jit(solution)/shard_map/ppermute | solution.py:347
  59.3 10.5 %collective-permute-start.3 = (f32[256,128]{1,0:T(8,128)S(1)}, f32[256,128]{1,0:T(8,128)S(1)}, u32[]{:S(2)}, u32[]{:S(2)}) collective-permute-start(f32[256,128]{1,0:T(8,128)S(1)} %get-tuple-element.24), channel_id=1, source_target_pairs={{1,2},{3,4},{5,6},{7,8},{9,10},{11,12},{13,14},{15,16},{17,18},{19... | collective-permute-start | bytes 393224 | tf_op jit(solution)/shard_map/ppermute | solution.py:347

commit v8 on v7

--- a/solution.py
+++ b/solution.py
@@ -252,7 +252,7 @@
         field[EDGE + layers : 2 * EDGE + layers] = blank
 
 
-def share_kernel(layers, own, lines, for_mate, for_cross):
+def share_kernel(layers, own, lines, for_cross, for_mate):
     mine = own[pl.ds(2 * ROWS, layers, stride=BLOCK), :]
     for magnet in range(lines.shape[0] // layers):
         lines[layers * magnet : layers * (magnet + 1)] = mine
@@ -269,7 +269,7 @@
         for_cross[part] = jnp.where(even, early, late)
 
 
-def first_kernel(layers, own, mate, cross, fresh, base, store, warm, cond):
+def first_kernel(layers, own, cross, mate, fresh, base, store, warm, cond):
     block = own.shape[0] // layers
     index, count = place()
     body = slice(EDGE, EDGE + layers)
@@ -344,7 +344,8 @@
     crossing = [(i, i + 1) for i in range(1, count - 1, 2)] + [(i + 1, i) for i in range(1, count - 1, 2)]
 
     def exchange(for_mate, for_cross):
-        return lax.ppermute(for_mate, BOTH, mates), lax.ppermute(for_cross, BOTH, crossing)
+        over = lax.ppermute(for_cross, BOTH, crossing)
+        return lax.ppermute(for_mate, BOTH, mates), over
 
     def call(kernel, name, shapes, *operands, scratch=(), spaces=None, cost=None, room=8 << 20):
         return pl.pallas_call(
@@ -389,7 +390,7 @@
         cost=pl.CostEstimate(flops=10**8, bytes_accessed=2 * 10**6, transcendentals=0),
     )
     bricks, bins = lax.optimization_barrier((bricks.reshape(stack), bins))
-    lines, *edges = call(
+    lines, over, beside = call(
         functools.partial(share_kernel, layers),
         "share",
         [(magnets * layers, spokes)] + [(2 * HALO * layers, spokes)] * 2,
@@ -404,7 +405,7 @@
         "first",
         [padded, plain, plain],
         bricks,
-        *exchange(*edges),
+        *exchange(beside, over)[::-1],
         scratch=[pltpu.VMEM(padded, f32), pltpu.VMEM(padded, f32)],
         cost=pl.CostEstimate(flops=0, bytes_accessed=0, transcendentals=0),
     )

time: 93.3 us -> 91.3 us (0.979)
  waiting for transfers between devices: 31.2 us -> 29.2 us
    ppermute x4, waiting for transfers between devices: 9.04 us -> 7.01 us  [the longest x2 6.54 us: exchange(): over = lax.ppermute(for_cross, BOTH, crossing)]
where the time goes in v8:
time: 91.3 us; the launch traced here: 90.8 us
  starting transfers between devices  32.1 us (35%)
  waiting for transfers between devices  29.2 us (32%)
  blocking collectives  20.2 us (22%)
  Pallas kernels  6.72 us (7%)
  local copies, waits for them, and re-layouts  1.89 us (2%)
    all_to_all x1, waiting for transfers between devices, local(): lax.all_to_all(packed.reshape(layers, BLOCK, 1, spokes), 'slab', 0, 0)  22.2 us
    all_to_all x1, blocking collectives, local(): heated = lax.all_to_all(heated.reshape(layers, ROWS, spokes), 'slab', 0, 0)  20.2 us
    ppermute x2, starting transfers between devices, exchange(): over = lax.ppermute(for_cross, BOTH, crossing)  14.8 us
    all_to_all x1, starting transfers between devices, local(): lax.all_to_all(lines.reshape(magnets, layers, spokes), 'magnet', 0, 0)  7.39 us
    pallas_call x7, Pallas kernels, call(): pl.pallas_call(kernel, out_shape=tuple((jax.ShapeDtypeStruct(dims, f32) f...  6.72 us
    ppermute x2, waiting for transfers between devices, exchange(): over = lax.ppermute(for_cross, BOTH, crossing)  6.54 us
    all_to_all x1, starting transfers between devices, local(): lax.all_to_all(packed.reshape(layers, BLOCK, 1, spokes), 'slab', 0, 0)  5.88 us
    ppermute x2, starting transfers between devices, exchange(): return (lax.ppermute(for_mate, BOTH, mates), over)  3.95 us
  transfers between devices with their start and end apart: 6, of which 3 were waited for; matrix products, arithmetic and copies ran while one was open for 0% of the time, Pallas kernels for 2%

profile of v8, /device:TPU:8, one launch (start us, length us, event | category | flops | bytes accessed | tf_op | source)
XLA Modules:
  0.0 90.8 jit_solution(6995004782618661419)
XLA Ops:
  0.6 0.0 copy-start.1
  0.6 1.5 %sheet.1.own = f32[32,512]{1,0:T(8,128)} custom-call(f32[8,512]{1,0:T(8,128)} %warmth.1, f32[8,512]{1,0:T(8,128)} %voltage.1, s32[8,512]{1,0:T(8,128)} %pattern.1, s32[256,512]{1,0:T(8,128)} %cells.1), custom_call_target="tpu_custom_call" | custom-call | tf_op jit(solution)/shard_map/sheet/pallas_call | solution.py:351
  2.1 12.9 %collective-permute-start.1 = (f32[32,512]{1,0:T(8,128)}, f32[32,512]{1,0:T(8,128)S(1)}, u32[]{:S(2)}, u32[]{:S(2)}) collective-permute-start(f32[32,512]{1,0:T(8,128)} %sheet.1.own), channel_id=1, source_target_pairs={{1,2},{3,4},{5,6},{7,8},{9,10},{11,12},{13,14},{15,16},{17,18},{19... | collective-permute-start | bytes 196616 | tf_op jit(solution)/shard_map/ppermute | solution.py:347
  15.0 1.9 %collective-permute-start = (f32[32,512]{1,0:T(8,128)}, f32[32,512]{1,0:T(8,128)S(1)}, u32[]{:S(2)}, u32[]{:S(2)}) collective-permute-start(f32[32,512]{1,0:T(8,128)} %sheet.1.own), channel_id=1, source_target_pairs={{0,1},{1,0},{2,3},{3,2},{4,5},{5,4},{6,7},{7,6},{8,9},{9,8},{10,11... | collective-permute-start | bytes 196616 | tf_op jit(solution)/shard_map/ppermute | solution.py:348
  17.0 0.0 copy-done.1
  17.0 0.0 copy-start.2
  17.0 0.9 copy-done.2
  17.9 0.0 copy-start
  17.9 0.0 collective-permute-done.1.cross
  17.9 0.5 collective-permute-done.mate
  18.4 0.3 copy-done
  18.7 1.1 %gram.1 = f32[544,128]{1,0:T(8,128)} custom-call(f32[32,512]{1,0:T(8,128)S(1)} %copy-done, f32[32,512]{1,0:T(8,128)S(1)} %collective-permute-done.mate, f32[32,512]{1,0:T(8,128)S(1)} %collective-permute-done.1.cross, f32[544,128]{1,0:T(8,128)S(1)} %pack.1.packed_in), custom_call_target="tpu_custom_call" | custom-call | tf_op jit(solution)/shard_map/gram/pallas_call | solution.py:351
  19.9 5.9 %all-to-all-start = ((f32[32,17,1,128]{3,2,1,0:T(1,128)}), f32[32,17,1,128]{3,2,1,0:T(1,128)S(1)}, u32[]{:S(2)}, u32[]{:S(2)}) async-start(f32[32,17,1,128]{3,2,1,0:T(1,128)} %bitcast.2), calls=%async_computation | async-start | bytes 557056 | tf_op jit(solution)/shard_map/all_to_all | solution.py:382
  25.8 1.2 %deposit.1 = (f32[16,16,128]{2,1,0:T(8,128)S(1)}, f32[8,512]{1,0:T(8,128)S(1)}, f32[8,512]{1,0:T(8,128)S(1)}, f32[8,512]{1,0:T(8,128)S(1)}) custom-call(f32[32,512]{1,0:T(8,128)S(1)} %copy-done, f32[32,512]{1,0:T(8,128)S(1)} %collective-permute-done.mate, f32[32,512]{1,0:T(8,128)S(1)} %collective-permute-done.1.cross), custom_call_target="tpu_custom_call" | custom-call | flops 100000000 | bytes 2000000 | tf_op jit(solution)/shard_map/deposit/pallas_call | solution.py:351
  27.0 22.2 %all-to-all-done = f32[32,17,1,128]{3,2,1,0:T(1,128)S(1)} async-done(((f32[32,17,1,128]{3,2,1,0:T(1,128)}), f32[32,17,1,128]{3,2,1,0:T(1,128)S(1)}, u32[]{:S(2)}, u32[]{:S(2)}) %all-to-all-start) | async-done | bytes 278560 | tf_op jit(solution)/shard_map/all_to_all | solution.py:382
  49.2 0.8 share.1
  50.0 7.4 %all-to-all-start.1 = ((f32[16,32,128]{2,1,0:T(8,128)}), f32[16,32,128]{2,1,0:T(8,128)S(1)}, u32[]{:S(2)}, u32[]{:S(2)}) async-start(f32[16,32,128]{2,1,0:T(8,128)} %bitcast.4), calls=%async_computation.1 | async-start | bytes 524288 | tf_op jit(solution)/shard_map/all_to_all | solution.py:399
  57.4 1.9 %collective-permute-start.2 = (f32[256,128]{1,0:T(8,128)S(1)}, f32[256,128]{1,0:T(8,128)S(1)}, u32[]{:S(2)}, u32[]{:S(2)}) collective-permute-start(f32[256,128]{1,0:T(8,128)S(1)} %get-tuple-element.23), channel_id=1, source_target_pairs={{1,2},{3,4},{5,6},{7,8},{9,10},{11,12},{13,14},{15,16},{17,18},{19... | collective-permute-start | bytes 393224 | tf_op jit(solution)/shard_map/ppermute | solution.py:347
  59.3 2.0 %collective-permute-start.3 = (f32[256,128]{1,0:T(8,128)S(1)}, f32[256,128]{1,0:T(8,128)S(1)}, u32[]{:S(2)}, u32[]{:S(2)}) collective-permute-start(f32[256,128]{1,0:T(8,128)S(1)} %get-tuple-element.24), channel_id=1, source_target_pairs={{0,1},{1,0},{2,3},{3,2},{4,5},{5,4},{6,7},{7,6},{8,9},{9,8},{10,11... | collective-permute-start | bytes 393224 | tf_op jit(solution)/shard_map/ppermute | solution.py:348
  61.3 6.5 %collective-permute-done.2.cross = f32[256,128]{1,0:T(8,128)S(1)} collective-permute-done((f32[256,128]{1,0:T(8,128)S(1)}, f32[256,128]{1,0:T(8,128)S(1)}, u32[]{:S(2)}, u32[]{:S(2)}) %collective-permute-start.2) | collective-permute-done | bytes 131104 | tf_op jit(solution)/shard_map/ppermute | solution.py:347
  67.9 0.0 collective-permute-done.3.mate
  67.9 0.5 first.1
  68.3 0.0 all-to-all-done.1
  68.3 1.6 %heat.1 = (f32[8,512]{1,0:T(8,128)}, f32[256,128]{1,0:T(8,128)S(1)}) custom-call(f32[512,128]{1,0:T(8,128)S(1)} %bitcast.10, f32[8,512]{1,0:T(8,128)S(1)} %get-tuple-element.19.w0, f32[8,512]{1,0:T(8,128)S(1)} %get-tuple-element.20.w1, f32[8,512]{1,0:T(8,128)S(1)} %get-tuple-element.21.w2, f32[16,16,128]{2,1,0:T(8,128)S(1)} %get-tuple-element.22.bins, ...), custom_call_target="tpu_custom_call" | custom-call | tf_op jit(solution)/shard_map/heat/pallas_call | solution.py:351
  70.0 20.2 %all_to_all.15 = f32[32,8,128]{2,1,0:T(8,128)S(1)} all-to-all(f32[32,8,128]{2,1,0:T(8,128)S(1)} %bitcast.11), channel_id=1, replica_groups=mesh['magnet'=16,'slab'=32] {'slab'}, dimensions={0} | all-to-all | bytes 262144 | tf_op jit(solution)/shard_map/all_to_all | solution.py:422
  90.1 0.7 copy.10
  (1 shorter events, 0.0 us)
Async XLA Ops:
  0.6 16.3 %copy-start.1 = (f32[1,256,128]{2,1,0:T(8,128)S(1)}, f32[1,256,128]{2,1,0:T(8,128)}, u32[]{:S(2)}) copy-start(f32[1,256,128]{2,1,0:T(8,128)} %param.10) | copy-start | bytes 393220
  2.1 15.8 %collective-permute-start.1 = (f32[32,512]{1,0:T(8,128)}, f32[32,512]{1,0:T(8,128)S(1)}, u32[]{:S(2)}, u32[]{:S(2)}) collective-permute-start(f32[32,512]{1,0:T(8,128)} %sheet.1.own), channel_id=1, source_target_pairs={{1,2},{3,4},{5,6},{7,8},{9,10},{11,12},{13,14},{15,16},{17,18},{19... | collective-permute-start | bytes 196616 | tf_op jit(solution)/shard_map/ppermute | solution.py:347
  15.0 3.4 %collective-permute-start = (f32[32,512]{1,0:T(8,128)}, f32[32,512]{1,0:T(8,128)S(1)}, u32[]{:S(2)}, u32[]{:S(2)}) collective-permute-start(f32[32,512]{1,0:T(8,128)} %sheet.1.own), channel_id=1, source_target_pairs={{0,1},{1,0},{2,3},{3,2},{4,5},{5,4},{6,7},{7,6},{8,9},{9,8},{10,11... | collective-permute-start | bytes 196616 | tf_op jit(solution)/shard_map/ppermute | solution.py:348
  17.0 0.9 copy-start.2
  17.9 0.8 copy-start
  19.9 29.3 %all-to-all-start = ((f32[32,17,1,128]{3,2,1,0:T(1,128)}), f32[32,17,1,128]{3,2,1,0:T(1,128)S(1)}, u32[]{:S(2)}, u32[]{:S(2)}) async-start(f32[32,17,1,128]{3,2,1,0:T(1,128)} %bitcast.2), calls=%async_computation | async-start | bytes 557056 | tf_op jit(solution)/shard_map/all_to_all | solution.py:382
  50.0 18.4 %all-to-all-start.1 = ((f32[16,32,128]{2,1,0:T(8,128)}), f32[16,32,128]{2,1,0:T(8,128)S(1)}, u32[]{:S(2)}, u32[]{:S(2)}) async-start(f32[16,32,128]{2,1,0:T(8,128)} %bitcast.4), calls=%async_computation.1 | async-start | bytes 524288 | tf_op jit(solution)/shard_map/all_to_all | solution.py:399
  57.4 10.5 %collective-permute-start.2 = (f32[256,128]{1,0:T(8,128)S(1)}, f32[256,128]{1,0:T(8,128)S(1)}, u32[]{:S(2)}, u32[]{:S(2)}) collective-permute-start(f32[256,128]{1,0:T(8,128)S(1)} %get-tuple-element.23), channel_id=1, source_target_pairs={{1,2},{3,4},{5,6},{7,8},{9,10},{11,12},{13,14},{15,16},{17,18},{19... | collective-permute-start | bytes 393224 | tf_op jit(solution)/shard_map/ppermute | solution.py:347
  59.3 8.6 %collective-permute-start.3 = (f32[256,128]{1,0:T(8,128)S(1)}, f32[256,128]{1,0:T(8,128)S(1)}, u32[]{:S(2)}, u32[]{:S(2)}) collective-permute-start(f32[256,128]{1,0:T(8,128)S(1)} %get-tuple-element.24), channel_id=1, source_target_pairs={{0,1},{1,0},{2,3},{3,2},{4,5},{5,4},{6,7},{7,6},{8,9},{9,8},{10,11... | collective-permute-start | bytes 393224 | tf_op jit(solution)/shard_map/ppermute | solution.py:348

commit v9 on v8

--- a/solution.py
+++ b/solution.py
@@ -269,7 +269,7 @@
         for_cross[part] = jnp.where(even, early, late)
 
 
-def first_kernel(layers, own, cross, mate, fresh, base, store, warm, cond):
+def first_kernel(layers, own, edge, cross, mate, fresh, base, store, warm, cond):
     block = own.shape[0] // layers
     index, count = place()
     body = slice(EDGE, EDGE + layers)
@@ -279,7 +279,10 @@
             if HALO <= row < HALO + ROWS:
                 return own[pl.ds(ROWS * array + row - HALO, layers, stride=block), :]
             at = HALO * array + row % HALO
-            return sides(index, *(ref[pl.ds(at, layers, stride=2 * HALO), :] for ref in (mate, cross)))[int(row >= HALO)]
+            near = sides(index, *(ref[pl.ds(at, layers, stride=2 * HALO), :] for ref in (mate, cross)))[int(row >= HALO)]
+            at = ROWS * array + (row + ROWS - HALO if row < HALO else row - HALO - ROWS)
+            last = lax.axis_index("slab") == (0 if row < HALO else layers - 1)
+            return jnp.where(last, edge[pl.ds(at, layers, stride=block), :], near)
 
         there = 1.0
         if row < HALO:
@@ -340,12 +343,13 @@
     magnets, layers = lax.axis_size("magnet"), lax.axis_size("slab")
     count = magnets * layers
     width, spokes = foil_warmth.shape[1], prior_block_warmth.shape[2]
-    mates = [(i, i ^ 1) for i in range(count)]
-    crossing = [(i, i + 1) for i in range(1, count - 1, 2)] + [(i + 1, i) for i in range(1, count - 1, 2)]
-
-    def exchange(for_mate, for_cross):
-        over = lax.ppermute(for_cross, BOTH, crossing)
-        return lax.ppermute(for_mate, BOTH, mates), over
+    mates = [(i, i + 1) for i in range(0, count, 2)]
+    crossing = [(i, i + 1) for i in range(1, count - 1, 2)]
+    ends = [pair for pair in crossing if pair[1] % layers == 0]
+    inner = [pair for pair in crossing if pair[1] % layers]
+
+    def swap(array, pairs):
+        return lax.ppermute(array, BOTH, pairs + [(j, i) for i, j in pairs])
 
     def call(kernel, name, shapes, *operands, scratch=(), spaces=None, cost=None, room=8 << 20):
         return pl.pallas_call(
@@ -372,7 +376,8 @@
         spaces=pltpu.HBM,
         room=66846720,
     )
-    around = exchange(sheet, sheet)
+    across = swap(sheet, crossing)
+    around = (swap(sheet, mates), across)
     stack = (layers * BLOCK, spokes)
     (packed,) = call(
         pack_kernel, "pack", [stack], prior_block_warmth.reshape(-1, spokes), substance_kind.reshape(-1, spokes)
@@ -405,7 +410,9 @@
         "first",
         [padded, plain, plain],
         bricks,
-        *exchange(beside, over)[::-1],
+        swap(bricks, ends),
+        swap(over, inner),
+        swap(beside, mates),
         scratch=[pltpu.VMEM(padded, f32), pltpu.VMEM(padded, f32)],
         cost=pl.CostEstimate(flops=0, bytes_accessed=0, transcendentals=0),
     )

time: 91.3 us -> 91.2 us (level)
  the two profiles are of different devices: /device:TPU:8 before, /device:TPU:1 now
where the time goes in v9:
time: 91.2 us; the launch traced here: 90.6 us
  starting transfers between devices  34.2 us (38%)
  waiting for transfers between devices  24.7 us (27%)
  blocking collectives  22 us (24%)
  Pallas kernels  6.71 us (7%)
  local copies, waits for them, and re-layouts  2.23 us (2%)
    all_to_all x1, blocking collectives, local(): heated = lax.all_to_all(heated.reshape(layers, ROWS, spokes), 'slab', 0, 0)  22 us
    all_to_all x1, waiting for transfers between devices, local(): lax.all_to_all(packed.reshape(layers, BLOCK, 1, spokes), 'slab', 0, 0)  21.7 us
    ppermute x5, starting transfers between devices, swap(): return lax.ppermute(array, BOTH, pairs + [(j, i) for i, j in pairs])  14.9 us
    all_to_all x1, starting transfers between devices, local(): lax.all_to_all(packed.reshape(layers, BLOCK, 1, spokes), 'slab', 0, 0)  12.5 us
    all_to_all x1, starting transfers between devices, local(): lax.all_to_all(lines.reshape(magnets, layers, spokes), 'magnet', 0, 0)  6.75 us
    pallas_call x7, Pallas kernels, call(): pl.pallas_call(kernel, out_shape=tuple((jax.ShapeDtypeStruct(dims, f32) f...  6.71 us
    unnamed x7, local copies, waits for them, and re-layouts  2.23 us
    ppermute x5, waiting for transfers between devices, swap(): return lax.ppermute(array, BOTH, pairs + [(j, i) for i, j in pairs])  1.89 us
  transfers between devices with their start and end apart: 7, of which 4 were waited for; matrix products, arithmetic and copies ran while one was open for 0% of the time, Pallas kernels for 3%

profile of v9, /device:TPU:1, one launch (start us, length us, event | category | flops | bytes accessed | tf_op | source)
XLA Modules:
  0.0 90.6 jit_solution(8728258062241812588)
XLA Ops:
  0.6 0.0 copy-start.1
  0.6 1.5 %sheet.1.own = f32[32,512]{1,0:T(8,128)} custom-call(f32[8,512]{1,0:T(8,128)} %warmth.1, f32[8,512]{1,0:T(8,128)} %voltage.1, s32[8,512]{1,0:T(8,128)} %pattern.1, s32[256,512]{1,0:T(8,128)} %cells.1), custom_call_target="tpu_custom_call" | custom-call | tf_op jit(solution)/shard_map/sheet/pallas_call | solution.py:355
  2.1 4.9 %collective-permute-start.1 = (f32[32,512]{1,0:T(8,128)}, f32[32,512]{1,0:T(8,128)S(1)}, u32[]{:S(2)}, u32[]{:S(2)}) collective-permute-start(f32[32,512]{1,0:T(8,128)} %sheet.1.own), channel_id=1, source_target_pairs={{1,2},{3,4},{5,6},{7,8},{9,10},{11,12},{13,14},{15,16},{17,18},{19... | collective-permute-start | bytes 196616 | tf_op jit(solution)/shard_map/ppermute | solution.py:352
  7.1 4.5 %collective-permute-start = (f32[32,512]{1,0:T(8,128)}, f32[32,512]{1,0:T(8,128)S(1)}, u32[]{:S(2)}, u32[]{:S(2)}) collective-permute-start(f32[32,512]{1,0:T(8,128)} %sheet.1.own), channel_id=1, source_target_pairs={{0,1},{2,3},{4,5},{6,7},{8,9},{10,11},{12,13},{14,15},{16,17},{18,... | collective-permute-start | bytes 196616 | tf_op jit(solution)/shard_map/ppermute | solution.py:352
  11.6 0.0 copy-done.1
  11.6 0.0 copy-start.2
  11.6 0.9 copy-done.2
  12.5 0.0 copy-start
  12.5 0.0 collective-permute-done.1.cross
  12.5 0.1 collective-permute-done.mate
  12.7 0.7 copy-done
  13.3 1.1 %gram.1 = f32[544,128]{1,0:T(8,128)} custom-call(f32[32,512]{1,0:T(8,128)S(1)} %copy-done, f32[32,512]{1,0:T(8,128)S(1)} %collective-permute-done.mate, f32[32,512]{1,0:T(8,128)S(1)} %collective-permute-done.1.cross, f32[544,128]{1,0:T(8,128)S(1)} %pack.1.packed_in), custom_call_target="tpu_custom_call" | custom-call | tf_op jit(solution)/shard_map/gram/pallas_call | solution.py:355
  14.5 12.5 %all-to-all-start = ((f32[32,17,1,128]{3,2,1,0:T(1,128)}), f32[32,17,1,128]{3,2,1,0:T(1,128)S(1)}, u32[]{:S(2)}, u32[]{:S(2)}) async-start(f32[32,17,1,128]{3,2,1,0:T(1,128)} %bitcast.2), calls=%async_computation | async-start | bytes 557056 | tf_op jit(solution)/shard_map/all_to_all | solution.py:387
  27.0 1.2 %deposit.1 = (f32[16,16,128]{2,1,0:T(8,128)S(1)}, f32[8,512]{1,0:T(8,128)S(1)}, f32[8,512]{1,0:T(8,128)S(1)}, f32[8,512]{1,0:T(8,128)S(1)}) custom-call(f32[32,512]{1,0:T(8,128)S(1)} %copy-done, f32[32,512]{1,0:T(8,128)S(1)} %collective-permute-done.mate, f32[32,512]{1,0:T(8,128)S(1)} %collective-permute-done.1.cross), custom_call_target="tpu_custom_call" | custom-call | flops 100000000 | bytes 2000000 | tf_op jit(solution)/shard_map/deposit/pallas_call | solution.py:355
  28.3 21.7 %all-to-all-done = f32[32,17,1,128]{3,2,1,0:T(1,128)S(1)} async-done(((f32[32,17,1,128]{3,2,1,0:T(1,128)}), f32[32,17,1,128]{3,2,1,0:T(1,128)S(1)}, u32[]{:S(2)}, u32[]{:S(2)}) %all-to-all-start) | async-done | bytes 278560 | tf_op jit(solution)/shard_map/all_to_all | solution.py:387
  50.0 0.7 collective-permute-start.2
  50.7 0.8 share.1
  51.4 6.8 %all-to-all-start.1 = ((f32[16,32,128]{2,1,0:T(8,128)}), f32[16,32,128]{2,1,0:T(8,128)S(1)}, u32[]{:S(2)}, u32[]{:S(2)}) async-start(f32[16,32,128]{2,1,0:T(8,128)} %bitcast.4), calls=%async_computation.1 | async-start | bytes 524288 | tf_op jit(solution)/shard_map/all_to_all | solution.py:404
  58.2 2.5 %collective-permute-start.3 = (f32[256,128]{1,0:T(8,128)S(1)}, f32[256,128]{1,0:T(8,128)S(1)}, u32[]{:S(2)}, u32[]{:S(2)}) collective-permute-start(f32[256,128]{1,0:T(8,128)S(1)} %get-tuple-element.23), channel_id=1, source_target_pairs={{1,2},{3,4},{5,6},{7,8},{9,10},{11,12},{13,14},{15,16},{17,18},{19... | collective-permute-start | bytes 393224 | tf_op jit(solution)/shard_map/ppermute | solution.py:352
  60.7 2.3 %collective-permute-start.4 = (f32[256,128]{1,0:T(8,128)S(1)}, f32[256,128]{1,0:T(8,128)S(1)}, u32[]{:S(2)}, u32[]{:S(2)}) collective-permute-start(f32[256,128]{1,0:T(8,128)S(1)} %get-tuple-element.24), channel_id=1, source_target_pairs={{0,1},{2,3},{4,5},{6,7},{8,9},{10,11},{12,13},{14,15},{16,17},{18,... | collective-permute-start | bytes 393224 | tf_op jit(solution)/shard_map/ppermute | solution.py:352
  63.0 1.8 %collective-permute-done.3.cross = f32[256,128]{1,0:T(8,128)S(1)} collective-permute-done((f32[256,128]{1,0:T(8,128)S(1)}, f32[256,128]{1,0:T(8,128)S(1)}, u32[]{:S(2)}, u32[]{:S(2)}) %collective-permute-start.3) | collective-permute-done | bytes 131104 | tf_op jit(solution)/shard_map/ppermute | solution.py:352
  64.8 0.0 collective-permute-done.4.mate
  64.8 0.0 collective-permute-done.2.edge
  64.8 0.5 first.1
  65.2 1.1 %all-to-all-done.1 = f32[16,32,128]{2,1,0:T(8,128)S(1)} async-done(((f32[16,32,128]{2,1,0:T(8,128)}), f32[16,32,128]{2,1,0:T(8,128)S(1)}, u32[]{:S(2)}, u32[]{:S(2)}) %all-to-all-start.1) | async-done | bytes 262176 | tf_op jit(solution)/shard_map/all_to_all | solution.py:404
  66.3 1.6 %heat.1 = (f32[8,512]{1,0:T(8,128)}, f32[256,128]{1,0:T(8,128)S(1)}) custom-call(f32[512,128]{1,0:T(8,128)S(1)} %bitcast.11, f32[8,512]{1,0:T(8,128)S(1)} %get-tuple-element.19.w0, f32[8,512]{1,0:T(8,128)S(1)} %get-tuple-element.20.w1, f32[8,512]{1,0:T(8,128)S(1)} %get-tuple-element.21.w2, f32[16,16,128]{2,1,0:T(8,128)S(1)} %get-tuple-element.22.bins, ...), custom_call_target="tpu_custom_call" | custom-call | tf_op jit(solution)/shard_map/heat/pallas_call | solution.py:355
  67.9 22.0 %all_to_all.15 = f32[32,8,128]{2,1,0:T(8,128)S(1)} all-to-all(f32[32,8,128]{2,1,0:T(8,128)S(1)} %bitcast.12), channel_id=1, replica_groups=mesh['magnet'=16,'slab'=32] {'slab'}, dimensions={0} | all-to-all | bytes 262144 | tf_op jit(solution)/shard_map/all_to_all | solution.py:429
  90.0 0.7 copy.10
  (1 shorter events, 0.0 us)
Async XLA Ops:
  0.6 11.0 %copy-start.1 = (f32[1,256,128]{2,1,0:T(8,128)S(1)}, f32[1,256,128]{2,1,0:T(8,128)}, u32[]{:S(2)}) copy-start(f32[1,256,128]{2,1,0:T(8,128)} %param.10) | copy-start | bytes 393220
  2.1 10.4 %collective-permute-start.1 = (f32[32,512]{1,0:T(8,128)}, f32[32,512]{1,0:T(8,128)S(1)}, u32[]{:S(2)}, u32[]{:S(2)}) collective-permute-start(f32[32,512]{1,0:T(8,128)} %sheet.1.own), channel_id=1, source_target_pairs={{1,2},{3,4},{5,6},{7,8},{9,10},{11,12},{13,14},{15,16},{17,18},{19... | collective-permute-start | bytes 196616 | tf_op jit(solution)/shard_map/ppermute | solution.py:352
  7.1 5.6 %collective-permute-start = (f32[32,512]{1,0:T(8,128)}, f32[32,512]{1,0:T(8,128)S(1)}, u32[]{:S(2)}, u32[]{:S(2)}) collective-permute-start(f32[32,512]{1,0:T(8,128)} %sheet.1.own), channel_id=1, source_target_pairs={{0,1},{2,3},{4,5},{6,7},{8,9},{10,11},{12,13},{14,15},{16,17},{18,... | collective-permute-start | bytes 196616 | tf_op jit(solution)/shard_map/ppermute | solution.py:352
  11.6 0.9 %copy-start.2 = (s32[1,256,128]{2,1,0:T(8,128)S(1)}, s32[1,256,128]{2,1,0:T(8,128)}, u32[]{:S(2)}) copy-start(s32[1,256,128]{2,1,0:T(8,128)} %param.11) | copy-start | bytes 393220
  12.5 0.8 copy-start
  14.5 35.5 %all-to-all-start = ((f32[32,17,1,128]{3,2,1,0:T(1,128)}), f32[32,17,1,128]{3,2,1,0:T(1,128)S(1)}, u32[]{:S(2)}, u32[]{:S(2)}) async-start(f32[32,17,1,128]{3,2,1,0:T(1,128)} %bitcast.2), calls=%async_computation | async-start | bytes 557056 | tf_op jit(solution)/shard_map/all_to_all | solution.py:387
  50.0 14.8 %collective-permute-start.2 = (f32[544,128]{1,0:T(8,128)S(1)}, f32[544,128]{1,0:T(8,128)S(1)}, u32[]{:S(2)}, u32[]{:S(2)}) collective-permute-start(f32[544,128]{1,0:T(8,128)S(1)} %bitcast.8), channel_id=1, source_target_pairs={{31,32},{63,64},{95,96},{127,128},{159,160},{191,192},{223,224},{2... | collective-permute-start | bytes 835592 | tf_op jit(solution)/shard_map/ppermute | solution.py:352
  51.4 14.9 %all-to-all-start.1 = ((f32[16,32,128]{2,1,0:T(8,128)}), f32[16,32,128]{2,1,0:T(8,128)S(1)}, u32[]{:S(2)}, u32[]{:S(2)}) async-start(f32[16,32,128]{2,1,0:T(8,128)} %bitcast.4), calls=%async_computation.1 | async-start | bytes 524288 | tf_op jit(solution)/shard_map/all_to_all | solution.py:404
  58.2 6.6 %collective-permute-start.3 = (f32[256,128]{1,0:T(8,128)S(1)}, f32[256,128]{1,0:T(8,128)S(1)}, u32[]{:S(2)}, u32[]{:S(2)}) collective-permute-start(f32[256,128]{1,0:T(8,128)S(1)} %get-tuple-element.23), channel_id=1, source_target_pairs={{1,2},{3,4},{5,6},{7,8},{9,10},{11,12},{13,14},{15,16},{17,18},{19... | collective-permute-start | bytes 393224 | tf_op jit(solution)/shard_map/ppermute | solution.py:352
  60.7 4.0 %collective-permute-start.4 = (f32[256,128]{1,0:T(8,128)S(1)}, f32[256,128]{1,0:T(8,128)S(1)}, u32[]{:S(2)}, u32[]{:S(2)}) collective-permute-start(f32[256,128]{1,0:T(8,128)S(1)} %get-tuple-element.24), channel_id=1, source_target_pairs={{0,1},{2,3},{4,5},{6,7},{8,9},{10,11},{12,13},{14,15},{16,17},{18,... | collective-permute-start | bytes 393224 | tf_op jit(solution)/shard_map/ppermute | solution.py:352

commit v10 on v9

--- a/solution.py
+++ b/solution.py
@@ -252,7 +252,7 @@
         field[EDGE + layers : 2 * EDGE + layers] = blank
 
 
-def share_kernel(layers, own, lines, for_cross, for_mate):
+def share_kernel(layers, own, lines, for_cross, for_mate, for_end):
     mine = own[pl.ds(2 * ROWS, layers, stride=BLOCK), :]
     for magnet in range(lines.shape[0] // layers):
         lines[layers * magnet : layers * (magnet + 1)] = mine
@@ -267,9 +267,10 @@
         part = slice(2 * HALO * layer, 2 * HALO * (layer + 1))
         for_mate[part] = jnp.where(even, late, early)
         for_cross[part] = jnp.where(even, early, late)
-
-
-def first_kernel(layers, own, edge, cross, mate, fresh, base, store, warm, cond):
+        for_end[part] = jnp.where(even, early, late)
+
+
+def first_kernel(layers, own, cross, mate, end, fresh, base, store, warm, cond):
     block = own.shape[0] // layers
     index, count = place()
     body = slice(EDGE, EDGE + layers)
@@ -278,11 +279,10 @@
         def rows_of(array):
             if HALO <= row < HALO + ROWS:
                 return own[pl.ds(ROWS * array + row - HALO, layers, stride=block), :]
-            at = HALO * array + row % HALO
-            near = sides(index, *(ref[pl.ds(at, layers, stride=2 * HALO), :] for ref in (mate, cross)))[int(row >= HALO)]
-            at = ROWS * array + (row + ROWS - HALO if row < HALO else row - HALO - ROWS)
+            at = pl.ds(HALO * array + row % HALO, layers, stride=2 * HALO)
+            near = sides(index, mate[at, :], cross[at, :])[int(row >= HALO)]
             last = lax.axis_index("slab") == (0 if row < HALO else layers - 1)
-            return jnp.where(last, edge[pl.ds(at, layers, stride=block), :], near)
+            return jnp.where(last, end[at, :], near)
 
         there = 1.0
         if row < HALO:
@@ -395,10 +395,10 @@
         cost=pl.CostEstimate(flops=10**8, bytes_accessed=2 * 10**6, transcendentals=0),
     )
     bricks, bins = lax.optimization_barrier((bricks.reshape(stack), bins))
-    lines, over, beside = call(
+    lines, over, beside, end = call(
         functools.partial(share_kernel, layers),
         "share",
-        [(magnets * layers, spokes)] + [(2 * HALO * layers, spokes)] * 2,
+        [(magnets * layers, spokes)] + [(2 * HALO * layers, spokes)] * 3,
         bricks,
     )
     lines = lax.all_to_all(lines.reshape(magnets, layers, spokes), "magnet", 0, 0).reshape(count, spokes)
@@ -410,9 +410,9 @@
         "first",
         [padded, plain, plain],
         bricks,
-        swap(bricks, ends),
         swap(over, inner),
         swap(beside, mates),
+        swap(end, ends),
         scratch=[pltpu.VMEM(padded, f32), pltpu.VMEM(padded, f32)],
         cost=pl.CostEstimate(flops=0, bytes_accessed=0, transcendentals=0),
     )

time: 91.2 us -> 95.3 us (1.045)
  the two profiles are of different devices: /device:TPU:1 before, /device:TPU:8 now
where the time goes in v10:
time: 95.3 us; the launch traced here: 94.8 us
  starting transfers between devices  36.4 us (38%)
  waiting for transfers between devices  28.8 us (30%)
  blocking collectives  20.2 us (21%)
  Pallas kernels  6.75 us (7%)
  local copies, waits for them, and re-layouts  1.89 us (2%)
    ppermute x5, starting transfers between devices, swap(): return lax.ppermute(array, BOTH, pairs + [(j, i) for i, j in pairs])  23.1 us
    all_to_all x1, waiting for transfers between devices, local(): lax.all_to_all(packed.reshape(layers, BLOCK, 1, spokes), 'slab', 0, 0)  22.2 us
    all_to_all x1, blocking collectives, local(): heated = lax.all_to_all(heated.reshape(layers, ROWS, spokes), 'slab', 0, 0)  20.2 us
    all_to_all x1, starting transfers between devices, local(): lax.all_to_all(lines.reshape(magnets, layers, spokes), 'magnet', 0, 0)  7.39 us
    pallas_call x7, Pallas kernels, call(): pl.pallas_call(kernel, out_shape=tuple((jax.ShapeDtypeStruct(dims, f32) f...  6.75 us
    ppermute x5, waiting for transfers between devices, swap(): return lax.ppermute(array, BOTH, pairs + [(j, i) for i, j in pairs])  6.64 us
    all_to_all x1, starting transfers between devices, local(): lax.all_to_all(packed.reshape(layers, BLOCK, 1, spokes), 'slab', 0, 0)  5.88 us
  transfers between devices with their start and end apart: 7, of which 3 were waited for; matrix products, arithmetic and copies ran while one was open for 0% of the time, Pallas kernels for 2%

profile of v10, /device:TPU:8, one launch (start us, length us, event | category | flops | bytes accessed | tf_op | source)
XLA Modules:
  0.0 94.8 jit_solution(17174169036714915105)
XLA Ops:
  0.6 0.0 copy-start.1
  0.6 1.5 %sheet.1.own = f32[32,512]{1,0:T(8,128)} custom-call(f32[8,512]{1,0:T(8,128)} %warmth.1, f32[8,512]{1,0:T(8,128)} %voltage.1, s32[8,512]{1,0:T(8,128)} %pattern.1, s32[256,512]{1,0:T(8,128)} %cells.1), custom_call_target="tpu_custom_call" | custom-call | tf_op jit(solution)/shard_map/sheet/pallas_call | solution.py:355
  2.1 12.9 %collective-permute-start.1 = (f32[32,512]{1,0:T(8,128)}, f32[32,512]{1,0:T(8,128)S(1)}, u32[]{:S(2)}, u32[]{:S(2)}) collective-permute-start(f32[32,512]{1,0:T(8,128)} %sheet.1.own), channel_id=1, source_target_pairs={{1,2},{3,4},{5,6},{7,8},{9,10},{11,12},{13,14},{15,16},{17,18},{19... | collective-permute-start | bytes 196616 | tf_op jit(solution)/shard_map/ppermute | solution.py:352
  15.0 1.9 %collective-permute-start = (f32[32,512]{1,0:T(8,128)}, f32[32,512]{1,0:T(8,128)S(1)}, u32[]{:S(2)}, u32[]{:S(2)}) collective-permute-start(f32[32,512]{1,0:T(8,128)} %sheet.1.own), channel_id=1, source_target_pairs={{0,1},{2,3},{4,5},{6,7},{8,9},{10,11},{12,13},{14,15},{16,17},{18,... | collective-permute-start | bytes 196616 | tf_op jit(solution)/shard_map/ppermute | solution.py:352
  17.0 0.0 copy-done.1
  17.0 0.0 copy-start.2
  17.0 0.9 copy-done.2
  17.9 0.0 copy-start
  17.9 0.0 collective-permute-done.1.cross
  17.9 0.5 collective-permute-done.mate
  18.4 0.3 copy-done
  18.7 1.1 %gram.1 = f32[544,128]{1,0:T(8,128)} custom-call(f32[32,512]{1,0:T(8,128)S(1)} %copy-done, f32[32,512]{1,0:T(8,128)S(1)} %collective-permute-done.mate, f32[32,512]{1,0:T(8,128)S(1)} %collective-permute-done.1.cross, f32[544,128]{1,0:T(8,128)S(1)} %pack.1.packed_in), custom_call_target="tpu_custom_call" | custom-call | tf_op jit(solution)/shard_map/gram/pallas_call | solution.py:355
  19.9 5.9 %all-to-all-start = ((f32[32,17,1,128]{3,2,1,0:T(1,128)}), f32[32,17,1,128]{3,2,1,0:T(1,128)S(1)}, u32[]{:S(2)}, u32[]{:S(2)}) async-start(f32[32,17,1,128]{3,2,1,0:T(1,128)} %bitcast.2), calls=%async_computation | async-start | bytes 557056 | tf_op jit(solution)/shard_map/all_to_all | solution.py:387
  25.8 1.2 %deposit.1 = (f32[16,16,128]{2,1,0:T(8,128)S(1)}, f32[8,512]{1,0:T(8,128)S(1)}, f32[8,512]{1,0:T(8,128)S(1)}, f32[8,512]{1,0:T(8,128)S(1)}) custom-call(f32[32,512]{1,0:T(8,128)S(1)} %copy-done, f32[32,512]{1,0:T(8,128)S(1)} %collective-permute-done.mate, f32[32,512]{1,0:T(8,128)S(1)} %collective-permute-done.1.cross), custom_call_target="tpu_custom_call" | custom-call | flops 100000000 | bytes 2000000 | tf_op jit(solution)/shard_map/deposit/pallas_call | solution.py:355
  27.0 22.2 %all-to-all-done = f32[32,17,1,128]{3,2,1,0:T(1,128)S(1)} async-done(((f32[32,17,1,128]{3,2,1,0:T(1,128)}), f32[32,17,1,128]{3,2,1,0:T(1,128)S(1)}, u32[]{:S(2)}, u32[]{:S(2)}) %all-to-all-start) | async-done | bytes 278560 | tf_op jit(solution)/shard_map/all_to_all | solution.py:387
  49.2 0.8 share.1
  50.0 7.4 %all-to-all-start.1 = ((f32[16,32,128]{2,1,0:T(8,128)}), f32[16,32,128]{2,1,0:T(8,128)S(1)}, u32[]{:S(2)}, u32[]{:S(2)}) async-start(f32[16,32,128]{2,1,0:T(8,128)} %bitcast.4), calls=%async_computation.1 | async-start | bytes 524288 | tf_op jit(solution)/shard_map/all_to_all | solution.py:404
  57.4 0.7 collective-permute-start.2
  58.0 3.3 %collective-permute-start.3 = (f32[256,128]{1,0:T(8,128)S(1)}, f32[256,128]{1,0:T(8,128)S(1)}, u32[]{:S(2)}, u32[]{:S(2)}) collective-permute-start(f32[256,128]{1,0:T(8,128)S(1)} %get-tuple-element.25), channel_id=1, source_target_pairs={{0,1},{2,3},{4,5},{6,7},{8,9},{10,11},{12,13},{14,15},{16,17},{18,... | collective-permute-start | bytes 393224 | tf_op jit(solution)/shard_map/ppermute | solution.py:352
  61.3 4.3 %collective-permute-start.4 = (f32[256,128]{1,0:T(8,128)S(1)}, f32[256,128]{1,0:T(8,128)S(1)}, u32[]{:S(2)}, u32[]{:S(2)}) collective-permute-start(f32[256,128]{1,0:T(8,128)S(1)} %get-tuple-element.26), channel_id=1, source_target_pairs={{31,32},{63,64},{95,96},{127,128},{159,160},{191,192},{223,224},{2... | collective-permute-start | bytes 393224 | tf_op jit(solution)/shard_map/ppermute | solution.py:352
  65.6 0.0 collective-permute-done.2.cross
  65.7 0.0 collective-permute-done.3.mate
  65.7 6.2 %collective-permute-done.4.end = f32[256,128]{1,0:T(8,128)S(1)} collective-permute-done((f32[256,128]{1,0:T(8,128)S(1)}, f32[256,128]{1,0:T(8,128)S(1)}, u32[]{:S(2)}, u32[]{:S(2)}) %collective-permute-start.4) | collective-permute-done | bytes 131104 | tf_op jit(solution)/shard_map/ppermute | solution.py:352
  71.8 0.5 first.1
  72.3 0.0 all-to-all-done.1
  72.3 1.6 %heat.1 = (f32[8,512]{1,0:T(8,128)}, f32[256,128]{1,0:T(8,128)S(1)}) custom-call(f32[512,128]{1,0:T(8,128)S(1)} %bitcast.10, f32[8,512]{1,0:T(8,128)S(1)} %get-tuple-element.20.w0, f32[8,512]{1,0:T(8,128)S(1)} %get-tuple-element.21.w1, f32[8,512]{1,0:T(8,128)S(1)} %get-tuple-element.22.w2, f32[16,16,128]{2,1,0:T(8,128)S(1)} %get-tuple-element.23.bins, ...), custom_call_target="tpu_custom_call" | custom-call | tf_op jit(solution)/shard_map/heat/pallas_call | solution.py:355
  73.9 20.2 %all_to_all.15 = f32[32,8,128]{2,1,0:T(8,128)S(1)} all-to-all(f32[32,8,128]{2,1,0:T(8,128)S(1)} %bitcast.11), channel_id=1, replica_groups=mesh['magnet'=16,'slab'=32] {'slab'}, dimensions={0} | all-to-all | bytes 262144 | tf_op jit(solution)/shard_map/all_to_all | solution.py:429
  94.1 0.7 copy.10
  (1 shorter events, 0.0 us)
Async XLA Ops:
  0.6 16.3 %copy-start.1 = (f32[1,256,128]{2,1,0:T(8,128)S(1)}, f32[1,256,128]{2,1,0:T(8,128)}, u32[]{:S(2)}) copy-start(f32[1,256,128]{2,1,0:T(8,128)} %param.10) | copy-start | bytes 393220
  2.1 15.8 %collective-permute-start.1 = (f32[32,512]{1,0:T(8,128)}, f32[32,512]{1,0:T(8,128)S(1)}, u32[]{:S(2)}, u32[]{:S(2)}) collective-permute-start(f32[32,512]{1,0:T(8,128)} %sheet.1.own), channel_id=1, source_target_pairs={{1,2},{3,4},{5,6},{7,8},{9,10},{11,12},{13,14},{15,16},{17,18},{19... | collective-permute-start | bytes 196616 | tf_op jit(solution)/shard_map/ppermute | solution.py:352
  15.0 3.4 %collective-permute-start = (f32[32,512]{1,0:T(8,128)}, f32[32,512]{1,0:T(8,128)S(1)}, u32[]{:S(2)}, u32[]{:S(2)}) collective-permute-start(f32[32,512]{1,0:T(8,128)} %sheet.1.own), channel_id=1, source_target_pairs={{0,1},{2,3},{4,5},{6,7},{8,9},{10,11},{12,13},{14,15},{16,17},{18,... | collective-permute-start | bytes 196616 | tf_op jit(solution)/shard_map/ppermute | solution.py:352
  17.0 0.9 copy-start.2
  17.9 0.8 copy-start
  19.9 29.3 %all-to-all-start = ((f32[32,17,1,128]{3,2,1,0:T(1,128)}), f32[32,17,1,128]{3,2,1,0:T(1,128)S(1)}, u32[]{:S(2)}, u32[]{:S(2)}) async-start(f32[32,17,1,128]{3,2,1,0:T(1,128)} %bitcast.2), calls=%async_computation | async-start | bytes 557056 | tf_op jit(solution)/shard_map/all_to_all | solution.py:387
  50.0 22.4 %all-to-all-start.1 = ((f32[16,32,128]{2,1,0:T(8,128)}), f32[16,32,128]{2,1,0:T(8,128)S(1)}, u32[]{:S(2)}, u32[]{:S(2)}) async-start(f32[16,32,128]{2,1,0:T(8,128)} %bitcast.4), calls=%async_computation.1 | async-start | bytes 524288 | tf_op jit(solution)/shard_map/all_to_all | solution.py:404
  57.4 8.3 %collective-permute-start.2 = (f32[256,128]{1,0:T(8,128)S(1)}, f32[256,128]{1,0:T(8,128)S(1)}, u32[]{:S(2)}, u32[]{:S(2)}) collective-permute-start(f32[256,128]{1,0:T(8,128)S(1)} %get-tuple-element.24), channel_id=1, source_target_pairs={{1,2},{3,4},{5,6},{7,8},{9,10},{11,12},{13,14},{15,16},{17,18},{19... | collective-permute-start | bytes 393224 | tf_op jit(solution)/shard_map/ppermute | solution.py:352
  58.0 7.6 %collective-permute-start.3 = (f32[256,128]{1,0:T(8,128)S(1)}, f32[256,128]{1,0:T(8,128)S(1)}, u32[]{:S(2)}, u32[]{:S(2)}) collective-permute-start(f32[256,128]{1,0:T(8,128)S(1)} %get-tuple-element.25), channel_id=1, source_target_pairs={{0,1},{2,3},{4,5},{6,7},{8,9},{10,11},{12,13},{14,15},{16,17},{18,... | collective-permute-start | bytes 393224 | tf_op jit(solution)/shard_map/ppermute | solution.py:352
  61.3 10.5 %collective-permute-start.4 = (f32[256,128]{1,0:T(8,128)S(1)}, f32[256,128]{1,0:T(8,128)S(1)}, u32[]{:S(2)}, u32[]{:S(2)}) collective-permute-start(f32[256,128]{1,0:T(8,128)S(1)} %get-tuple-element.26), channel_id=1, source_target_pairs={{31,32},{63,64},{95,96},{127,128},{159,160},{191,192},{223,224},{2... | collective-permute-start | bytes 393224 | tf_op jit(solution)/shard_map/ppermute | solution.py:352

commit v11 on v7

--- a/solution.py
+++ b/solution.py
@@ -252,24 +252,17 @@
         field[EDGE + layers : 2 * EDGE + layers] = blank
 
 
-def share_kernel(layers, own, lines, for_mate, for_cross):
+def share_kernel(layers, own, lines, early, late):
     mine = own[pl.ds(2 * ROWS, layers, stride=BLOCK), :]
     for magnet in range(lines.shape[0] // layers):
         lines[layers * magnet : layers * (magnet + 1)] = mine
-    even = place()[0] % 2 == 0
     for layer in range(layers):
-        at = BLOCK * layer
-
-        def rows_from(first):
-            return jnp.concatenate([own[at + i + first : at + i + first + HALO] for i in (0, ROWS)], axis=0)
-
-        early, late = rows_from(0), rows_from(ROWS - HALO)
         part = slice(2 * HALO * layer, 2 * HALO * (layer + 1))
-        for_mate[part] = jnp.where(even, late, early)
-        for_cross[part] = jnp.where(even, early, late)
-
-
-def first_kernel(layers, own, mate, cross, fresh, base, store, warm, cond):
+        for out, first in ((early, BLOCK * layer), (late, BLOCK * layer + ROWS - HALO)):
+            out[part] = jnp.concatenate([own[first : first + HALO], own[first + ROWS : first + ROWS + HALO]], axis=0)
+
+
+def first_kernel(layers, own, after, before, fresh, base, store, warm, cond):
     block = own.shape[0] // layers
     index, count = place()
     body = slice(EDGE, EDGE + layers)
@@ -278,8 +271,8 @@
         def rows_of(array):
             if HALO <= row < HALO + ROWS:
                 return own[pl.ds(ROWS * array + row - HALO, layers, stride=block), :]
-            at = HALO * array + row % HALO
-            return sides(index, *(ref[pl.ds(at, layers, stride=2 * HALO), :] for ref in (mate, cross)))[int(row >= HALO)]
+            source = before if row < HALO else after
+            return source[pl.ds(HALO * array + row % HALO, layers, stride=2 * HALO), :]
 
         there = 1.0
         if row < HALO:
@@ -341,10 +334,9 @@
     count = magnets * layers
     width, spokes = foil_warmth.shape[1], prior_block_warmth.shape[2]
     mates = [(i, i ^ 1) for i in range(count)]
-    crossing = [(i, i + 1) for i in range(1, count - 1, 2)] + [(i + 1, i) for i in range(1, count - 1, 2)]
-
-    def exchange(for_mate, for_cross):
-        return lax.ppermute(for_mate, BOTH, mates), lax.ppermute(for_cross, BOTH, crossing)
+    onward = [(i, i + 1) for i in range(count - 1)]
+    backward = [(i + 1, i) for i in range(count - 1)]
+    crossing = onward[1::2] + backward[1::2]
 
     def call(kernel, name, shapes, *operands, scratch=(), spaces=None, cost=None, room=8 << 20):
         return pl.pallas_call(
@@ -371,7 +363,8 @@
         spaces=pltpu.HBM,
         room=66846720,
     )
-    around = exchange(sheet, sheet)
+    across = lax.ppermute(sheet, BOTH, crossing)
+    around = (lax.ppermute(sheet, BOTH, mates), across)
     stack = (layers * BLOCK, spokes)
     (packed,) = call(
         pack_kernel, "pack", [stack], prior_block_warmth.reshape(-1, spokes), substance_kind.reshape(-1, spokes)
@@ -389,7 +382,7 @@
         cost=pl.CostEstimate(flops=10**8, bytes_accessed=2 * 10**6, transcendentals=0),
     )
     bricks, bins = lax.optimization_barrier((bricks.reshape(stack), bins))
-    lines, *edges = call(
+    lines, early, late = call(
         functools.partial(share_kernel, layers),
         "share",
         [(magnets * layers, spokes)] + [(2 * HALO * layers, spokes)] * 2,
@@ -404,7 +397,8 @@
         "first",
         [padded, plain, plain],
         bricks,
-        *exchange(*edges),
+        lax.ppermute(early, BOTH, backward),
+        lax.ppermute(late, BOTH, onward),
         scratch=[pltpu.VMEM(padded, f32), pltpu.VMEM(padded, f32)],
         cost=pl.CostEstimate(flops=0, bytes_accessed=0, transcendentals=0),
     )

time: 93.3 us -> 93.2 us (level)
  transfers between devices with their start and end apart: 6 -> 6, of which waited for: 3 -> 4; matrix products, arithmetic and copies ran while one was open for 0% -> 0% of each run, Pallas kernels for 2% -> 2%
where the time goes in v11:
time: 93.2 us; the launch traced here: 92.7 us
  starting transfers between devices  32.4 us (35%)
  waiting for transfers between devices  30.8 us (33%)
  blocking collectives  20.2 us (22%)
  Pallas kernels  6.71 us (7%)
  local copies, waits for them, and re-layouts  1.89 us (2%)
    all_to_all x1, waiting for transfers between devices, local(): lax.all_to_all(packed.reshape(layers, BLOCK, 1, spokes), 'slab', 0, 0)  22.2 us
    all_to_all x1, blocking collectives, local(): heated = lax.all_to_all(heated.reshape(layers, ROWS, spokes), 'slab', 0, 0)  20.2 us
    ppermute x1, starting transfers between devices, local(): across = lax.ppermute(sheet, BOTH, crossing)  12.9 us
    ppermute x1, waiting for transfers between devices, local(): lax.ppermute(late, BOTH, onward)  8.01 us
    all_to_all x1, starting transfers between devices, local(): lax.all_to_all(lines.reshape(magnets, layers, spokes), 'magnet', 0, 0)  7.39 us
    pallas_call x7, Pallas kernels, call(): pl.pallas_call(kernel, out_shape=tuple((jax.ShapeDtypeStruct(dims, f32) f...  6.71 us
    all_to_all x1, starting transfers between devices, local(): lax.all_to_all(packed.reshape(layers, BLOCK, 1, spokes), 'slab', 0, 0)  5.88 us
    ppermute x1, starting transfers between devices, local(): lax.ppermute(late, BOTH, onward)  2.41 us
  transfers between devices with their start and end apart: 6, of which 4 were waited for; matrix products, arithmetic and copies ran while one was open for 0% of the time, Pallas kernels for 2%

profile of v11, /device:TPU:8, one launch (start us, length us, event | category | flops | bytes accessed | tf_op | source)
XLA Modules:
  0.0 92.7 jit_solution(798374578247112342)
XLA Ops:
  0.6 0.0 copy-start.1
  0.6 1.5 %sheet.1.own = f32[32,512]{1,0:T(8,128)} custom-call(f32[8,512]{1,0:T(8,128)} %warmth.1, f32[8,512]{1,0:T(8,128)} %voltage.1, s32[8,512]{1,0:T(8,128)} %pattern.1, s32[256,512]{1,0:T(8,128)} %cells.1), custom_call_target="tpu_custom_call" | custom-call | tf_op jit(solution)/shard_map/sheet/pallas_call | solution.py:342
  2.1 12.9 %collective-permute-start.1 = (f32[32,512]{1,0:T(8,128)}, f32[32,512]{1,0:T(8,128)S(1)}, u32[]{:S(2)}, u32[]{:S(2)}) collective-permute-start(f32[32,512]{1,0:T(8,128)} %sheet.1.own), channel_id=1, source_target_pairs={{1,2},{3,4},{5,6},{7,8},{9,10},{11,12},{13,14},{15,16},{17,18},{19... | collective-permute-start | bytes 196616 | tf_op jit(solution)/shard_map/ppermute | solution.py:366
  15.0 1.9 %collective-permute-start = (f32[32,512]{1,0:T(8,128)}, f32[32,512]{1,0:T(8,128)S(1)}, u32[]{:S(2)}, u32[]{:S(2)}) collective-permute-start(f32[32,512]{1,0:T(8,128)} %sheet.1.own), channel_id=1, source_target_pairs={{0,1},{1,0},{2,3},{3,2},{4,5},{5,4},{6,7},{7,6},{8,9},{9,8},{10,11... | collective-permute-start | bytes 196616 | tf_op jit(solution)/shard_map/ppermute | solution.py:367
  17.0 0.0 copy-done.1
  17.0 0.0 copy-start.2
  17.0 0.9 copy-done.2
  17.9 0.0 copy-start
  17.9 0.0 collective-permute-done.1.cross
  17.9 0.5 collective-permute-done.mate
  18.4 0.3 copy-done
  18.7 1.1 %gram.1 = f32[544,128]{1,0:T(8,128)} custom-call(f32[32,512]{1,0:T(8,128)S(1)} %copy-done, f32[32,512]{1,0:T(8,128)S(1)} %collective-permute-done.mate, f32[32,512]{1,0:T(8,128)S(1)} %collective-permute-done.1.cross, f32[544,128]{1,0:T(8,128)S(1)} %pack.1.packed_in), custom_call_target="tpu_custom_call" | custom-call | tf_op jit(solution)/shard_map/gram/pallas_call | solution.py:342
  19.9 5.9 %all-to-all-start = ((f32[32,17,1,128]{3,2,1,0:T(1,128)}), f32[32,17,1,128]{3,2,1,0:T(1,128)S(1)}, u32[]{:S(2)}, u32[]{:S(2)}) async-start(f32[32,17,1,128]{3,2,1,0:T(1,128)} %bitcast.2), calls=%async_computation | async-start | bytes 557056 | tf_op jit(solution)/shard_map/all_to_all | solution.py:374
  25.8 1.2 %deposit.1 = (f32[16,16,128]{2,1,0:T(8,128)S(1)}, f32[8,512]{1,0:T(8,128)S(1)}, f32[8,512]{1,0:T(8,128)S(1)}, f32[8,512]{1,0:T(8,128)S(1)}) custom-call(f32[32,512]{1,0:T(8,128)S(1)} %copy-done, f32[32,512]{1,0:T(8,128)S(1)} %collective-permute-done.mate, f32[32,512]{1,0:T(8,128)S(1)} %collective-permute-done.1.cross), custom_call_target="tpu_custom_call" | custom-call | flops 100000000 | bytes 2000000 | tf_op jit(solution)/shard_map/deposit/pallas_call | solution.py:342
  27.0 22.2 %all-to-all-done = f32[32,17,1,128]{3,2,1,0:T(1,128)S(1)} async-done(((f32[32,17,1,128]{3,2,1,0:T(1,128)}), f32[32,17,1,128]{3,2,1,0:T(1,128)S(1)}, u32[]{:S(2)}, u32[]{:S(2)}) %all-to-all-start) | async-done | bytes 278560 | tf_op jit(solution)/shard_map/all_to_all | solution.py:374
  49.2 0.8 share.1
  50.0 7.4 %all-to-all-start.1 = ((f32[16,32,128]{2,1,0:T(8,128)}), f32[16,32,128]{2,1,0:T(8,128)S(1)}, u32[]{:S(2)}, u32[]{:S(2)}) async-start(f32[16,32,128]{2,1,0:T(8,128)} %bitcast.4), calls=%async_computation.1 | async-start | bytes 524288 | tf_op jit(solution)/shard_map/all_to_all | solution.py:391
  57.4 1.9 %collective-permute-start.2 = (f32[256,128]{1,0:T(8,128)S(1)}, f32[256,128]{1,0:T(8,128)S(1)}, u32[]{:S(2)}, u32[]{:S(2)}) collective-permute-start(f32[256,128]{1,0:T(8,128)S(1)} %get-tuple-element.23), channel_id=1, source_target_pairs={{1,0},{2,1},{3,2},{4,3},{5,4},{6,5},{7,6},{8,7},{9,8},{10,9},{11,1... | collective-permute-start | bytes 393224 | tf_op jit(solution)/shard_map/ppermute | solution.py:400
  59.3 2.4 %collective-permute-start.3 = (f32[256,128]{1,0:T(8,128)S(1)}, f32[256,128]{1,0:T(8,128)S(1)}, u32[]{:S(2)}, u32[]{:S(2)}) collective-permute-start(f32[256,128]{1,0:T(8,128)S(1)} %get-tuple-element.24), channel_id=1, source_target_pairs={{0,1},{1,2},{2,3},{3,4},{4,5},{5,6},{6,7},{7,8},{8,9},{9,10},{10,1... | collective-permute-start | bytes 393224 | tf_op jit(solution)/shard_map/ppermute | solution.py:401
  61.7 0.1 collective-permute-done.2.after
  61.8 8.0 %collective-permute-done.3.before = f32[256,128]{1,0:T(8,128)S(1)} collective-permute-done((f32[256,128]{1,0:T(8,128)S(1)}, f32[256,128]{1,0:T(8,128)S(1)}, u32[]{:S(2)}, u32[]{:S(2)}) %collective-permute-start.3) | collective-permute-done | bytes 131104 | tf_op jit(solution)/shard_map/ppermute | solution.py:401
  69.8 0.4 first.1
  70.2 0.0 all-to-all-done.1
  70.2 1.6 %heat.1 = (f32[8,512]{1,0:T(8,128)}, f32[256,128]{1,0:T(8,128)S(1)}) custom-call(f32[512,128]{1,0:T(8,128)S(1)} %bitcast.10, f32[8,512]{1,0:T(8,128)S(1)} %get-tuple-element.19.w0, f32[8,512]{1,0:T(8,128)S(1)} %get-tuple-element.20.w1, f32[8,512]{1,0:T(8,128)S(1)} %get-tuple-element.21.w2, f32[16,16,128]{2,1,0:T(8,128)S(1)} %get-tuple-element.22.bins, ...), custom_call_target="tpu_custom_call" | custom-call | tf_op jit(solution)/shard_map/heat/pallas_call | solution.py:342
  71.9 20.2 %all_to_all.15 = f32[32,8,128]{2,1,0:T(8,128)S(1)} all-to-all(f32[32,8,128]{2,1,0:T(8,128)S(1)} %bitcast.11), channel_id=1, replica_groups=mesh['magnet'=16,'slab'=32] {'slab'}, dimensions={0} | all-to-all | bytes 262144 | tf_op jit(solution)/shard_map/all_to_all | solution.py:415
  92.0 0.7 copy.10
  (1 shorter events, 0.0 us)
Async XLA Ops:
  0.6 16.3 %copy-start.1 = (f32[1,256,128]{2,1,0:T(8,128)S(1)}, f32[1,256,128]{2,1,0:T(8,128)}, u32[]{:S(2)}) copy-start(f32[1,256,128]{2,1,0:T(8,128)} %param.10) | copy-start | bytes 393220
  2.1 15.8 %collective-permute-start.1 = (f32[32,512]{1,0:T(8,128)}, f32[32,512]{1,0:T(8,128)S(1)}, u32[]{:S(2)}, u32[]{:S(2)}) collective-permute-start(f32[32,512]{1,0:T(8,128)} %sheet.1.own), channel_id=1, source_target_pairs={{1,2},{3,4},{5,6},{7,8},{9,10},{11,12},{13,14},{15,16},{17,18},{19... | collective-permute-start | bytes 196616 | tf_op jit(solution)/shard_map/ppermute | solution.py:366
  15.0 3.4 %collective-permute-start = (f32[32,512]{1,0:T(8,128)}, f32[32,512]{1,0:T(8,128)S(1)}, u32[]{:S(2)}, u32[]{:S(2)}) collective-permute-start(f32[32,512]{1,0:T(8,128)} %sheet.1.own), channel_id=1, source_target_pairs={{0,1},{1,0},{2,3},{3,2},{4,5},{5,4},{6,7},{7,6},{8,9},{9,8},{10,11... | collective-permute-start | bytes 196616 | tf_op jit(solution)/shard_map/ppermute | solution.py:367
  17.0 0.9 copy-start.2
  17.9 0.8 copy-start
  19.9 29.3 %all-to-all-start = ((f32[32,17,1,128]{3,2,1,0:T(1,128)}), f32[32,17,1,128]{3,2,1,0:T(1,128)S(1)}, u32[]{:S(2)}, u32[]{:S(2)}) async-start(f32[32,17,1,128]{3,2,1,0:T(1,128)} %bitcast.2), calls=%async_computation | async-start | bytes 557056 | tf_op jit(solution)/shard_map/all_to_all | solution.py:374
  50.0 20.3 %all-to-all-start.1 = ((f32[16,32,128]{2,1,0:T(8,128)}), f32[16,32,128]{2,1,0:T(8,128)S(1)}, u32[]{:S(2)}, u32[]{:S(2)}) async-start(f32[16,32,128]{2,1,0:T(8,128)} %bitcast.4), calls=%async_computation.1 | async-start | bytes 524288 | tf_op jit(solution)/shard_map/all_to_all | solution.py:391
  57.4 4.4 %collective-permute-start.2 = (f32[256,128]{1,0:T(8,128)S(1)}, f32[256,128]{1,0:T(8,128)S(1)}, u32[]{:S(2)}, u32[]{:S(2)}) collective-permute-start(f32[256,128]{1,0:T(8,128)S(1)} %get-tuple-element.23), channel_id=1, source_target_pairs={{1,0},{2,1},{3,2},{4,3},{5,4},{6,5},{7,6},{8,7},{9,8},{10,9},{11,1... | collective-permute-start | bytes 393224 | tf_op jit(solution)/shard_map/ppermute | solution.py:400
  59.3 10.5 %collective-permute-start.3 = (f32[256,128]{1,0:T(8,128)S(1)}, f32[256,128]{1,0:T(8,128)S(1)}, u32[]{:S(2)}, u32[]{:S(2)}) collective-permute-start(f32[256,128]{1,0:T(8,128)S(1)} %get-tuple-element.24), channel_id=1, source_target_pairs={{0,1},{1,2},{2,3},{3,4},{4,5},{5,6},{6,7},{7,8},{8,9},{9,10},{10,1... | collective-permute-start | bytes 393224 | tf_op jit(solution)/shard_map/ppermute | solution.py:401

commit v12 on v8

--- a/solution.py
+++ b/solution.py
@@ -139,6 +139,7 @@
 
 def solve_small(lines):
     total = jnp.sum(lines, axis=0, keepdims=True)
+    total = total / total[:, 0:1]
     g00, g01, g02, g11, g12, g22, k22 = (total[:, i : i + 1] for i in range(7))
     gram = ((g00, g01, g02), (g01, g11, g12), (g02, g12, g22))
     k11, k12 = 0.5 * (g12 + g01), 0.5 * (g22 + g02)
@@ -252,7 +253,7 @@
         field[EDGE + layers : 2 * EDGE + layers] = blank
 
 
-def share_kernel(layers, own, lines, for_cross, for_mate):
+def share_kernel(layers, own, lines, for_cross):
     mine = own[pl.ds(2 * ROWS, layers, stride=BLOCK), :]
     for magnet in range(lines.shape[0] // layers):
         lines[layers * magnet : layers * (magnet + 1)] = mine
@@ -265,7 +266,6 @@
 
         early, late = rows_from(0), rows_from(ROWS - HALO)
         part = slice(2 * HALO * layer, 2 * HALO * (layer + 1))
-        for_mate[part] = jnp.where(even, late, early)
         for_cross[part] = jnp.where(even, early, late)
 
 
@@ -278,8 +278,9 @@
         def rows_of(array):
             if HALO <= row < HALO + ROWS:
                 return own[pl.ds(ROWS * array + row - HALO, layers, stride=block), :]
-            at = HALO * array + row % HALO
-            return sides(index, *(ref[pl.ds(at, layers, stride=2 * HALO), :] for ref in (mate, cross)))[int(row >= HALO)]
+            near = mate[pl.ds(ROWS * array + (row + ROWS - HALO) % ROWS, layers, stride=block), :]
+            far = cross[pl.ds(HALO * array + row % HALO, layers, stride=2 * HALO), :]
+            return sides(index, near, far)[int(row >= HALO)]
 
         there = 1.0
         if row < HALO:
@@ -390,10 +391,10 @@
         cost=pl.CostEstimate(flops=10**8, bytes_accessed=2 * 10**6, transcendentals=0),
     )
     bricks, bins = lax.optimization_barrier((bricks.reshape(stack), bins))
-    lines, over, beside = call(
+    lines, over = call(
         functools.partial(share_kernel, layers),
         "share",
-        [(magnets * layers, spokes)] + [(2 * HALO * layers, spokes)] * 2,
+        [(magnets * layers, spokes)] + [(2 * HALO * layers, spokes)],
         bricks,
     )
     lines = lax.all_to_all(lines.reshape(magnets, layers, spokes), "magnet", 0, 0).reshape(count, spokes)
@@ -405,7 +406,7 @@
         "first",
         [padded, plain, plain],
         bricks,
-        *exchange(beside, over)[::-1],
+        *exchange(bricks, over)[::-1],
         scratch=[pltpu.VMEM(padded, f32), pltpu.VMEM(padded, f32)],
         cost=pl.CostEstimate(flops=0, bytes_accessed=0, transcendentals=0),
     )

time: 91.3 us -> 93.5 us (1.024)
  waiting for transfers between devices: 29.2 us -> 31.3 us
    ppermute x2, waiting for transfers between devices: 6.54 us -> 8.58 us  [exchange(): over = lax.ppermute(for_cross, BOTH, crossing)]
  transfers between devices with their start and end apart: 6 -> 6, of which waited for: 3 -> 3; matrix products, arithmetic and copies ran while one was open for 0% -> 0% of each run, Pallas kernels for 2% -> 3%
where the time goes in v12:
time: 93.5 us; the launch traced here: 92.9 us
  starting transfers between devices  31.9 us (34%)
  waiting for transfers between devices  31.3 us (33%)
  blocking collectives  20.2 us (22%)
  Pallas kernels  6.98 us (7%)
  local copies, waits for them, and re-layouts  1.89 us (2%)
    all_to_all x1, waiting for transfers between devices, local(): lax.all_to_all(packed.reshape(layers, BLOCK, 1, spokes), 'slab', 0, 0)  22.2 us
    all_to_all x1, blocking collectives, local(): heated = lax.all_to_all(heated.reshape(layers, ROWS, spokes), 'slab', 0, 0)  20.2 us
    ppermute x2, starting transfers between devices, exchange(): over = lax.ppermute(for_cross, BOTH, crossing)  14.8 us
    ppermute x2, waiting for transfers between devices, exchange(): over = lax.ppermute(for_cross, BOTH, crossing)  8.58 us
    all_to_all x1, starting transfers between devices, local(): lax.all_to_all(lines.reshape(magnets, layers, spokes), 'magnet', 0, 0)  7.39 us
    pallas_call x7, Pallas kernels, call(): pl.pallas_call(kernel, out_shape=tuple((jax.ShapeDtypeStruct(dims, f32) f...  6.98 us
    all_to_all x1, starting transfers between devices, local(): lax.all_to_all(packed.reshape(layers, BLOCK, 1, spokes), 'slab', 0, 0)  5.88 us
    ppermute x2, starting transfers between devices, exchange(): return (lax.ppermute(for_mate, BOTH, mates), over)  3.83 us
  transfers between devices with their start and end apart: 6, of which 3 were waited for; matrix products, arithmetic and copies ran while one was open for 0% of the time, Pallas kernels for 3%

profile of v12, /device:TPU:8, one launch (start us, length us, event | category | flops | bytes accessed | tf_op | source)
XLA Modules:
  0.0 92.9 jit_solution(15502394592260188717)
XLA Ops:
  0.6 0.0 copy-start.1
  0.6 1.5 %sheet.1.own = f32[32,512]{1,0:T(8,128)} custom-call(f32[8,512]{1,0:T(8,128)} %warmth.1, f32[8,512]{1,0:T(8,128)} %voltage.1, s32[8,512]{1,0:T(8,128)} %pattern.1, s32[256,512]{1,0:T(8,128)} %cells.1), custom_call_target="tpu_custom_call" | custom-call | tf_op jit(solution)/shard_map/sheet/pallas_call | solution.py:352
  2.1 12.9 %collective-permute-start.1 = (f32[32,512]{1,0:T(8,128)}, f32[32,512]{1,0:T(8,128)S(1)}, u32[]{:S(2)}, u32[]{:S(2)}) collective-permute-start(f32[32,512]{1,0:T(8,128)} %sheet.1.own), channel_id=1, source_target_pairs={{1,2},{3,4},{5,6},{7,8},{9,10},{11,12},{13,14},{15,16},{17,18},{19... | collective-permute-start | bytes 196616 | tf_op jit(solution)/shard_map/ppermute | solution.py:348
  15.0 1.9 %collective-permute-start = (f32[32,512]{1,0:T(8,128)}, f32[32,512]{1,0:T(8,128)S(1)}, u32[]{:S(2)}, u32[]{:S(2)}) collective-permute-start(f32[32,512]{1,0:T(8,128)} %sheet.1.own), channel_id=1, source_target_pairs={{0,1},{1,0},{2,3},{3,2},{4,5},{5,4},{6,7},{7,6},{8,9},{9,8},{10,11... | collective-permute-start | bytes 196616 | tf_op jit(solution)/shard_map/ppermute | solution.py:349
  17.0 0.0 copy-done.1
  17.0 0.0 copy-start.2
  17.0 0.9 copy-done.2
  17.9 0.0 copy-start
  17.9 0.0 collective-permute-done.1.cross
  17.9 0.5 collective-permute-done.mate
  18.4 0.3 copy-done
  18.7 1.1 %gram.1 = f32[544,128]{1,0:T(8,128)} custom-call(f32[32,512]{1,0:T(8,128)S(1)} %copy-done, f32[32,512]{1,0:T(8,128)S(1)} %collective-permute-done.mate, f32[32,512]{1,0:T(8,128)S(1)} %collective-permute-done.1.cross, f32[544,128]{1,0:T(8,128)S(1)} %pack.1.packed_in), custom_call_target="tpu_custom_call" | custom-call | tf_op jit(solution)/shard_map/gram/pallas_call | solution.py:352
  19.9 5.9 %all-to-all-start = ((f32[32,17,1,128]{3,2,1,0:T(1,128)}), f32[32,17,1,128]{3,2,1,0:T(1,128)S(1)}, u32[]{:S(2)}, u32[]{:S(2)}) async-start(f32[32,17,1,128]{3,2,1,0:T(1,128)} %bitcast.2), calls=%async_computation | async-start | bytes 557056 | tf_op jit(solution)/shard_map/all_to_all | solution.py:383
  25.8 1.2 %deposit.1 = (f32[16,16,128]{2,1,0:T(8,128)S(1)}, f32[8,512]{1,0:T(8,128)S(1)}, f32[8,512]{1,0:T(8,128)S(1)}, f32[8,512]{1,0:T(8,128)S(1)}) custom-call(f32[32,512]{1,0:T(8,128)S(1)} %copy-done, f32[32,512]{1,0:T(8,128)S(1)} %collective-permute-done.mate, f32[32,512]{1,0:T(8,128)S(1)} %collective-permute-done.1.cross), custom_call_target="tpu_custom_call" | custom-call | flops 100000000 | bytes 2000000 | tf_op jit(solution)/shard_map/deposit/pallas_call | solution.py:352
  27.0 22.2 %all-to-all-done = f32[32,17,1,128]{3,2,1,0:T(1,128)S(1)} async-done(((f32[32,17,1,128]{3,2,1,0:T(1,128)}), f32[32,17,1,128]{3,2,1,0:T(1,128)S(1)}, u32[]{:S(2)}, u32[]{:S(2)}) %all-to-all-start) | async-done | bytes 278560 | tf_op jit(solution)/shard_map/all_to_all | solution.py:383
  49.2 1.9 %collective-permute-start.3 = (f32[544,128]{1,0:T(8,128)S(1)}, f32[544,128]{1,0:T(8,128)S(1)}, u32[]{:S(2)}, u32[]{:S(2)}) collective-permute-start(f32[544,128]{1,0:T(8,128)S(1)} %bitcast.8), channel_id=1, source_target_pairs={{0,1},{1,0},{2,3},{3,2},{4,5},{5,4},{6,7},{7,6},{8,9},{9,8},{10,11... | collective-permute-start | bytes 835592 | tf_op jit(solution)/shard_map/ppermute | solution.py:349
  51.1 0.8 share.1
  51.9 7.4 %all-to-all-start.1 = ((f32[16,32,128]{2,1,0:T(8,128)}), f32[16,32,128]{2,1,0:T(8,128)S(1)}, u32[]{:S(2)}, u32[]{:S(2)}) async-start(f32[16,32,128]{2,1,0:T(8,128)} %bitcast.4), calls=%async_computation.1 | async-start | bytes 524288 | tf_op jit(solution)/shard_map/all_to_all | solution.py:400
  59.3 1.9 %collective-permute-start.2 = (f32[256,128]{1,0:T(8,128)S(1)}, f32[256,128]{1,0:T(8,128)S(1)}, u32[]{:S(2)}, u32[]{:S(2)}) collective-permute-start(f32[256,128]{1,0:T(8,128)S(1)} %get-tuple-element.22), channel_id=1, source_target_pairs={{1,2},{3,4},{5,6},{7,8},{9,10},{11,12},{13,14},{15,16},{17,18},{19... | collective-permute-start | bytes 393224 | tf_op jit(solution)/shard_map/ppermute | solution.py:348
  61.2 8.6 %collective-permute-done.2.cross = f32[256,128]{1,0:T(8,128)S(1)} collective-permute-done((f32[256,128]{1,0:T(8,128)S(1)}, f32[256,128]{1,0:T(8,128)S(1)}, u32[]{:S(2)}, u32[]{:S(2)}) %collective-permute-start.2) | collective-permute-done | bytes 131104 | tf_op jit(solution)/shard_map/ppermute | solution.py:348
  69.8 0.0 collective-permute-done.3.mate
  69.8 0.4 first.1
  70.2 0.0 all-to-all-done.1
  70.2 1.9 %heat.1 = (f32[8,512]{1,0:T(8,128)}, f32[256,128]{1,0:T(8,128)S(1)}) custom-call(f32[512,128]{1,0:T(8,128)S(1)} %bitcast.11, f32[8,512]{1,0:T(8,128)S(1)} %get-tuple-element.18.w0, f32[8,512]{1,0:T(8,128)S(1)} %get-tuple-element.19.w1, f32[8,512]{1,0:T(8,128)S(1)} %get-tuple-element.20.w2, f32[16,16,128]{2,1,0:T(8,128)S(1)} %get-tuple-element.21.bins, ...), custom_call_target="tpu_custom_call" | custom-call | tf_op jit(solution)/shard_map/heat/pallas_call | solution.py:352
  72.1 20.2 %all_to_all.15 = f32[32,8,128]{2,1,0:T(8,128)S(1)} all-to-all(f32[32,8,128]{2,1,0:T(8,128)S(1)} %bitcast.12), channel_id=1, replica_groups=mesh['magnet'=16,'slab'=32] {'slab'}, dimensions={0} | all-to-all | bytes 262144 | tf_op jit(solution)/shard_map/all_to_all | solution.py:423
  92.3 0.7 copy.10
  (1 shorter events, 0.0 us)
Async XLA Ops:
  0.6 16.3 %copy-start.1 = (f32[1,256,128]{2,1,0:T(8,128)S(1)}, f32[1,256,128]{2,1,0:T(8,128)}, u32[]{:S(2)}) copy-start(f32[1,256,128]{2,1,0:T(8,128)} %param.10) | copy-start | bytes 393220
  2.1 15.8 %collective-permute-start.1 = (f32[32,512]{1,0:T(8,128)}, f32[32,512]{1,0:T(8,128)S(1)}, u32[]{:S(2)}, u32[]{:S(2)}) collective-permute-start(f32[32,512]{1,0:T(8,128)} %sheet.1.own), channel_id=1, source_target_pairs={{1,2},{3,4},{5,6},{7,8},{9,10},{11,12},{13,14},{15,16},{17,18},{19... | collective-permute-start | bytes 196616 | tf_op jit(solution)/shard_map/ppermute | solution.py:348
  15.0 3.4 %collective-permute-start = (f32[32,512]{1,0:T(8,128)}, f32[32,512]{1,0:T(8,128)S(1)}, u32[]{:S(2)}, u32[]{:S(2)}) collective-permute-start(f32[32,512]{1,0:T(8,128)} %sheet.1.own), channel_id=1, source_target_pairs={{0,1},{1,0},{2,3},{3,2},{4,5},{5,4},{6,7},{7,6},{8,9},{9,8},{10,11... | collective-permute-start | bytes 196616 | tf_op jit(solution)/shard_map/ppermute | solution.py:349
  17.0 0.9 copy-start.2
  17.9 0.8 copy-start
  19.9 29.3 %all-to-all-start = ((f32[32,17,1,128]{3,2,1,0:T(1,128)}), f32[32,17,1,128]{3,2,1,0:T(1,128)S(1)}, u32[]{:S(2)}, u32[]{:S(2)}) async-start(f32[32,17,1,128]{3,2,1,0:T(1,128)} %bitcast.2), calls=%async_computation | async-start | bytes 557056 | tf_op jit(solution)/shard_map/all_to_all | solution.py:383
  49.2 20.6 %collective-permute-start.3 = (f32[544,128]{1,0:T(8,128)S(1)}, f32[544,128]{1,0:T(8,128)S(1)}, u32[]{:S(2)}, u32[]{:S(2)}) collective-permute-start(f32[544,128]{1,0:T(8,128)S(1)} %bitcast.8), channel_id=1, source_target_pairs={{0,1},{1,0},{2,3},{3,2},{4,5},{5,4},{6,7},{7,6},{8,9},{9,8},{10,11... | collective-permute-start | bytes 835592 | tf_op jit(solution)/shard_map/ppermute | solution.py:349
  51.9 18.3 %all-to-all-start.1 = ((f32[16,32,128]{2,1,0:T(8,128)}), f32[16,32,128]{2,1,0:T(8,128)S(1)}, u32[]{:S(2)}, u32[]{:S(2)}) async-start(f32[16,32,128]{2,1,0:T(8,128)} %bitcast.4), calls=%async_computation.1 | async-start | bytes 524288 | tf_op jit(solution)/shard_map/all_to_all | solution.py:400
  59.3 10.5 %collective-permute-start.2 = (f32[256,128]{1,0:T(8,128)S(1)}, f32[256,128]{1,0:T(8,128)S(1)}, u32[]{:S(2)}, u32[]{:S(2)}) collective-permute-start(f32[256,128]{1,0:T(8,128)S(1)} %get-tuple-element.22), channel_id=1, source_target_pairs={{1,2},{3,4},{5,6},{7,8},{9,10},{11,12},{13,14},{15,16},{17,18},{19... | collective-permute-start | bytes 393224 | tf_op jit(solution)/shard_map/ppermute | solution.py:348

commit v13 on v8

--- a/solution.py
+++ b/solution.py
@@ -25,6 +25,7 @@
 SCALE = 9.6
 BOTH = ("magnet", "slab")
 BLOCK = 2 * ROWS + 1
+COPIES = 24
 
 
 def place():
@@ -124,7 +125,7 @@
     return (w0, w1, w2), apply, inside, (c_down, c_right, c_left)
 
 
-def gram_kernel(own, mate, cross, packed_in, packed):
+def gram_kernel(own, cross, mate, packed_in, packed):
     (w0, w1, w2), apply, _, _ = basis(own, mate, cross)
     w0, w1, w2, w3 = (w[ROWS : 2 * ROWS] for w in (w0, w1, w2, apply(w2)))
     lane = lax.broadcasted_iota(jnp.int32, (1, 128), 1)
@@ -254,8 +255,7 @@
 
 def share_kernel(layers, own, lines, for_cross, for_mate):
     mine = own[pl.ds(2 * ROWS, layers, stride=BLOCK), :]
-    for magnet in range(lines.shape[0] // layers):
-        lines[layers * magnet : layers * (magnet + 1)] = mine
+    lines[...] = jnp.broadcast_to(jnp.sum(mine, axis=0, keepdims=True), lines.shape)
     even = place()[0] % 2 == 0
     for layer in range(layers):
         at = BLOCK * layer
@@ -305,7 +305,7 @@
 def heat_kernel(layers, lines, w0, w1, w2, bins, fresh, base, store, potential, heated, warm, cond):
     spokes = heated.shape[-1]
     body = slice(EDGE, EDGE + layers)
-    f = solve_small(lines[...])
+    f = solve_small(lines[pl.ds(0, lines.shape[0] // COPIES, stride=COPIES), :])
     potential[...] = f[0] * w0[...] + f[1] * w1[...] + f[2] * w2[...]
     sublane = lax.broadcasted_iota(jnp.int32, (8, spokes), 0)
     weight = jnp.zeros((8, spokes), jnp.float32)
@@ -377,7 +377,7 @@
     (packed,) = call(
         pack_kernel, "pack", [stack], prior_block_warmth.reshape(-1, spokes), substance_kind.reshape(-1, spokes)
     )
-    (packed,) = call(gram_kernel, "gram", [stack], sheet, *around, packed)
+    (packed,) = call(gram_kernel, "gram", [stack], sheet, *around[::-1], packed)
 
     bricks = lax.all_to_all(packed.reshape(layers, BLOCK, 1, spokes), "slab", 0, 0)
     bins, *fields = call(
@@ -393,10 +393,10 @@
     lines, over, beside = call(
         functools.partial(share_kernel, layers),
         "share",
-        [(magnets * layers, spokes)] + [(2 * HALO * layers, spokes)] * 2,
+        [(magnets * COPIES, spokes)] + [(2 * HALO * layers, spokes)] * 2,
         bricks,
     )
-    lines = lax.all_to_all(lines.reshape(magnets, layers, spokes), "magnet", 0, 0).reshape(count, spokes)
+    lines = lax.all_to_all(lines.reshape(magnets, COPIES, spokes), "magnet", 0, 0).reshape(magnets * COPIES, spokes)
 
     padded = (SPAN, layers + 2 * EDGE, spokes)
     plain = (SPAN, layers, spokes)

time: 91.3 us -> 93.1 us (1.020)
  starting transfers between devices: 32.1 us -> 33.5 us
    ppermute x2, waiting for transfers between devices: 6.54 us -> 7.78 us  [exchange(): over = lax.ppermute(for_cross, BOTH, crossing)]
where the time goes in v13:
time: 93.1 us; the launch traced here: 92.6 us
  starting transfers between devices  33.5 us (36%)
  waiting for transfers between devices  30 us (32%)
  blocking collectives  20.2 us (22%)
  Pallas kernels  6.64 us (7%)
  local copies, waits for them, and re-layouts  1.56 us (2%)
    all_to_all x1, waiting for transfers between devices, local(): lax.all_to_all(packed.reshape(layers, BLOCK, 1, spokes), 'slab', 0, 0)  22.2 us
    all_to_all x1, blocking collectives, local(): heated = lax.all_to_all(heated.reshape(layers, ROWS, spokes), 'slab', 0, 0)  20.2 us
    ppermute x2, starting transfers between devices, exchange(): over = lax.ppermute(for_cross, BOTH, crossing)  15.5 us
    ppermute x2, waiting for transfers between devices, exchange(): over = lax.ppermute(for_cross, BOTH, crossing)  7.78 us
    all_to_all x1, starting transfers between devices, local(): lax.all_to_all(lines.reshape(magnets, COPIES, spokes), 'magnet', 0, 0)  7.39 us
    all_to_all x1, starting transfers between devices, local(): lax.all_to_all(packed.reshape(layers, BLOCK, 1, spokes), 'slab', 0, 0)  6.69 us
    pallas_call x7, Pallas kernels, call(): pl.pallas_call(kernel, out_shape=tuple((jax.ShapeDtypeStruct(dims, f32) f...  6.64 us
    ppermute x2, starting transfers between devices, exchange(): return (lax.ppermute(for_mate, BOTH, mates), over)  3.95 us
  transfers between devices with their start and end apart: 6, of which 3 were waited for; matrix products, arithmetic and copies ran while one was open for 0% of the time, Pallas kernels for 2%

profile of v13, /device:TPU:8, one launch (start us, length us, event | category | flops | bytes accessed | tf_op | source)
XLA Modules:
  0.0 92.6 jit_solution(17347645179870984039)
XLA Ops:
  0.6 0.0 copy-start.1
  0.6 1.5 %sheet.1.own = f32[32,512]{1,0:T(8,128)} custom-call(f32[8,512]{1,0:T(8,128)} %warmth.1, f32[8,512]{1,0:T(8,128)} %voltage.1, s32[8,512]{1,0:T(8,128)} %pattern.1, s32[256,512]{1,0:T(8,128)} %cells.1), custom_call_target="tpu_custom_call" | custom-call | tf_op jit(solution)/shard_map/sheet/pallas_call | solution.py:351
  2.1 1.9 %collective-permute-start.1 = (f32[32,512]{1,0:T(8,128)}, f32[32,512]{1,0:T(8,128)S(1)}, u32[]{:S(2)}, u32[]{:S(2)}) collective-permute-start(f32[32,512]{1,0:T(8,128)} %sheet.1.own), channel_id=1, source_target_pairs={{0,1},{1,0},{2,3},{3,2},{4,5},{5,4},{6,7},{7,6},{8,9},{9,8},{10,11... | collective-permute-start | bytes 196616 | tf_op jit(solution)/shard_map/ppermute | solution.py:348
  4.0 13.6 %collective-permute-start = (f32[32,512]{1,0:T(8,128)}, f32[32,512]{1,0:T(8,128)S(1)}, u32[]{:S(2)}, u32[]{:S(2)}) collective-permute-start(f32[32,512]{1,0:T(8,128)} %sheet.1.own), channel_id=1, source_target_pairs={{1,2},{3,4},{5,6},{7,8},{9,10},{11,12},{13,14},{15,16},{17,18},{19... | collective-permute-start | bytes 196616 | tf_op jit(solution)/shard_map/ppermute | solution.py:347
  17.6 0.0 copy-done.1
  17.6 0.0 copy-start.2
  17.7 0.9 copy-done.2
  18.6 0.0 copy-start
  18.6 0.0 collective-permute-done.1.mate
  18.6 1.2 %collective-permute-done.cross = f32[32,512]{1,0:T(8,128)S(1)} collective-permute-done((f32[32,512]{1,0:T(8,128)}, f32[32,512]{1,0:T(8,128)S(1)}, u32[]{:S(2)}, u32[]{:S(2)}) %collective-permute-start) | collective-permute-done | bytes 65568 | tf_op jit(solution)/shard_map/ppermute | solution.py:347
  19.8 0.0 copy-done
  19.8 1.2 %gram.1 = f32[544,128]{1,0:T(8,128)} custom-call(f32[32,512]{1,0:T(8,128)S(1)} %copy-done, f32[32,512]{1,0:T(8,128)S(1)} %collective-permute-done.cross, f32[32,512]{1,0:T(8,128)S(1)} %collective-permute-done.1.mate, f32[544,128]{1,0:T(8,128)S(1)} %pack.1.packed_in), custom_call_target="tpu_custom_call" | custom-call | tf_op jit(solution)/shard_map/gram/pallas_call | solution.py:351
  21.0 6.7 %all-to-all-start = ((f32[32,17,1,128]{3,2,1,0:T(1,128)}), f32[32,17,1,128]{3,2,1,0:T(1,128)S(1)}, u32[]{:S(2)}, u32[]{:S(2)}) async-start(f32[32,17,1,128]{3,2,1,0:T(1,128)} %bitcast.2), calls=%async_computation | async-start | bytes 557056 | tf_op jit(solution)/shard_map/all_to_all | solution.py:382
  27.7 1.2 %deposit.1 = (f32[16,16,128]{2,1,0:T(8,128)S(1)}, f32[8,512]{1,0:T(8,128)S(1)}, f32[8,512]{1,0:T(8,128)S(1)}, f32[8,512]{1,0:T(8,128)S(1)}) custom-call(f32[32,512]{1,0:T(8,128)S(1)} %copy-done, f32[32,512]{1,0:T(8,128)S(1)} %collective-permute-done.1.mate, f32[32,512]{1,0:T(8,128)S(1)} %collective-permute-done.cross), custom_call_target="tpu_custom_call" | custom-call | flops 100000000 | bytes 2000000 | tf_op jit(solution)/shard_map/deposit/pallas_call | solution.py:351
  28.9 22.2 %all-to-all-done = f32[32,17,1,128]{3,2,1,0:T(1,128)S(1)} async-done(((f32[32,17,1,128]{3,2,1,0:T(1,128)}), f32[32,17,1,128]{3,2,1,0:T(1,128)S(1)}, u32[]{:S(2)}, u32[]{:S(2)}) %all-to-all-start) | async-done | bytes 278560 | tf_op jit(solution)/shard_map/all_to_all | solution.py:382
  51.1 0.7 share.1
  51.9 7.4 %all-to-all-start.1 = ((f32[16,24,128]{2,1,0:T(8,128)}), f32[16,24,128]{2,1,0:T(8,128)S(1)}, u32[]{:S(2)}, u32[]{:S(2)}) async-start(f32[16,24,128]{2,1,0:T(8,128)} %bitcast.4), calls=%async_computation.1 | async-start | bytes 393216 | tf_op jit(solution)/shard_map/all_to_all | solution.py:399
  59.3 1.9 %collective-permute-start.2 = (f32[256,128]{1,0:T(8,128)S(1)}, f32[256,128]{1,0:T(8,128)S(1)}, u32[]{:S(2)}, u32[]{:S(2)}) collective-permute-start(f32[256,128]{1,0:T(8,128)S(1)} %get-tuple-element.23), channel_id=1, source_target_pairs={{1,2},{3,4},{5,6},{7,8},{9,10},{11,12},{13,14},{15,16},{17,18},{19... | collective-permute-start | bytes 393224 | tf_op jit(solution)/shard_map/ppermute | solution.py:347
  61.2 2.0 %collective-permute-start.3 = (f32[256,128]{1,0:T(8,128)S(1)}, f32[256,128]{1,0:T(8,128)S(1)}, u32[]{:S(2)}, u32[]{:S(2)}) collective-permute-start(f32[256,128]{1,0:T(8,128)S(1)} %get-tuple-element.24), channel_id=1, source_target_pairs={{0,1},{1,0},{2,3},{3,2},{4,5},{5,4},{6,7},{7,6},{8,9},{9,8},{10,11... | collective-permute-start | bytes 393224 | tf_op jit(solution)/shard_map/ppermute | solution.py:348
  63.2 6.5 %collective-permute-done.2.cross = f32[256,128]{1,0:T(8,128)S(1)} collective-permute-done((f32[256,128]{1,0:T(8,128)S(1)}, f32[256,128]{1,0:T(8,128)S(1)}, u32[]{:S(2)}, u32[]{:S(2)}) %collective-permute-start.2) | collective-permute-done | bytes 131104 | tf_op jit(solution)/shard_map/ppermute | solution.py:347
  69.8 0.0 collective-permute-done.3.mate
  69.8 0.5 first.1
  70.2 0.0 all-to-all-done.1
  70.2 1.6 %heat.1 = (f32[8,512]{1,0:T(8,128)}, f32[256,128]{1,0:T(8,128)S(1)}) custom-call(f32[384,128]{1,0:T(8,128)S(1)} %bitcast.10, f32[8,512]{1,0:T(8,128)S(1)} %get-tuple-element.19.w0, f32[8,512]{1,0:T(8,128)S(1)} %get-tuple-element.20.w1, f32[8,512]{1,0:T(8,128)S(1)} %get-tuple-element.21.w2, f32[16,16,128]{2,1,0:T(8,128)S(1)} %get-tuple-element.22.bins, ...), custom_call_target="tpu_custom_call" | custom-call | tf_op jit(solution)/shard_map/heat/pallas_call | solution.py:351
  71.8 20.2 %all_to_all.15 = f32[32,8,128]{2,1,0:T(8,128)S(1)} all-to-all(f32[32,8,128]{2,1,0:T(8,128)S(1)} %bitcast.11), channel_id=1, replica_groups=mesh['magnet'=16,'slab'=32] {'slab'}, dimensions={0} | all-to-all | bytes 262144 | tf_op jit(solution)/shard_map/all_to_all | solution.py:422
  91.9 0.7 copy.10
  (1 shorter events, 0.0 us)
Async XLA Ops:
  0.6 17.0 %copy-start.1 = (f32[1,256,128]{2,1,0:T(8,128)S(1)}, f32[1,256,128]{2,1,0:T(8,128)}, u32[]{:S(2)}) copy-start(f32[1,256,128]{2,1,0:T(8,128)} %param.10) | copy-start | bytes 393220
  2.1 16.5 %collective-permute-start.1 = (f32[32,512]{1,0:T(8,128)}, f32[32,512]{1,0:T(8,128)S(1)}, u32[]{:S(2)}, u32[]{:S(2)}) collective-permute-start(f32[32,512]{1,0:T(8,128)} %sheet.1.own), channel_id=1, source_target_pairs={{0,1},{1,0},{2,3},{3,2},{4,5},{5,4},{6,7},{7,6},{8,9},{9,8},{10,11... | collective-permute-start | bytes 196616 | tf_op jit(solution)/shard_map/ppermute | solution.py:348
  4.0 15.8 %collective-permute-start = (f32[32,512]{1,0:T(8,128)}, f32[32,512]{1,0:T(8,128)S(1)}, u32[]{:S(2)}, u32[]{:S(2)}) collective-permute-start(f32[32,512]{1,0:T(8,128)} %sheet.1.own), channel_id=1, source_target_pairs={{1,2},{3,4},{5,6},{7,8},{9,10},{11,12},{13,14},{15,16},{17,18},{19... | collective-permute-start | bytes 196616 | tf_op jit(solution)/shard_map/ppermute | solution.py:347
  17.6 0.9 copy-start.2
  18.6 1.3 %copy-start = (f32[32,512]{1,0:T(8,128)S(1)}, f32[32,512]{1,0:T(8,128)}, u32[]{:S(2)}) copy-start(f32[32,512]{1,0:T(8,128)} %sheet.1.own) | copy-start | bytes 196612
  21.0 30.1 %all-to-all-start = ((f32[32,17,1,128]{3,2,1,0:T(1,128)}), f32[32,17,1,128]{3,2,1,0:T(1,128)S(1)}, u32[]{:S(2)}, u32[]{:S(2)}) async-start(f32[32,17,1,128]{3,2,1,0:T(1,128)} %bitcast.2), calls=%async_computation | async-start | bytes 557056 | tf_op jit(solution)/shard_map/all_to_all | solution.py:382
  51.9 18.4 %all-to-all-start.1 = ((f32[16,24,128]{2,1,0:T(8,128)}), f32[16,24,128]{2,1,0:T(8,128)S(1)}, u32[]{:S(2)}, u32[]{:S(2)}) async-start(f32[16,24,128]{2,1,0:T(8,128)} %bitcast.4), calls=%async_computation.1 | async-start | bytes 393216 | tf_op jit(solution)/shard_map/all_to_all | solution.py:399
  59.3 10.5 %collective-permute-start.2 = (f32[256,128]{1,0:T(8,128)S(1)}, f32[256,128]{1,0:T(8,128)S(1)}, u32[]{:S(2)}, u32[]{:S(2)}) collective-permute-start(f32[256,128]{1,0:T(8,128)S(1)} %get-tuple-element.23), channel_id=1, source_target_pairs={{1,2},{3,4},{5,6},{7,8},{9,10},{11,12},{13,14},{15,16},{17,18},{19... | collective-permute-start | bytes 393224 | tf_op jit(solution)/shard_map/ppermute | solution.py:347
  61.2 8.6 %collective-permute-start.3 = (f32[256,128]{1,0:T(8,128)S(1)}, f32[256,128]{1,0:T(8,128)S(1)}, u32[]{:S(2)}, u32[]{:S(2)}) collective-permute-start(f32[256,128]{1,0:T(8,128)S(1)} %get-tuple-element.24), channel_id=1, source_target_pairs={{0,1},{1,0},{2,3},{3,2},{4,5},{5,4},{6,7},{7,6},{8,9},{9,8},{10,11... | collective-permute-start | bytes 393224 | tf_op jit(solution)/shard_map/ppermute | solution.py:348

commit v14 on v9

--- a/solution.py
+++ b/solution.py
@@ -25,6 +25,7 @@
 SCALE = 9.6
 BOTH = ("magnet", "slab")
 BLOCK = 2 * ROWS + 1
+COPIES = 24
 
 
 def place():
@@ -254,8 +255,7 @@
 
 def share_kernel(layers, own, lines, for_cross, for_mate):
     mine = own[pl.ds(2 * ROWS, layers, stride=BLOCK), :]
-    for magnet in range(lines.shape[0] // layers):
-        lines[layers * magnet : layers * (magnet + 1)] = mine
+    lines[...] = jnp.broadcast_to(jnp.sum(mine, axis=0, keepdims=True), lines.shape)
     even = place()[0] % 2 == 0
     for layer in range(layers):
         at = BLOCK * layer
@@ -308,7 +308,7 @@
 def heat_kernel(layers, lines, w0, w1, w2, bins, fresh, base, store, potential, heated, warm, cond):
     spokes = heated.shape[-1]
     body = slice(EDGE, EDGE + layers)
-    f = solve_small(lines[...])
+    f = solve_small(lines[pl.ds(0, lines.shape[0] // COPIES, stride=COPIES), :])
     potential[...] = f[0] * w0[...] + f[1] * w1[...] + f[2] * w2[...]
     sublane = lax.broadcasted_iota(jnp.int32, (8, spokes), 0)
     weight = jnp.zeros((8, spokes), jnp.float32)
@@ -398,10 +398,10 @@
     lines, over, beside = call(
         functools.partial(share_kernel, layers),
         "share",
-        [(magnets * layers, spokes)] + [(2 * HALO * layers, spokes)] * 2,
+        [(magnets * COPIES, spokes)] + [(2 * HALO * layers, spokes)] * 2,
         bricks,
     )
-    lines = lax.all_to_all(lines.reshape(magnets, layers, spokes), "magnet", 0, 0).reshape(count, spokes)
+    lines = lax.all_to_all(lines.reshape(magnets, COPIES, spokes), "magnet", 0, 0).reshape(magnets * COPIES, spokes)
 
     padded = (SPAN, layers + 2 * EDGE, spokes)
     plain = (SPAN, layers, spokes)

time: 91.2 us -> 90.7 us (level)
  no operation moved by 1% of the time
where the time goes in v14:
time: 90.7 us; the launch traced here: 90.2 us
  starting transfers between devices  34.2 us (38%)
  waiting for transfers between devices  24.3 us (27%)
  blocking collectives  22 us (24%)
  Pallas kernels  6.63 us (7%)
  local copies, waits for them, and re-layouts  2.23 us (2%)
    all_to_all x1, blocking collectives, local(): heated = lax.all_to_all(heated.reshape(layers, ROWS, spokes), 'slab', 0, 0)  22 us
    all_to_all x1, waiting for transfers between devices, local(): lax.all_to_all(packed.reshape(layers, BLOCK, 1, spokes), 'slab', 0, 0)  21.7 us
    ppermute x5, starting transfers between devices, swap(): return lax.ppermute(array, BOTH, pairs + [(j, i) for i, j in pairs])  14.9 us
    all_to_all x1, starting transfers between devices, local(): lax.all_to_all(packed.reshape(layers, BLOCK, 1, spokes), 'slab', 0, 0)  12.5 us
    all_to_all x1, starting transfers between devices, local(): lax.all_to_all(lines.reshape(magnets, COPIES, spokes), 'magnet', 0, 0)  6.75 us
    pallas_call x7, Pallas kernels, call(): pl.pallas_call(kernel, out_shape=tuple((jax.ShapeDtypeStruct(dims, f32) f...  6.63 us
    unnamed x7, local copies, waits for them, and re-layouts  2.23 us
    ppermute x5, waiting for transfers between devices, swap(): return lax.ppermute(array, BOTH, pairs + [(j, i) for i, j in pairs])  1.89 us
  transfers between devices with their start and end apart: 7, of which 4 were waited for; matrix products, arithmetic and copies ran while one was open for 0% of the time, Pallas kernels for 3%

profile of v14, /device:TPU:1, one launch (start us, length us, event | category | flops | bytes accessed | tf_op | source)
XLA Modules:
  0.0 90.2 jit_solution(16673011876505855620)
XLA Ops:
  0.6 0.0 copy-start.1
  0.6 1.5 %sheet.1.own = f32[32,512]{1,0:T(8,128)} custom-call(f32[8,512]{1,0:T(8,128)} %warmth.1, f32[8,512]{1,0:T(8,128)} %voltage.1, s32[8,512]{1,0:T(8,128)} %pattern.1, s32[256,512]{1,0:T(8,128)} %cells.1), custom_call_target="tpu_custom_call" | custom-call | tf_op jit(solution)/shard_map/sheet/pallas_call | solution.py:355
  2.1 4.9 %collective-permute-start.1 = (f32[32,512]{1,0:T(8,128)}, f32[32,512]{1,0:T(8,128)S(1)}, u32[]{:S(2)}, u32[]{:S(2)}) collective-permute-start(f32[32,512]{1,0:T(8,128)} %sheet.1.own), channel_id=1, source_target_pairs={{1,2},{3,4},{5,6},{7,8},{9,10},{11,12},{13,14},{15,16},{17,18},{19... | collective-permute-start | bytes 196616 | tf_op jit(solution)/shard_map/ppermute | solution.py:352
  7.1 4.5 %collective-permute-start = (f32[32,512]{1,0:T(8,128)}, f32[32,512]{1,0:T(8,128)S(1)}, u32[]{:S(2)}, u32[]{:S(2)}) collective-permute-start(f32[32,512]{1,0:T(8,128)} %sheet.1.own), channel_id=1, source_target_pairs={{0,1},{2,3},{4,5},{6,7},{8,9},{10,11},{12,13},{14,15},{16,17},{18,... | collective-permute-start | bytes 196616 | tf_op jit(solution)/shard_map/ppermute | solution.py:352
  11.6 0.0 copy-done.1
  11.6 0.0 copy-start.2
  11.6 0.9 copy-done.2
  12.5 0.0 copy-start
  12.5 0.0 collective-permute-done.1.cross
  12.5 0.1 collective-permute-done.mate
  12.7 0.7 copy-done
  13.3 1.1 %gram.1 = f32[544,128]{1,0:T(8,128)} custom-call(f32[32,512]{1,0:T(8,128)S(1)} %copy-done, f32[32,512]{1,0:T(8,128)S(1)} %collective-permute-done.mate, f32[32,512]{1,0:T(8,128)S(1)} %collective-permute-done.1.cross, f32[544,128]{1,0:T(8,128)S(1)} %pack.1.packed_in), custom_call_target="tpu_custom_call" | custom-call | tf_op jit(solution)/shard_map/gram/pallas_call | solution.py:355
  14.5 12.5 %all-to-all-start = ((f32[32,17,1,128]{3,2,1,0:T(1,128)}), f32[32,17,1,128]{3,2,1,0:T(1,128)S(1)}, u32[]{:S(2)}, u32[]{:S(2)}) async-start(f32[32,17,1,128]{3,2,1,0:T(1,128)} %bitcast.2), calls=%async_computation | async-start | bytes 557056 | tf_op jit(solution)/shard_map/all_to_all | solution.py:387
  27.0 1.2 %deposit.1 = (f32[16,16,128]{2,1,0:T(8,128)S(1)}, f32[8,512]{1,0:T(8,128)S(1)}, f32[8,512]{1,0:T(8,128)S(1)}, f32[8,512]{1,0:T(8,128)S(1)}) custom-call(f32[32,512]{1,0:T(8,128)S(1)} %copy-done, f32[32,512]{1,0:T(8,128)S(1)} %collective-permute-done.mate, f32[32,512]{1,0:T(8,128)S(1)} %collective-permute-done.1.cross), custom_call_target="tpu_custom_call" | custom-call | flops 100000000 | bytes 2000000 | tf_op jit(solution)/shard_map/deposit/pallas_call | solution.py:355
  28.3 21.7 %all-to-all-done = f32[32,17,1,128]{3,2,1,0:T(1,128)S(1)} async-done(((f32[32,17,1,128]{3,2,1,0:T(1,128)}), f32[32,17,1,128]{3,2,1,0:T(1,128)S(1)}, u32[]{:S(2)}, u32[]{:S(2)}) %all-to-all-start) | async-done | bytes 278560 | tf_op jit(solution)/shard_map/all_to_all | solution.py:387
  50.0 0.7 collective-permute-start.2
  50.7 0.7 share.1
  51.4 6.8 %all-to-all-start.1 = ((f32[16,24,128]{2,1,0:T(8,128)}), f32[16,24,128]{2,1,0:T(8,128)S(1)}, u32[]{:S(2)}, u32[]{:S(2)}) async-start(f32[16,24,128]{2,1,0:T(8,128)} %bitcast.4), calls=%async_computation.1 | async-start | bytes 393216 | tf_op jit(solution)/shard_map/all_to_all | solution.py:404
  58.2 2.5 %collective-permute-start.3 = (f32[256,128]{1,0:T(8,128)S(1)}, f32[256,128]{1,0:T(8,128)S(1)}, u32[]{:S(2)}, u32[]{:S(2)}) collective-permute-start(f32[256,128]{1,0:T(8,128)S(1)} %get-tuple-element.23), channel_id=1, source_target_pairs={{1,2},{3,4},{5,6},{7,8},{9,10},{11,12},{13,14},{15,16},{17,18},{19... | collective-permute-start | bytes 393224 | tf_op jit(solution)/shard_map/ppermute | solution.py:352
  60.7 2.3 %collective-permute-start.4 = (f32[256,128]{1,0:T(8,128)S(1)}, f32[256,128]{1,0:T(8,128)S(1)}, u32[]{:S(2)}, u32[]{:S(2)}) collective-permute-start(f32[256,128]{1,0:T(8,128)S(1)} %get-tuple-element.24), channel_id=1, source_target_pairs={{0,1},{2,3},{4,5},{6,7},{8,9},{10,11},{12,13},{14,15},{16,17},{18,... | collective-permute-start | bytes 393224 | tf_op jit(solution)/shard_map/ppermute | solution.py:352
  63.0 1.8 %collective-permute-done.3.cross = f32[256,128]{1,0:T(8,128)S(1)} collective-permute-done((f32[256,128]{1,0:T(8,128)S(1)}, f32[256,128]{1,0:T(8,128)S(1)}, u32[]{:S(2)}, u32[]{:S(2)}) %collective-permute-start.3) | collective-permute-done | bytes 131104 | tf_op jit(solution)/shard_map/ppermute | solution.py:352
  64.7 0.0 collective-permute-done.4.mate
  64.7 0.0 collective-permute-done.2.edge
  64.7 0.5 first.1
  65.2 0.7 all-to-all-done.1
  65.9 1.6 %heat.1 = (f32[8,512]{1,0:T(8,128)}, f32[256,128]{1,0:T(8,128)S(1)}) custom-call(f32[384,128]{1,0:T(8,128)S(1)} %bitcast.11, f32[8,512]{1,0:T(8,128)S(1)} %get-tuple-element.19.w0, f32[8,512]{1,0:T(8,128)S(1)} %get-tuple-element.20.w1, f32[8,512]{1,0:T(8,128)S(1)} %get-tuple-element.21.w2, f32[16,16,128]{2,1,0:T(8,128)S(1)} %get-tuple-element.22.bins, ...), custom_call_target="tpu_custom_call" | custom-call | tf_op jit(solution)/shard_map/heat/pallas_call | solution.py:355
  67.5 22.0 %all_to_all.15 = f32[32,8,128]{2,1,0:T(8,128)S(1)} all-to-all(f32[32,8,128]{2,1,0:T(8,128)S(1)} %bitcast.12), channel_id=1, replica_groups=mesh['magnet'=16,'slab'=32] {'slab'}, dimensions={0} | all-to-all | bytes 262144 | tf_op jit(solution)/shard_map/all_to_all | solution.py:429
  89.5 0.7 copy.10
  (1 shorter events, 0.0 us)
Async XLA Ops:
  0.6 11.0 %copy-start.1 = (f32[1,256,128]{2,1,0:T(8,128)S(1)}, f32[1,256,128]{2,1,0:T(8,128)}, u32[]{:S(2)}) copy-start(f32[1,256,128]{2,1,0:T(8,128)} %param.10) | copy-start | bytes 393220
  2.1 10.4 %collective-permute-start.1 = (f32[32,512]{1,0:T(8,128)}, f32[32,512]{1,0:T(8,128)S(1)}, u32[]{:S(2)}, u32[]{:S(2)}) collective-permute-start(f32[32,512]{1,0:T(8,128)} %sheet.1.own), channel_id=1, source_target_pairs={{1,2},{3,4},{5,6},{7,8},{9,10},{11,12},{13,14},{15,16},{17,18},{19... | collective-permute-start | bytes 196616 | tf_op jit(solution)/shard_map/ppermute | solution.py:352
  7.1 5.6 %collective-permute-start = (f32[32,512]{1,0:T(8,128)}, f32[32,512]{1,0:T(8,128)S(1)}, u32[]{:S(2)}, u32[]{:S(2)}) collective-permute-start(f32[32,512]{1,0:T(8,128)} %sheet.1.own), channel_id=1, source_target_pairs={{0,1},{2,3},{4,5},{6,7},{8,9},{10,11},{12,13},{14,15},{16,17},{18,... | collective-permute-start | bytes 196616 | tf_op jit(solution)/shard_map/ppermute | solution.py:352
  11.6 0.9 %copy-start.2 = (s32[1,256,128]{2,1,0:T(8,128)S(1)}, s32[1,256,128]{2,1,0:T(8,128)}, u32[]{:S(2)}) copy-start(s32[1,256,128]{2,1,0:T(8,128)} %param.11) | copy-start | bytes 393220
  12.5 0.8 copy-start
  14.5 35.5 %all-to-all-start = ((f32[32,17,1,128]{3,2,1,0:T(1,128)}), f32[32,17,1,128]{3,2,1,0:T(1,128)S(1)}, u32[]{:S(2)}, u32[]{:S(2)}) async-start(f32[32,17,1,128]{3,2,1,0:T(1,128)} %bitcast.2), calls=%async_computation | async-start | bytes 557056 | tf_op jit(solution)/shard_map/all_to_all | solution.py:387
  50.0 14.7 %collective-permute-start.2 = (f32[544,128]{1,0:T(8,128)S(1)}, f32[544,128]{1,0:T(8,128)S(1)}, u32[]{:S(2)}, u32[]{:S(2)}) collective-permute-start(f32[544,128]{1,0:T(8,128)S(1)} %bitcast.8), channel_id=1, source_target_pairs={{31,32},{63,64},{95,96},{127,128},{159,160},{191,192},{223,224},{2... | collective-permute-start | bytes 835592 | tf_op jit(solution)/shard_map/ppermute | solution.py:352
  51.4 14.5 %all-to-all-start.1 = ((f32[16,24,128]{2,1,0:T(8,128)}), f32[16,24,128]{2,1,0:T(8,128)S(1)}, u32[]{:S(2)}, u32[]{:S(2)}) async-start(f32[16,24,128]{2,1,0:T(8,128)} %bitcast.4), calls=%async_computation.1 | async-start | bytes 393216 | tf_op jit(solution)/shard_map/all_to_all | solution.py:404
  58.2 6.6 %collective-permute-start.3 = (f32[256,128]{1,0:T(8,128)S(1)}, f32[256,128]{1,0:T(8,128)S(1)}, u32[]{:S(2)}, u32[]{:S(2)}) collective-permute-start(f32[256,128]{1,0:T(8,128)S(1)} %get-tuple-element.23), channel_id=1, source_target_pairs={{1,2},{3,4},{5,6},{7,8},{9,10},{11,12},{13,14},{15,16},{17,18},{19... | collective-permute-start | bytes 393224 | tf_op jit(solution)/shard_map/ppermute | solution.py:352
  60.7 4.0 %collective-permute-start.4 = (f32[256,128]{1,0:T(8,128)S(1)}, f32[256,128]{1,0:T(8,128)S(1)}, u32[]{:S(2)}, u32[]{:S(2)}) collective-permute-start(f32[256,128]{1,0:T(8,128)S(1)} %get-tuple-element.24), channel_id=1, source_target_pairs={{0,1},{2,3},{4,5},{6,7},{8,9},{10,11},{12,13},{14,15},{16,17},{18,... | collective-permute-start | bytes 393224 | tf_op jit(solution)/shard_map/ppermute | solution.py:352

commit v15 on v14

--- a/solution.py
+++ b/solution.py
@@ -305,11 +305,13 @@
     substep_rows(range(1, SPAN - 1), layers, warm, cond, base, done)
 
 
-def heat_kernel(layers, lines, w0, w1, w2, bins, fresh, base, store, potential, heated, warm, cond):
+def heat_kernel(layers, lines, w0, w1, w2, bins, fresh, base, store, potential_out, heated, warm, cond, potential, sem):
     spokes = heated.shape[-1]
     body = slice(EDGE, EDGE + layers)
     f = solve_small(lines[pl.ds(0, lines.shape[0] // COPIES, stride=COPIES), :])
     potential[...] = f[0] * w0[...] + f[1] * w1[...] + f[2] * w2[...]
+    leaving = pltpu.make_async_copy(potential, potential_out, sem)
+    leaving.start()
     sublane = lax.broadcasted_iota(jnp.int32, (8, spokes), 0)
     weight = jnp.zeros((8, spokes), jnp.float32)
     for pair, (i, j) in enumerate(PAIRS):
@@ -336,6 +338,7 @@
                 heated[pl.ds(row - HALO, layers, stride=ROWS), :] = t
 
         substep_rows(range(substep + 1, SPAN - 1 - substep), layers, warm.at[substep % 2], cond, base, done)
+    leaving.wait()
 
 
 def local(foil_warmth, terminal_voltage_input, foil_segment_pattern, underlying_block_map, prior_block_warmth, substance_kind):
@@ -351,12 +354,12 @@
     def swap(array, pairs):
         return lax.ppermute(array, BOTH, pairs + [(j, i) for i, j in pairs])
 
-    def call(kernel, name, shapes, *operands, scratch=(), spaces=None, cost=None, room=8 << 20):
+    def call(kernel, name, shapes, *operands, scratch=(), spaces=None, outs=None, cost=None, room=8 << 20):
         return pl.pallas_call(
             kernel,
             out_shape=tuple(jax.ShapeDtypeStruct(dims, f32) for dims in shapes),
             in_specs=[pl.BlockSpec(memory_space=spaces or pltpu.VMEM)] * len(operands),
-            out_specs=(pl.BlockSpec(memory_space=pltpu.VMEM),) * len(shapes),
+            out_specs=tuple(pl.BlockSpec(memory_space=space) for space in outs or (pltpu.VMEM,) * len(shapes)),
             scratch_shapes=scratch,
             cost_estimate=cost,
             compiler_params=pltpu.CompilerParams(vmem_limit_bytes=room),
@@ -424,7 +427,13 @@
         *fields,
         bins,
         *stage,
-        scratch=[pltpu.VMEM((2,) + padded, f32), pltpu.VMEM(padded, f32)],
+        outs=(pltpu.HBM, pltpu.VMEM),
+        scratch=[
+            pltpu.VMEM((2,) + padded, f32),
+            pltpu.VMEM(padded, f32),
+            pltpu.VMEM(rows, f32),
+            pltpu.SemaphoreType.DMA(()),
+        ],
     )
     heated = lax.all_to_all(heated.reshape(layers, ROWS, spokes), "slab", 0, 0)
     return potential, heated.reshape(prior_block_warmth.shape)

time: 90.7 us -> 90.7 us (level)
  no operation moved by 1% of the time
where the time goes in v15:
time: 90.7 us; the launch traced here: 90.2 us
  starting transfers between devices  34.2 us (38%)
  waiting for transfers between devices  24.3 us (27%)
  blocking collectives  22 us (24%)
  Pallas kernels  6.64 us (7%)
  local copies, waits for them, and re-layouts  2.23 us (2%)
    all_to_all x1, blocking collectives, local(): heated = lax.all_to_all(heated.reshape(layers, ROWS, spokes), 'slab', 0, 0)  22 us
    all_to_all x1, waiting for transfers between devices, local(): lax.all_to_all(packed.reshape(layers, BLOCK, 1, spokes), 'slab', 0, 0)  21.7 us
    ppermute x5, starting transfers between devices, swap(): return lax.ppermute(array, BOTH, pairs + [(j, i) for i, j in pairs])  14.9 us
    all_to_all x1, starting transfers between devices, local(): lax.all_to_all(packed.reshape(layers, BLOCK, 1, spokes), 'slab', 0, 0)  12.5 us
    all_to_all x1, starting transfers between devices, local(): lax.all_to_all(lines.reshape(magnets, COPIES, spokes), 'magnet', 0, 0)  6.75 us
    pallas_call x7, Pallas kernels, call(): pl.pallas_call(kernel, out_shape=tuple((jax.ShapeDtypeStruct(dims, f32) f...  6.64 us
    unnamed x7, local copies, waits for them, and re-layouts  2.23 us
    ppermute x5, waiting for transfers between devices, swap(): return lax.ppermute(array, BOTH, pairs + [(j, i) for i, j in pairs])  1.89 us
  transfers between devices with their start and end apart: 7, of which 4 were waited for; matrix products, arithmetic and copies ran while one was open for 0% of the time, Pallas kernels for 3%

profile of v15, /device:TPU:1, one launch (start us, length us, event | category | flops | bytes accessed | tf_op | source)
XLA Modules:
  0.0 90.2 jit_solution(7825024698052277180)
XLA Ops:
  0.6 0.0 copy-start.1
  0.6 1.5 %sheet.1.own = f32[32,512]{1,0:T(8,128)} custom-call(f32[8,512]{1,0:T(8,128)} %warmth.1, f32[8,512]{1,0:T(8,128)} %voltage.1, s32[8,512]{1,0:T(8,128)} %pattern.1, s32[256,512]{1,0:T(8,128)} %cells.1), custom_call_target="tpu_custom_call" | custom-call | tf_op jit(solution)/shard_map/sheet/pallas_call | solution.py:358
  2.1 4.9 %collective-permute-start.1 = (f32[32,512]{1,0:T(8,128)}, f32[32,512]{1,0:T(8,128)S(1)}, u32[]{:S(2)}, u32[]{:S(2)}) collective-permute-start(f32[32,512]{1,0:T(8,128)} %sheet.1.own), channel_id=1, source_target_pairs={{1,2},{3,4},{5,6},{7,8},{9,10},{11,12},{13,14},{15,16},{17,18},{19... | collective-permute-start | bytes 196616 | tf_op jit(solution)/shard_map/ppermute | solution.py:355
  7.1 4.5 %collective-permute-start = (f32[32,512]{1,0:T(8,128)}, f32[32,512]{1,0:T(8,128)S(1)}, u32[]{:S(2)}, u32[]{:S(2)}) collective-permute-start(f32[32,512]{1,0:T(8,128)} %sheet.1.own), channel_id=1, source_target_pairs={{0,1},{2,3},{4,5},{6,7},{8,9},{10,11},{12,13},{14,15},{16,17},{18,... | collective-permute-start | bytes 196616 | tf_op jit(solution)/shard_map/ppermute | solution.py:355
  11.6 0.0 copy-done.1
  11.6 0.0 copy-start.2
  11.6 0.9 copy-done.2
  12.5 0.0 copy-start
  12.5 0.0 collective-permute-done.1.cross
  12.5 0.1 collective-permute-done.mate
  12.7 0.7 copy-done
  13.3 1.1 %gram.1 = f32[544,128]{1,0:T(8,128)} custom-call(f32[32,512]{1,0:T(8,128)S(1)} %copy-done, f32[32,512]{1,0:T(8,128)S(1)} %collective-permute-done.mate, f32[32,512]{1,0:T(8,128)S(1)} %collective-permute-done.1.cross, f32[544,128]{1,0:T(8,128)S(1)} %pack.1.packed_in), custom_call_target="tpu_custom_call" | custom-call | tf_op jit(solution)/shard_map/gram/pallas_call | solution.py:358
  14.5 12.5 %all-to-all-start = ((f32[32,17,1,128]{3,2,1,0:T(1,128)}), f32[32,17,1,128]{3,2,1,0:T(1,128)S(1)}, u32[]{:S(2)}, u32[]{:S(2)}) async-start(f32[32,17,1,128]{3,2,1,0:T(1,128)} %bitcast.2), calls=%async_computation | async-start | bytes 557056 | tf_op jit(solution)/shard_map/all_to_all | solution.py:390
  27.0 1.2 %deposit.1 = (f32[16,16,128]{2,1,0:T(8,128)S(1)}, f32[8,512]{1,0:T(8,128)S(1)}, f32[8,512]{1,0:T(8,128)S(1)}, f32[8,512]{1,0:T(8,128)S(1)}) custom-call(f32[32,512]{1,0:T(8,128)S(1)} %copy-done, f32[32,512]{1,0:T(8,128)S(1)} %collective-permute-done.mate, f32[32,512]{1,0:T(8,128)S(1)} %collective-permute-done.1.cross), custom_call_target="tpu_custom_call" | custom-call | flops 100000000 | bytes 2000000 | tf_op jit(solution)/shard_map/deposit/pallas_call | solution.py:358
  28.3 21.7 %all-to-all-done = f32[32,17,1,128]{3,2,1,0:T(1,128)S(1)} async-done(((f32[32,17,1,128]{3,2,1,0:T(1,128)}), f32[32,17,1,128]{3,2,1,0:T(1,128)S(1)}, u32[]{:S(2)}, u32[]{:S(2)}) %all-to-all-start) | async-done | bytes 278560 | tf_op jit(solution)/shard_map/all_to_all | solution.py:390
  50.0 0.7 collective-permute-start.2
  50.7 0.7 share.1
  51.4 6.8 %all-to-all-start.1 = ((f32[16,24,128]{2,1,0:T(8,128)}), f32[16,24,128]{2,1,0:T(8,128)S(1)}, u32[]{:S(2)}, u32[]{:S(2)}) async-start(f32[16,24,128]{2,1,0:T(8,128)} %bitcast.4), calls=%async_computation.1 | async-start | bytes 393216 | tf_op jit(solution)/shard_map/all_to_all | solution.py:407
  58.2 2.5 %collective-permute-start.3 = (f32[256,128]{1,0:T(8,128)S(1)}, f32[256,128]{1,0:T(8,128)S(1)}, u32[]{:S(2)}, u32[]{:S(2)}) collective-permute-start(f32[256,128]{1,0:T(8,128)S(1)} %get-tuple-element.23), channel_id=1, source_target_pairs={{1,2},{3,4},{5,6},{7,8},{9,10},{11,12},{13,14},{15,16},{17,18},{19... | collective-permute-start | bytes 393224 | tf_op jit(solution)/shard_map/ppermute | solution.py:355
  60.7 2.3 %collective-permute-start.4 = (f32[256,128]{1,0:T(8,128)S(1)}, f32[256,128]{1,0:T(8,128)S(1)}, u32[]{:S(2)}, u32[]{:S(2)}) collective-permute-start(f32[256,128]{1,0:T(8,128)S(1)} %get-tuple-element.24), channel_id=1, source_target_pairs={{0,1},{2,3},{4,5},{6,7},{8,9},{10,11},{12,13},{14,15},{16,17},{18,... | collective-permute-start | bytes 393224 | tf_op jit(solution)/shard_map/ppermute | solution.py:355
  63.0 1.8 %collective-permute-done.3.cross = f32[256,128]{1,0:T(8,128)S(1)} collective-permute-done((f32[256,128]{1,0:T(8,128)S(1)}, f32[256,128]{1,0:T(8,128)S(1)}, u32[]{:S(2)}, u32[]{:S(2)}) %collective-permute-start.3) | collective-permute-done | bytes 131104 | tf_op jit(solution)/shard_map/ppermute | solution.py:355
  64.7 0.0 collective-permute-done.4.mate
  64.7 0.0 collective-permute-done.2.edge
  64.7 0.5 first.1
  65.2 0.7 all-to-all-done.1
  65.9 1.6 %heat.1 = (f32[8,512]{1,0:T(8,128)}, f32[256,128]{1,0:T(8,128)S(1)}) custom-call(f32[384,128]{1,0:T(8,128)S(1)} %bitcast.11, f32[8,512]{1,0:T(8,128)S(1)} %get-tuple-element.19.w0, f32[8,512]{1,0:T(8,128)S(1)} %get-tuple-element.20.w1, f32[8,512]{1,0:T(8,128)S(1)} %get-tuple-element.21.w2, f32[16,16,128]{2,1,0:T(8,128)S(1)} %get-tuple-element.22.bins, ...), custom_call_target="tpu_custom_call" | custom-call | tf_op jit(solution)/shard_map/heat/pallas_call | solution.py:358
  67.5 22.0 %all_to_all.15 = f32[32,8,128]{2,1,0:T(8,128)S(1)} all-to-all(f32[32,8,128]{2,1,0:T(8,128)S(1)} %bitcast.12), channel_id=1, replica_groups=mesh['magnet'=16,'slab'=32] {'slab'}, dimensions={0} | all-to-all | bytes 262144 | tf_op jit(solution)/shard_map/all_to_all | solution.py:438
  89.5 0.7 copy.10
  (1 shorter events, 0.0 us)
Async XLA Ops:
  0.6 11.0 %copy-start.1 = (f32[1,256,128]{2,1,0:T(8,128)S(1)}, f32[1,256,128]{2,1,0:T(8,128)}, u32[]{:S(2)}) copy-start(f32[1,256,128]{2,1,0:T(8,128)} %param.10) | copy-start | bytes 393220
  2.1 10.4 %collective-permute-start.1 = (f32[32,512]{1,0:T(8,128)}, f32[32,512]{1,0:T(8,128)S(1)}, u32[]{:S(2)}, u32[]{:S(2)}) collective-permute-start(f32[32,512]{1,0:T(8,128)} %sheet.1.own), channel_id=1, source_target_pairs={{1,2},{3,4},{5,6},{7,8},{9,10},{11,12},{13,14},{15,16},{17,18},{19... | collective-permute-start | bytes 196616 | tf_op jit(solution)/shard_map/ppermute | solution.py:355
  7.1 5.6 %collective-permute-start = (f32[32,512]{1,0:T(8,128)}, f32[32,512]{1,0:T(8,128)S(1)}, u32[]{:S(2)}, u32[]{:S(2)}) collective-permute-start(f32[32,512]{1,0:T(8,128)} %sheet.1.own), channel_id=1, source_target_pairs={{0,1},{2,3},{4,5},{6,7},{8,9},{10,11},{12,13},{14,15},{16,17},{18,... | collective-permute-start | bytes 196616 | tf_op jit(solution)/shard_map/ppermute | solution.py:355
  11.6 0.9 %copy-start.2 = (s32[1,256,128]{2,1,0:T(8,128)S(1)}, s32[1,256,128]{2,1,0:T(8,128)}, u32[]{:S(2)}) copy-start(s32[1,256,128]{2,1,0:T(8,128)} %param.11) | copy-start | bytes 393220
  12.5 0.8 copy-start
  14.5 35.5 %all-to-all-start = ((f32[32,17,1,128]{3,2,1,0:T(1,128)}), f32[32,17,1,128]{3,2,1,0:T(1,128)S(1)}, u32[]{:S(2)}, u32[]{:S(2)}) async-start(f32[32,17,1,128]{3,2,1,0:T(1,128)} %bitcast.2), calls=%async_computation | async-start | bytes 557056 | tf_op jit(solution)/shard_map/all_to_all | solution.py:390
  50.0 14.7 %collective-permute-start.2 = (f32[544,128]{1,0:T(8,128)S(1)}, f32[544,128]{1,0:T(8,128)S(1)}, u32[]{:S(2)}, u32[]{:S(2)}) collective-permute-start(f32[544,128]{1,0:T(8,128)S(1)} %bitcast.8), channel_id=1, source_target_pairs={{31,32},{63,64},{95,96},{127,128},{159,160},{191,192},{223,224},{2... | collective-permute-start | bytes 835592 | tf_op jit(solution)/shard_map/ppermute | solution.py:355
  51.4 14.5 %all-to-all-start.1 = ((f32[16,24,128]{2,1,0:T(8,128)}), f32[16,24,128]{2,1,0:T(8,128)S(1)}, u32[]{:S(2)}, u32[]{:S(2)}) async-start(f32[16,24,128]{2,1,0:T(8,128)} %bitcast.4), calls=%async_computation.1 | async-start | bytes 393216 | tf_op jit(solution)/shard_map/all_to_all | solution.py:407
  58.2 6.6 %collective-permute-start.3 = (f32[256,128]{1,0:T(8,128)S(1)}, f32[256,128]{1,0:T(8,128)S(1)}, u32[]{:S(2)}, u32[]{:S(2)}) collective-permute-start(f32[256,128]{1,0:T(8,128)S(1)} %get-tuple-element.23), channel_id=1, source_target_pairs={{1,2},{3,4},{5,6},{7,8},{9,10},{11,12},{13,14},{15,16},{17,18},{19... | collective-permute-start | bytes 393224 | tf_op jit(solution)/shard_map/ppermute | solution.py:355
  60.7 4.0 %collective-permute-start.4 = (f32[256,128]{1,0:T(8,128)S(1)}, f32[256,128]{1,0:T(8,128)S(1)}, u32[]{:S(2)}, u32[]{:S(2)}) collective-permute-start(f32[256,128]{1,0:T(8,128)S(1)} %get-tuple-element.24), channel_id=1, source_target_pairs={{0,1},{2,3},{4,5},{6,7},{8,9},{10,11},{12,13},{14,15},{16,17},{18,... | collective-permute-start | bytes 393224 | tf_op jit(solution)/shard_map/ppermute | solution.py:355

commit v16 on v15

--- a/solution.py
+++ b/solution.py
@@ -146,8 +146,10 @@
     shifted = ((g01, g11, g12), (g11, k11, k12), (g12, k12, k22))
     energy = [[SCALE * shifted[i][j] + SHIFT * gram[i][j] for j in range(3)] for i in range(3)]
 
+    gram, energy = ([[m[i][j] * (1.0 if i == j else 2.0) for j in range(3)] for i in range(3)] for m in (gram, energy))
+
     def form(m, v):
-        return sum(v[i] * (v[i] * m[i][i] + 2.0 * sum((v[j] * m[i][j] for j in range(i + 1, len(v))), 0.0)) for i in range(len(v)))
+        return sum(v[i] * sum(v[j] * m[i][j] for j in range(i, len(v))) for i in range(len(v)))
 
     def ratio(num, den, low, high):
         return jnp.clip(num / jnp.maximum(den, 1e-37), low, high)

time: 90.7 us -> 90.7 us (level)
  no operation moved by 1% of the time
where the time goes in v16:
time: 90.7 us; the launch traced here: 90.2 us
  starting transfers between devices  34.2 us (38%)
  waiting for transfers between devices  24.3 us (27%)
  blocking collectives  22 us (24%)
  Pallas kernels  6.63 us (7%)
  local copies, waits for them, and re-layouts  2.23 us (2%)
    all_to_all x1, blocking collectives, local(): heated = lax.all_to_all(heated.reshape(layers, ROWS, spokes), 'slab', 0, 0)  22 us
    all_to_all x1, waiting for transfers between devices, local(): lax.all_to_all(packed.reshape(layers, BLOCK, 1, spokes), 'slab', 0, 0)  21.7 us
    ppermute x5, starting transfers between devices, swap(): return lax.ppermute(array, BOTH, pairs + [(j, i) for i, j in pairs])  14.9 us
    all_to_all x1, starting transfers between devices, local(): lax.all_to_all(packed.reshape(layers, BLOCK, 1, spokes), 'slab', 0, 0)  12.5 us
    all_to_all x1, starting transfers between devices, local(): lax.all_to_all(lines.reshape(magnets, COPIES, spokes), 'magnet', 0, 0)  6.75 us
    pallas_call x7, Pallas kernels, call(): pl.pallas_call(kernel, out_shape=tuple((jax.ShapeDtypeStruct(dims, f32) f...  6.63 us
    unnamed x7, local copies, waits for them, and re-layouts  2.23 us
    ppermute x5, waiting for transfers between devices, swap(): return lax.ppermute(array, BOTH, pairs + [(j, i) for i, j in pairs])  1.89 us
  transfers between devices with their start and end apart: 7, of which 4 were waited for; matrix products, arithmetic and copies ran while one was open for 0% of the time, Pallas kernels for 3%

profile of v16, /device:TPU:1, one launch (start us, length us, event | category | flops | bytes accessed | tf_op | source)
XLA Modules:
  0.0 90.2 jit_solution(7611628013066162874)
XLA Ops:
  0.6 0.0 copy-start.1
  0.6 1.5 %sheet.1.own = f32[32,512]{1,0:T(8,128)} custom-call(f32[8,512]{1,0:T(8,128)} %warmth.1, f32[8,512]{1,0:T(8,128)} %voltage.1, s32[8,512]{1,0:T(8,128)} %pattern.1, s32[256,512]{1,0:T(8,128)} %cells.1), custom_call_target="tpu_custom_call" | custom-call | tf_op jit(solution)/shard_map/sheet/pallas_call | solution.py:360
  2.1 4.9 %collective-permute-start.1 = (f32[32,512]{1,0:T(8,128)}, f32[32,512]{1,0:T(8,128)S(1)}, u32[]{:S(2)}, u32[]{:S(2)}) collective-permute-start(f32[32,512]{1,0:T(8,128)} %sheet.1.own), channel_id=1, source_target_pairs={{1,2},{3,4},{5,6},{7,8},{9,10},{11,12},{13,14},{15,16},{17,18},{19... | collective-permute-start | bytes 196616 | tf_op jit(solution)/shard_map/ppermute | solution.py:357
  7.1 4.5 %collective-permute-start = (f32[32,512]{1,0:T(8,128)}, f32[32,512]{1,0:T(8,128)S(1)}, u32[]{:S(2)}, u32[]{:S(2)}) collective-permute-start(f32[32,512]{1,0:T(8,128)} %sheet.1.own), channel_id=1, source_target_pairs={{0,1},{2,3},{4,5},{6,7},{8,9},{10,11},{12,13},{14,15},{16,17},{18,... | collective-permute-start | bytes 196616 | tf_op jit(solution)/shard_map/ppermute | solution.py:357
  11.6 0.0 copy-done.1
  11.6 0.0 copy-start.2
  11.6 0.9 copy-done.2
  12.5 0.0 copy-start
  12.5 0.0 collective-permute-done.1.cross
  12.5 0.1 collective-permute-done.mate
  12.7 0.7 copy-done
  13.3 1.1 %gram.1 = f32[544,128]{1,0:T(8,128)} custom-call(f32[32,512]{1,0:T(8,128)S(1)} %copy-done, f32[32,512]{1,0:T(8,128)S(1)} %collective-permute-done.mate, f32[32,512]{1,0:T(8,128)S(1)} %collective-permute-done.1.cross, f32[544,128]{1,0:T(8,128)S(1)} %pack.1.packed_in), custom_call_target="tpu_custom_call" | custom-call | tf_op jit(solution)/shard_map/gram/pallas_call | solution.py:360
  14.5 12.5 %all-to-all-start = ((f32[32,17,1,128]{3,2,1,0:T(1,128)}), f32[32,17,1,128]{3,2,1,0:T(1,128)S(1)}, u32[]{:S(2)}, u32[]{:S(2)}) async-start(f32[32,17,1,128]{3,2,1,0:T(1,128)} %bitcast.2), calls=%async_computation | async-start | bytes 557056 | tf_op jit(solution)/shard_map/all_to_all | solution.py:392
  27.0 1.2 %deposit.1 = (f32[16,16,128]{2,1,0:T(8,128)S(1)}, f32[8,512]{1,0:T(8,128)S(1)}, f32[8,512]{1,0:T(8,128)S(1)}, f32[8,512]{1,0:T(8,128)S(1)}) custom-call(f32[32,512]{1,0:T(8,128)S(1)} %copy-done, f32[32,512]{1,0:T(8,128)S(1)} %collective-permute-done.mate, f32[32,512]{1,0:T(8,128)S(1)} %collective-permute-done.1.cross), custom_call_target="tpu_custom_call" | custom-call | flops 100000000 | bytes 2000000 | tf_op jit(solution)/shard_map/deposit/pallas_call | solution.py:360
  28.3 21.7 %all-to-all-done = f32[32,17,1,128]{3,2,1,0:T(1,128)S(1)} async-done(((f32[32,17,1,128]{3,2,1,0:T(1,128)}), f32[32,17,1,128]{3,2,1,0:T(1,128)S(1)}, u32[]{:S(2)}, u32[]{:S(2)}) %all-to-all-start) | async-done | bytes 278560 | tf_op jit(solution)/shard_map/all_to_all | solution.py:392
  50.0 0.7 collective-permute-start.2
  50.7 0.7 share.1
  51.4 6.8 %all-to-all-start.1 = ((f32[16,24,128]{2,1,0:T(8,128)}), f32[16,24,128]{2,1,0:T(8,128)S(1)}, u32[]{:S(2)}, u32[]{:S(2)}) async-start(f32[16,24,128]{2,1,0:T(8,128)} %bitcast.4), calls=%async_computation.1 | async-start | bytes 393216 | tf_op jit(solution)/shard_map/all_to_all | solution.py:409
  58.2 2.5 %collective-permute-start.3 = (f32[256,128]{1,0:T(8,128)S(1)}, f32[256,128]{1,0:T(8,128)S(1)}, u32[]{:S(2)}, u32[]{:S(2)}) collective-permute-start(f32[256,128]{1,0:T(8,128)S(1)} %get-tuple-element.23), channel_id=1, source_target_pairs={{1,2},{3,4},{5,6},{7,8},{9,10},{11,12},{13,14},{15,16},{17,18},{19... | collective-permute-start | bytes 393224 | tf_op jit(solution)/shard_map/ppermute | solution.py:357
  60.7 2.3 %collective-permute-start.4 = (f32[256,128]{1,0:T(8,128)S(1)}, f32[256,128]{1,0:T(8,128)S(1)}, u32[]{:S(2)}, u32[]{:S(2)}) collective-permute-start(f32[256,128]{1,0:T(8,128)S(1)} %get-tuple-element.24), channel_id=1, source_target_pairs={{0,1},{2,3},{4,5},{6,7},{8,9},{10,11},{12,13},{14,15},{16,17},{18,... | collective-permute-start | bytes 393224 | tf_op jit(solution)/shard_map/ppermute | solution.py:357
  63.0 1.8 %collective-permute-done.3.cross = f32[256,128]{1,0:T(8,128)S(1)} collective-permute-done((f32[256,128]{1,0:T(8,128)S(1)}, f32[256,128]{1,0:T(8,128)S(1)}, u32[]{:S(2)}, u32[]{:S(2)}) %collective-permute-start.3) | collective-permute-done | bytes 131104 | tf_op jit(solution)/shard_map/ppermute | solution.py:357
  64.7 0.0 collective-permute-done.4.mate
  64.7 0.0 collective-permute-done.2.edge
  64.7 0.5 first.1
  65.2 0.7 all-to-all-done.1
  65.9 1.6 %heat.1 = (f32[8,512]{1,0:T(8,128)}, f32[256,128]{1,0:T(8,128)S(1)}) custom-call(f32[384,128]{1,0:T(8,128)S(1)} %bitcast.11, f32[8,512]{1,0:T(8,128)S(1)} %get-tuple-element.19.w0, f32[8,512]{1,0:T(8,128)S(1)} %get-tuple-element.20.w1, f32[8,512]{1,0:T(8,128)S(1)} %get-tuple-element.21.w2, f32[16,16,128]{2,1,0:T(8,128)S(1)} %get-tuple-element.22.bins, ...), custom_call_target="tpu_custom_call" | custom-call | tf_op jit(solution)/shard_map/heat/pallas_call | solution.py:360
  67.5 22.0 %all_to_all.15 = f32[32,8,128]{2,1,0:T(8,128)S(1)} all-to-all(f32[32,8,128]{2,1,0:T(8,128)S(1)} %bitcast.12), channel_id=1, replica_groups=mesh['magnet'=16,'slab'=32] {'slab'}, dimensions={0} | all-to-all | bytes 262144 | tf_op jit(solution)/shard_map/all_to_all | solution.py:440
  89.5 0.7 copy.10
  (1 shorter events, 0.0 us)
Async XLA Ops:
  0.6 11.0 %copy-start.1 = (f32[1,256,128]{2,1,0:T(8,128)S(1)}, f32[1,256,128]{2,1,0:T(8,128)}, u32[]{:S(2)}) copy-start(f32[1,256,128]{2,1,0:T(8,128)} %param.10) | copy-start | bytes 393220
  2.1 10.4 %collective-permute-start.1 = (f32[32,512]{1,0:T(8,128)}, f32[32,512]{1,0:T(8,128)S(1)}, u32[]{:S(2)}, u32[]{:S(2)}) collective-permute-start(f32[32,512]{1,0:T(8,128)} %sheet.1.own), channel_id=1, source_target_pairs={{1,2},{3,4},{5,6},{7,8},{9,10},{11,12},{13,14},{15,16},{17,18},{19... | collective-permute-start | bytes 196616 | tf_op jit(solution)/shard_map/ppermute | solution.py:357
  7.1 5.6 %collective-permute-start = (f32[32,512]{1,0:T(8,128)}, f32[32,512]{1,0:T(8,128)S(1)}, u32[]{:S(2)}, u32[]{:S(2)}) collective-permute-start(f32[32,512]{1,0:T(8,128)} %sheet.1.own), channel_id=1, source_target_pairs={{0,1},{2,3},{4,5},{6,7},{8,9},{10,11},{12,13},{14,15},{16,17},{18,... | collective-permute-start | bytes 196616 | tf_op jit(solution)/shard_map/ppermute | solution.py:357
  11.6 0.9 %copy-start.2 = (s32[1,256,128]{2,1,0:T(8,128)S(1)}, s32[1,256,128]{2,1,0:T(8,128)}, u32[]{:S(2)}) copy-start(s32[1,256,128]{2,1,0:T(8,128)} %param.11) | copy-start | bytes 393220
  12.5 0.8 copy-start
  14.5 35.5 %all-to-all-start = ((f32[32,17,1,128]{3,2,1,0:T(1,128)}), f32[32,17,1,128]{3,2,1,0:T(1,128)S(1)}, u32[]{:S(2)}, u32[]{:S(2)}) async-start(f32[32,17,1,128]{3,2,1,0:T(1,128)} %bitcast.2), calls=%async_computation | async-start | bytes 557056 | tf_op jit(solution)/shard_map/all_to_all | solution.py:392
  50.0 14.7 %collective-permute-start.2 = (f32[544,128]{1,0:T(8,128)S(1)}, f32[544,128]{1,0:T(8,128)S(1)}, u32[]{:S(2)}, u32[]{:S(2)}) collective-permute-start(f32[544,128]{1,0:T(8,128)S(1)} %bitcast.8), channel_id=1, source_target_pairs={{31,32},{63,64},{95,96},{127,128},{159,160},{191,192},{223,224},{2... | collective-permute-start | bytes 835592 | tf_op jit(solution)/shard_map/ppermute | solution.py:357
  51.4 14.5 %all-to-all-start.1 = ((f32[16,24,128]{2,1,0:T(8,128)}), f32[16,24,128]{2,1,0:T(8,128)S(1)}, u32[]{:S(2)}, u32[]{:S(2)}) async-start(f32[16,24,128]{2,1,0:T(8,128)} %bitcast.4), calls=%async_computation.1 | async-start | bytes 393216 | tf_op jit(solution)/shard_map/all_to_all | solution.py:409
  58.2 6.6 %collective-permute-start.3 = (f32[256,128]{1,0:T(8,128)S(1)}, f32[256,128]{1,0:T(8,128)S(1)}, u32[]{:S(2)}, u32[]{:S(2)}) collective-permute-start(f32[256,128]{1,0:T(8,128)S(1)} %get-tuple-element.23), channel_id=1, source_target_pairs={{1,2},{3,4},{5,6},{7,8},{9,10},{11,12},{13,14},{15,16},{17,18},{19... | collective-permute-start | bytes 393224 | tf_op jit(solution)/shard_map/ppermute | solution.py:357
  60.7 4.0 %collective-permute-start.4 = (f32[256,128]{1,0:T(8,128)S(1)}, f32[256,128]{1,0:T(8,128)S(1)}, u32[]{:S(2)}, u32[]{:S(2)}) collective-permute-start(f32[256,128]{1,0:T(8,128)S(1)} %get-tuple-element.24), channel_id=1, source_target_pairs={{0,1},{2,3},{4,5},{6,7},{8,9},{10,11},{12,13},{14,15},{16,17},{18,... | collective-permute-start | bytes 393224 | tf_op jit(solution)/shard_map/ppermute | solution.py:357
